TPU v7x, 32 devices: a whole 2x2x4 slice. The times are simulated.
32 devices in a mesh: grp: 4 (over x, core), loop: 8 (over z, y).
Axes of the slice: x: 2, y: 2, z: 4, core: 2. Of those that a mesh axis runs over, the one named last changes fastest.
Arguments:
- solid_temp: float32 [12, 256, 2048], P(None, 'grp', 'loop'), may hold values from -3 to 3
- kappa: float32 [12, 256, 2048], P(None, 'grp', 'loop'), may hold values from 0.5 to 1.5
- slope: float32 [12, 256, 2048], P(None, 'grp', 'loop'), may hold values from 0.02 to 0.25
- power: float32 [12, 256, 2048], P(None, 'grp', 'loop'), may hold values from 0.2 to 5
- coolant_temp: float32 [256, 2048], P('grp', 'loop'), may hold values from -4 to 4
- wall_coeff: float32 [256, 2048], P('grp', 'loop'), may hold values from 0.25 to 1
- channel_map: int32 [8, 256], P('loop'), may hold values from 0 to 255, each once within a row
- flow_dir: int32 [256], P('grp'), may hold values 0 or 1
- loop_link: int32 [256], replicated, may hold values from 0 to 255, each once
Outputs:
- solid_out: float32 [12, 256, 2048], P(None, 'grp', 'loop')
- coolant_out: float32 [256, 2048], P('grp', 'loop')
Inputs may be any that keep to these rules, and one draw needn't show every extreme that they name: Each row of channel_map is a permutation of 0 to 255. loop_link is a permutation of 0 to 255.
All inputs are finite; a program needn't handle non-finite values. No bound on the sum of `flow_dir` on one device may be relied on, other than what follows from the above.
Results may differ from a plain program's by a relative error of at most 0.0001.
Values sent between devices are 32-bit elements; how exact they have to be, the bound alone decides.
No kernel may reach another device: no remote copies, remote signals or barrier semaphores. Data moves between devices by JAX's collectives and lax.ppermute only.
A program may use at most 64 MiB of HBM per device.

v0:
```python
import jax
import jax.numpy as jnp
from jax import lax
from jax.sharding import PartitionSpec as P

STEPS = 2


time_step = 0.06
courant = 0.5
heat_gain = 0.5


def with_halo(block, sides, width):
    for axis, dim in sides:
        count = lax.axis_size(axis)
        forward = [(i, i + 1) for i in range(count - 1)]
        forward.append((count - 1, 0))
        backward = [(target, source) for source, target in forward]
        low = lax.ppermute(
            lax.slice_in_dim(block, block.shape[dim] - width, None, axis=dim), axis, forward
        )
        high = lax.ppermute(lax.slice_in_dim(block, 0, width, axis=dim), axis, backward)
        block = jnp.concatenate([low, block, high], axis=dim)
    return block


def block_heat(temp_ext, cond_ext, low_edge, high_edge):
    temp_in = temp_ext[:, 1:-1, 1:-1]
    cond_in = cond_ext[:, 1:-1, 1:-1]
    flux_z = 0.5 * (cond_in[1:] + cond_in[:-1]) * (temp_in[1:] - temp_in[:-1])
    zero_layer = jnp.zeros((1,) + flux_z.shape[1:], jnp.float32)
    heat = jnp.concatenate([flux_z, zero_layer], 0) - jnp.concatenate([zero_layer, flux_z], 0)
    temp_x = temp_ext[:, 1:-1, :]
    cond_x = cond_ext[:, 1:-1, :]
    flux_x = 0.5 * (cond_x[:, :, 1:] + cond_x[:, :, :-1]) * (temp_x[:, :, 1:] - temp_x[:, :, :-1])
    heat = heat + flux_x[:, :, 1:] - flux_x[:, :, :-1]
    temp_y = temp_ext[:, :, 1:-1]
    cond_y = cond_ext[:, :, 1:-1]
    flux_y = 0.5 * (cond_y[:, 1:, :] + cond_y[:, :-1, :]) * (temp_y[:, 1:, :] - temp_y[:, :-1, :])
    faces = flux_y.shape[1]
    face_id = lax.broadcasted_iota(jnp.int32, (1, faces, 1), 1)
    closed = jnp.logical_or(
        jnp.logical_and(face_id == 0, low_edge), jnp.logical_and(face_id == faces - 1, high_edge)
    )
    flux_y = jnp.where(closed, 0.0, flux_y)
    heat = heat + flux_y[:, 1:, :] - flux_y[:, :-1, :]
    return heat


def shards(
    solid_temp, kappa, slope, power, coolant_temp, wall_coeff, channel_map, flow_dir, loop_link
):
    group = lax.axis_index("grp")
    groups = lax.axis_size("grp")
    place = lax.axis_index("loop")
    places = lax.axis_size("loop")
    own_y = solid_temp.shape[1]
    cells_x = solid_temp.shape[2]
    own_count = coolant_temp.shape[0]
    die_local = channel_map.shape[0]
    die_cells = cells_x // die_local
    map_cells = jnp.repeat(channel_map.T, die_cells, axis=1, total_repeat_length=cells_x)
    inverse_map = jnp.argsort(channel_map, axis=1, stable=True)
    inverse_cells = jnp.repeat(inverse_map.T, die_cells, axis=1, total_repeat_length=cells_x)
    own_links = lax.dynamic_slice_in_dim(loop_link, group * own_count, own_count, 0)
    low_edge = group == 0
    high_edge = group == groups - 1
    first_place = place == 0
    last_place = place == places - 1
    temp = solid_temp
    flow = coolant_temp
    for step_index in range(STEPS):
        top_full = lax.all_gather(temp[0], "grp", axis=0, tiled=True)
        own_map = lax.dynamic_slice_in_dim(map_cells, group * own_count, own_count, 0)
        wall_temp = jnp.take_along_axis(top_full, own_map, axis=0)
        flux = wall_coeff * (wall_temp - flow)
        flux_all = lax.all_gather(flux, "grp", axis=0, tiled=True)
        own_inverse = lax.dynamic_slice_in_dim(inverse_cells, group * own_y, own_y, 0)
        sink = jnp.take_along_axis(flux_all, own_inverse, axis=0)
        flow_ext = with_halo(flow, (("loop", 1),), 1)
        left_col = flow_ext[:, 0]
        right_col = flow_ext[:, -1]
        edge_all = lax.all_gather(jnp.stack([left_col, right_col], 1), "grp", axis=0, tiled=True)
        relabel = jnp.take(edge_all, own_links, axis=0)
        left_col = jnp.where(first_place, relabel[:, 0], left_col)
        right_col = jnp.where(last_place, relabel[:, 1], right_col)
        before = jnp.concatenate([left_col[:, None], flow[:, :-1]], 1)
        after = jnp.concatenate([flow[:, 1:], right_col[:, None]], 1)
        upstream = jnp.where(flow_dir[:, None] == 1, before, after)
        new_flow = flow - courant * (flow - upstream) + heat_gain * flux
        cond = kappa * (1.0 + slope * temp)
        temp_ext, cond_ext = (
            with_halo(temp, (("grp", 1), ("loop", 2)), 1),
            with_halo(cond, (("grp", 1), ("loop", 2)), 1),
        )
        heat = block_heat(temp_ext, cond_ext, low_edge, high_edge)
        temp = temp + time_step * (heat + power)
        temp = temp.at[0].add(-time_step * sink)
        flow = new_flow
    return (temp, flow)


def solution(mesh):
    return jax.shard_map(
        shards,
        mesh=mesh,
        in_specs=(
            P(None, "grp", "loop"),
            P(None, "grp", "loop"),
            P(None, "grp", "loop"),
            P(None, "grp", "loop"),
            P("grp", "loop"),
            P("grp", "loop"),
            P("loop", None),
            P("grp"),
            P(),
        ),
        out_specs=(P(None, "grp", "loop"), P("grp", "loop")),
        check_vma=False,
    )
```

profile of v0, /device:TPU:0, one launch (start us, length us, event | category | flops | bytes accessed | tf_op | source)
XLA Modules:
  0.0 759.9 jit_solution(14737480315983378859)
XLA Ops:
  7.2 0.9 fusion.58
  8.1 3.0 collective-permute-start.16
  11.0 3.1 collective-permute-start.17
  14.1 1.8 add_multiply_fusion.1
  16.0 1.7 collective-permute-start.1
  17.9 0.6 iota.21
  18.7 0.5 copy-done.21
  19.5 6.2 all-gather
  25.7 130.5 %gather_fusion = f32[16384]{0:T(1024)S(1)} fusion(f32[256,256]{1,0:T(8,128)S(1)} %bitcast.38, s32[16384]{0:T(1024)S(1)} %bitcast.39), kind=kCustom, calls=%fused_computation.clone | custom fusion | bytes 262144 | tf_op jit(solution)/shard_map/jit(take_along_axis)/gather | solution.py:76
  156.6 5.1 all-gather.2
  161.8 0.6 gather_fusion.3
  162.8 0.7 fusion.55
  163.6 4.7 collective-permute-start.19
  168.3 5.8 all_gather.19
  174.1 1.4 collective-permute-start.5
  175.6 5.1 all-gather.3
  180.8 0.6 gather_fusion.5
  181.5 0.7 slice_select_fusion
  182.2 0.8 broadcast_compare_fusion.1
  182.9 0.5 copy-done.12
  183.7 130.6 %gather_fusion.1 = f32[16384]{0:T(1024)S(1)} fusion(f32[256,256]{1,0:T(8,128)S(1)} %all_gather.19, s32[16384]{0:T(1024)S(1)} %bitcast.41), kind=kCustom, calls=%fused_computation.2.clone | custom fusion | bytes 262144 | tf_op jit(solution)/shard_map/jit(take_along_axis)/gather | solution.py:80
  314.6 2.0 collective-permute-start.3
  317.0 2.8 collective-permute-start.6
  320.1 26.5 %collective-permute-done.2 = f32[12,66,1]{2,1,0:T(8,128)S(1)} collective-permute-done((f32[12,66,1]{2,1,0:T(8,128)S(1)}, f32[12,66,1]{2,1,0:T(8,128)S(1)}, u32[]{:S(2)}, u32[]{:S(2)}) %collective-permute-start.2) | collective-permute-done | bytes 3200 | tf_op jit(solution)/shard_map/ppermute | solution.py:23
  346.6 8.9 %collective-permute-done.6 = f32[12,66,1]{2,1,0:T(8,128)S(1)} collective-permute-done((f32[12,66,1]{2,1,0:T(8,128)S(1)}, f32[12,66,1]{2,1,0:T(8,128)S(1)}, u32[]{:S(2)}, u32[]{:S(2)}) %collective-permute-start.6) | collective-permute-done | bytes 3200 | tf_op jit(solution)/shard_map/ppermute | solution.py:23
  355.5 1.6 fusion.5
  357.1 0.5 fusion.19
  358.7 0.6 fusion.52
  359.3 0.6 fusion.51
  360.0 5.8 all-gather.1
  365.7 201.6 %gather_fusion.2 = f32[16384]{0:T(1024)} fusion(f32[256,256]{1,0:T(8,128)S(1)} %bitcast.37, s32[16384]{0:T(1024)S(1)} %bitcast.40), kind=kCustom, calls=%fused_computation.3.clone | custom fusion | bytes 262144 | tf_op jit(solution)/shard_map/jit(take_along_axis)/gather | solution.py:76
  567.4 0.9 reshape.265
  568.2 0.4 collective-permute-start.8
  568.6 1.4 collective-permute-start.9
  570.0 1.7 fusion.40
  571.7 5.8 all_gather.22
  577.5 130.5 %gather_fusion.4 = f32[16384]{0:T(1024)S(1)} fusion(f32[256,256]{1,0:T(8,128)S(1)} %all_gather.22, s32[16384]{0:T(1024)S(1)} %bitcast.42), kind=kCustom, calls=%fused_computation.4.clone | custom fusion | bytes 262144 | tf_op jit(solution)/shard_map/jit(take_along_axis)/gather | solution.py:80
  708.5 1.4 collective-permute-start.13
  709.9 0.8 pad_maximum_fusion.26
  710.9 1.3 collective-permute-start.10
  712.2 0.7 collective-permute-start.11
  713.3 4.0 collective-permute-start.14
  717.3 1.0 fusion.13
  718.3 24.7 %collective-permute-done.10 = f32[12,66,1]{2,1,0:T(8,128)S(1)} collective-permute-done((f32[12,66,1]{2,1,0:T(8,128)S(1)}, f32[12,66,1]{2,1,0:T(8,128)S(1)}, u32[]{:S(2)}, u32[]{:S(2)}) %collective-permute-start.10) | collective-permute-done | bytes 3200 | tf_op jit(solution)/shard_map/ppermute | solution.py:23
  743.0 7.6 collective-permute-done.14
  750.6 0.8 fusion.1
  751.4 0.5 fusion.16
  752.2 0.9 copy-done.5
  (122 shorter events, 5.3 us)
Async XLA Ops:
  7.2 175.0 %sort.19.cloned.1.call-start = ((), (), s32[]{:S(2)}) async-start(), calls=%async_computation | async-start | bytes 6176 | tf_op jit(solution)/shard_map/jit(argsort)/sort | solution.py:64
  8.1 148.4 %collective-permute-start.16 = (f32[64,1]{1,0:T(8,128)S(1)}, f32[64,1]{1,0:T(8,128)S(1)}, u32[]{:S(2)}, u32[]{:S(2)}) collective-permute-start(f32[64,1]{1,0:T(8,128)S(1)} %get-tuple-element.106), channel_id=1, source_target_pairs={{0,1},{1,2},{2,3},{3,4},{4,5},{5,6},{6,7},{7,0},{8,9},{9,10},{10,1... | collective-permute-start | bytes 776 | tf_op jit(solution)/shard_map/ppermute | solution.py:20
  11.0 6.7 copy-start
  11.0 7.4 copy-start.4
  11.0 145.5 %collective-permute-start.17 = (f32[64,1]{1,0:T(8,128)S(1)}, f32[64,1]{1,0:T(8,128)S(1)}, u32[]{:S(2)}, u32[]{:S(2)}) collective-permute-start(f32[64,1]{1,0:T(8,128)S(1)} %get-tuple-element.105), channel_id=1, source_target_pairs={{1,0},{2,1},{3,2},{4,3},{5,4},{6,5},{7,6},{0,7},{9,8},{10,9},{11,1... | collective-permute-start | bytes 776 | tf_op jit(solution)/shard_map/ppermute | solution.py:23
  16.0 298.3 %collective-permute-start = (f32[12,1,256]{2,1,0:T(1,128)S(1)}, f32[12,1,256]{2,1,0:T(1,128)S(1)}, u32[]{:S(2)}, u32[]{:S(2)}) collective-permute-start(f32[12,1,256]{2,1,0:T(1,128)S(1)} %get-tuple-element.97), channel_id=1, source_target_pairs={{0,8},{8,16},{16,24},{24,0},{1,9},{9,17},{17,25},{25,1},{2,10},{10... | collective-permute-start | bytes 36872 | tf_op jit(solution)/shard_map/ppermute | solution.py:20
  16.0 298.2 %collective-permute-start.1 = (f32[12,1,256]{2,1,0:T(1,128)S(1)}, f32[12,1,256]{2,1,0:T(1,128)S(1)}, u32[]{:S(2)}, u32[]{:S(2)}) collective-permute-start(f32[12,1,256]{2,1,0:T(1,128)S(1)} %get-tuple-element.98), channel_id=1, source_target_pairs={{8,0},{16,8},{24,16},{0,24},{9,1},{17,9},{25,17},{1,25},{10,2},{18... | collective-permute-start | bytes 36872 | tf_op jit(solution)/shard_map/ppermute | solution.py:23
  17.8 298.9 %collective-permute-start.4 = (f32[12,1,256]{2,1,0:T(1,128)S(1)}, f32[12,1,256]{2,1,0:T(1,128)S(1)}, u32[]{:S(2)}, u32[]{:S(2)}) collective-permute-start(f32[12,1,256]{2,1,0:T(1,128)S(1)} %get-tuple-element.95), channel_id=1, source_target_pairs={{0,8},{8,16},{16,24},{24,0},{1,9},{9,17},{17,25},{25,1},{2,10},{10... | collective-permute-start | bytes 36872 | tf_op jit(solution)/shard_map/ppermute | solution.py:20
  18.5 0.7 copy-start.21
  18.5 0.9 slice-start
  19.3 143.3 %copy-start.15 = (pred[64]{0:T(512)(128)(4,1)}, pred[64]{0:T(512)(128)(4,1)S(1)}, u32[]{:S(2)}) copy-start(pred[64]{0:T(512)(128)(4,1)S(1)} %get-tuple-element.81) | copy-start | bytes 196
  19.3 143.3 %copy-start.16 = (s32[64]{0:T(128)}, s32[64]{0:T(128)S(1)}, u32[]{:S(2)}) copy-start(s32[64]{0:T(128)S(1)} %get-tuple-element.82) | copy-start | bytes 772
  19.3 143.3 %copy-start.20 = (s32[64]{0:T(128)}, s32[64]{0:T(128)S(1)}, u32[]{:S(2)}) copy-start(s32[64]{0:T(128)S(1)} %broadcast_add_fusion) | copy-start | bytes 772
  25.7 130.6 %copy-start.25 = (s32[256]{0:T(256)S(1)}, s32[256]{0:T(256)}, u32[]{:S(2)}) copy-start(s32[256]{0:T(256)} %param.35) | copy-start | bytes 3076
  25.7 130.7 %copy-start.26 = (s32[64]{0:T(128)S(1)}, s32[64]{0:T(128)}, u32[]{:S(2)}) copy-start(s32[64]{0:T(128)} %param.34) | copy-start | bytes 772
  25.7 136.9 %copy-start.6 = (f32[64,256]{1,0:T(8,128)S(1)}, f32[64,256]{1,0:T(8,128)}, u32[]{:S(2)}) copy-start(f32[64,256]{1,0:T(8,128)} %param.32) | copy-start | bytes 196612
  156.4 25.0 %copy-start.22 = (pred[64]{0:T(512)(128)(4,1)}, pred[64]{0:T(512)(128)(4,1)S(1)}, u32[]{:S(2)}) copy-start(pred[64]{0:T(512)(128)(4,1)S(1)} %broadcast_compare_fusion.2) | copy-start | bytes 196
  156.4 163.3 %copy-start.23 = (pred[65]{0:T(512)(128)(4,1)}, pred[65]{0:T(512)(128)(4,1)S(1)}, u32[]{:S(2)}) copy-start(pred[65]{0:T(512)(128)(4,1)S(1)} %and_or_fusion) | copy-start | bytes 199
  163.6 10.5 %collective-permute-start.18 = (f32[64,1]{1,0:T(8,128)S(1)}, f32[64,1]{1,0:T(8,128)S(1)}, u32[]{:S(2)}, u32[]{:S(2)}) collective-permute-start(f32[64,1]{1,0:T(8,128)S(1)} %get-tuple-element.102), channel_id=1, source_target_pairs={{0,1},{1,2},{2,3},{3,4},{4,5},{5,6},{6,7},{7,0},{8,9},{9,10},{10,1... | collective-permute-start | bytes 776 | tf_op jit(solution)/shard_map/ppermute | solution.py:20
  163.6 11.9 %collective-permute-start.19 = (f32[64,1]{1,0:T(8,128)S(1)}, f32[64,1]{1,0:T(8,128)S(1)}, u32[]{:S(2)}, u32[]{:S(2)}) collective-permute-start(f32[64,1]{1,0:T(8,128)S(1)} %get-tuple-element.101), channel_id=1, source_target_pairs={{1,0},{2,1},{3,2},{4,3},{5,4},{6,5},{7,6},{0,7},{9,8},{10,9},{11,1... | collective-permute-start | bytes 776 | tf_op jit(solution)/shard_map/ppermute | solution.py:23
  174.1 142.6 %collective-permute-start.5 = (f32[12,1,256]{2,1,0:T(1,128)S(1)}, f32[12,1,256]{2,1,0:T(1,128)S(1)}, u32[]{:S(2)}, u32[]{:S(2)}) collective-permute-start(f32[12,1,256]{2,1,0:T(1,128)S(1)} %get-tuple-element.96), channel_id=1, source_target_pairs={{8,0},{16,8},{24,16},{0,24},{9,1},{17,9},{25,17},{1,25},{10,2},{18... | collective-permute-start | bytes 36872 | tf_op jit(solution)/shard_map/ppermute | solution.py:23
  182.9 0.6 copy-start.17
  314.3 5.5 copy-start.7
  314.6 32.0 %collective-permute-start.2 = (f32[12,66,1]{2,1,0:T(8,128)S(1)}, f32[12,66,1]{2,1,0:T(8,128)S(1)}, u32[]{:S(2)}, u32[]{:S(2)}) collective-permute-start(f32[12,66,1]{2,1,0:T(8,128)S(1)} %get-tuple-element.87), channel_id=1, source_target_pairs={{1,0},{2,1},{3,2},{4,3},{5,4},{6,5},{7,6},{0,7},{9,8},{10,9},{11,1... | collective-permute-start | bytes 9512 | tf_op jit(solution)/shard_map/ppermute | solution.py:23
  314.6 31.9 %collective-permute-start.3 = (f32[12,66,1]{2,1,0:T(8,128)S(1)}, f32[12,66,1]{2,1,0:T(8,128)S(1)}, u32[]{:S(2)}, u32[]{:S(2)}) collective-permute-start(f32[12,66,1]{2,1,0:T(8,128)S(1)} %get-tuple-element.88), channel_id=1, source_target_pairs={{0,1},{1,2},{2,3},{3,4},{4,5},{5,6},{6,7},{7,0},{8,9},{9,10},{10,1... | collective-permute-start | bytes 9512 | tf_op jit(solution)/shard_map/ppermute | solution.py:20
  316.6 3.1 copy-start.8
  316.7 3.1 copy-start.9
  317.0 38.5 %collective-permute-start.6 = (f32[12,66,1]{2,1,0:T(8,128)S(1)}, f32[12,66,1]{2,1,0:T(8,128)S(1)}, u32[]{:S(2)}, u32[]{:S(2)}) collective-permute-start(f32[12,66,1]{2,1,0:T(8,128)S(1)} %get-tuple-element.89), channel_id=1, source_target_pairs={{1,0},{2,1},{3,2},{4,3},{5,4},{6,5},{7,6},{0,7},{9,8},{10,9},{11,1... | collective-permute-start | bytes 9512 | tf_op jit(solution)/shard_map/ppermute | solution.py:23
  319.8 35.7 %collective-permute-start.7 = (f32[12,66,1]{2,1,0:T(8,128)S(1)}, f32[12,66,1]{2,1,0:T(8,128)S(1)}, u32[]{:S(2)}, u32[]{:S(2)}) collective-permute-start(f32[12,66,1]{2,1,0:T(8,128)S(1)} %get-tuple-element.90), channel_id=1, source_target_pairs={{0,1},{1,2},{2,3},{3,4},{4,5},{5,6},{6,7},{7,0},{8,9},{9,10},{10,1... | collective-permute-start | bytes 9512 | tf_op jit(solution)/shard_map/ppermute | solution.py:20
  320.1 36.9 %copy-start.1 = (f32[12,64,256]{2,1,0:T(8,128)S(1)}, f32[12,64,256]{2,1,0:T(8,128)}, u32[]{:S(2)}) copy-start(f32[12,64,256]{2,1,0:T(8,128)} %param.30) | copy-start | bytes 2359300
  357.1 0.6 copy-start.13
  357.1 0.7 copy-start.18
  357.1 1.1 copy-start.2
  357.1 1.4 copy-start.3
  568.2 141.7 %collective-permute-start.8 = (f32[12,1,256]{2,1,0:T(1,128)}, f32[12,1,256]{2,1,0:T(1,128)S(1)}, u32[]{:S(2)}, u32[]{:S(2)}) collective-permute-start(f32[12,1,256]{2,1,0:T(1,128)} %get-tuple-element.93), channel_id=1, source_target_pairs={{0,8},{8,16},{16,24},{24,0},{1,9},{9,17},{17,25},{25,1},{2,10},{10... | collective-permute-start | bytes 36872 | tf_op jit(solution)/shard_map/ppermute | solution.py:20
  568.6 141.3 %collective-permute-start.9 = (f32[12,1,256]{2,1,0:T(1,128)}, f32[12,1,256]{2,1,0:T(1,128)}, u32[]{:S(2)}, u32[]{:S(2)}) collective-permute-start(f32[12,1,256]{2,1,0:T(1,128)} %get-tuple-element.94), channel_id=1, source_target_pairs={{8,0},{16,8},{24,16},{0,24},{9,1},{17,9},{25,17},{1,25},{10,2},{18... | collective-permute-start | bytes 36872 | tf_op jit(solution)/shard_map/ppermute | solution.py:23
  577.5 130.6 %copy-start.11 = (f32[12,1,256]{2,1,0:T(1,128)S(1)}, f32[12,1,256]{2,1,0:T(1,128)}, u32[]{:S(2)}) copy-start(f32[12,1,256]{2,1,0:T(1,128)} %get-tuple-element.91) | copy-start | bytes 36868
  577.5 131.0 %copy-start.10 = (f32[12,1,256]{2,1,0:T(1,128)S(1)}, f32[12,1,256]{2,1,0:T(1,128)}, u32[]{:S(2)}) copy-start(f32[12,1,256]{2,1,0:T(1,128)} %get-tuple-element.92) | copy-start | bytes 36868
  708.1 4.9 collective-permute-start.12
  708.5 4.5 collective-permute-start.13
  710.9 32.1 %collective-permute-start.10 = (f32[12,66,1]{2,1,0:T(8,128)S(1)}, f32[12,66,1]{2,1,0:T(8,128)S(1)}, u32[]{:S(2)}, u32[]{:S(2)}) collective-permute-start(f32[12,66,1]{2,1,0:T(8,128)S(1)} %get-tuple-element.83), channel_id=1, source_target_pairs={{1,0},{2,1},{3,2},{4,3},{5,4},{6,5},{7,6},{0,7},{9,8},{10,9},{11,1... | collective-permute-start | bytes 9512 | tf_op jit(solution)/shard_map/ppermute | solution.py:23
  712.2 30.8 %collective-permute-start.11 = (f32[12,66,1]{2,1,0:T(8,128)S(1)}, f32[12,66,1]{2,1,0:T(8,128)S(1)}, u32[]{:S(2)}, u32[]{:S(2)}) collective-permute-start(f32[12,66,1]{2,1,0:T(8,128)S(1)} %get-tuple-element.84), channel_id=1, source_target_pairs={{0,1},{1,2},{2,3},{3,4},{4,5},{5,6},{6,7},{7,0},{8,9},{9,10},{10,1... | collective-permute-start | bytes 9512 | tf_op jit(solution)/shard_map/ppermute | solution.py:20
  713.1 4.2 copy-start.24
  713.3 37.3 %collective-permute-start.14 = (f32[12,66,1]{2,1,0:T(8,128)S(1)}, f32[12,66,1]{2,1,0:T(8,128)S(1)}, u32[]{:S(2)}, u32[]{:S(2)}) collective-permute-start(f32[12,66,1]{2,1,0:T(8,128)S(1)} %get-tuple-element.85), channel_id=1, source_target_pairs={{1,0},{2,1},{3,2},{4,3},{5,4},{6,5},{7,6},{0,7},{9,8},{10,9},{11,1... | collective-permute-start | bytes 9512 | tf_op jit(solution)/shard_map/ppermute | solution.py:23
  717.3 33.3 %collective-permute-start.15 = (f32[12,66,1]{2,1,0:T(8,128)S(1)}, f32[12,66,1]{2,1,0:T(8,128)S(1)}, u32[]{:S(2)}, u32[]{:S(2)}) collective-permute-start(f32[12,66,1]{2,1,0:T(8,128)S(1)} %get-tuple-element.86), channel_id=1, source_target_pairs={{0,1},{1,2},{2,3},{3,4},{4,5},{5,6},{6,7},{7,0},{8,9},{9,10},{10,1... | collective-permute-start | bytes 9512 | tf_op jit(solution)/shard_map/ppermute | solution.py:20
  751.4 0.6 copy-start.14
  751.4 0.7 copy-start.19
  752.2 0.9 copy-start.5
  (1 other events, 0.5 us)
Sparse Core Ops, SparseCore 0:
  18.6 2.5 sort.21.cloned.1.call-done
  (1 shorter events, 0.0 us)
where the time goes:
time: 761 us; the launch traced here: 760 us
  local copies, waits for them, and re-layouts  603 us (79%)
  waiting for transfers between devices  67.6 us (9%)
  blocking collectives  33.7 us (4%)
  starting transfers between devices  28.6 us (4%)
  between operations  14.6 us (2%)
  other arithmetic  12 us (2%)
    gather x4, local copies, waits for them, and re-layouts, shards(): wall_temp = jnp.take_along_axis(top_full, own_map, axis=0)  333 us
    gather x4, local copies, waits for them, and re-layouts, shards(): sink = jnp.take_along_axis(flux_all, own_inverse, axis=0)  261 us
    ppermute x10, waiting for transfers between devices, with_halo(): lax.ppermute(lax.slice_in_dim(block, 0, width, axis=dim), axis, backward)  67.6 us
    ppermute x10, starting transfers between devices, with_halo(): lax.ppermute(lax.slice_in_dim(block, 0, width, axis=dim), axis, backward)  22 us
  transfers between devices with their start and end apart: 20, of which 4 were waited for; matrix products, arithmetic and copies ran while one was open for 53% of the time, Pallas kernels for 0%

commit v1 on v0

v1 whole, which is shorter than its diff:
```python
import jax
import jax.numpy as jnp
from jax import lax
from jax.experimental import pallas as pl
from jax.experimental.pallas import tpu as pltpu
from jax.sharding import PartitionSpec as P

time_step = 0.06
courant = 0.5
heat_gain = 0.5
TILE = 128
F32 = jnp.float32
BF16 = jnp.bfloat16


def split3(value):
    high = value.astype(BF16)
    rest = value - high.astype(F32)
    middle = rest.astype(BF16)
    low = (rest - middle.astype(F32)).astype(BF16)
    return high, middle, low


def pick(chooser, value, dims):
    total = None
    for part in split3(value):
        term = lax.dot_general(chooser, part, (dims, ((), ())), preferred_element_type=F32)
        total = term if total is None else total + term
    return total


def pick_rows(value, chooser):
    total = None
    for part in split3(value):
        term = lax.dot_general(part, chooser, (((1,), (0,)), ((), ())), preferred_element_type=F32)
        total = term if total is None else total + term
    return total


def one_hot(index_row, first, count):
    shape = (count, index_row.shape[1])
    here = lax.broadcasted_iota(jnp.int32, shape, 0) + first
    return jnp.where(index_row == here, 1.0, 0.0).astype(BF16)


def face(cond_a, cond_b, temp_a, temp_b):
    return 0.5 * (cond_a + cond_b) * (temp_b - temp_a)


def closed_heat(temp_ref, kappa_ref, slope_ref, emit):
    layers, rows, cols = temp_ref.shape
    lane = lax.broadcasted_iota(jnp.int32, (rows, cols), 1)
    row = lax.broadcasted_iota(jnp.int32, (rows, cols), 0)
    temp = temp_ref[0]
    cond = kappa_ref[0] * (1.0 + slope_ref[0] * temp)
    flux_below = None
    for z in range(layers):
        flux_x = face(cond, pltpu.roll(cond, cols - 1, 1), temp, pltpu.roll(temp, cols - 1, 1))
        flux_x = jnp.where(lane == cols - 1, 0.0, flux_x)
        heat = flux_x - pltpu.roll(flux_x, 1, 1)
        flux_y = face(cond, pltpu.roll(cond, rows - 1, 0), temp, pltpu.roll(temp, rows - 1, 0))
        flux_y = jnp.where(row == rows - 1, 0.0, flux_y)
        heat = heat + flux_y - pltpu.roll(flux_y, 1, 0)
        if flux_below is not None:
            heat = heat - flux_below
        if z + 1 < layers:
            temp_up = temp_ref[z + 1]
            cond_up = kappa_ref[z + 1] * (1.0 + slope_ref[z + 1] * temp_up)
            flux_below = face(cond, cond_up, temp, temp_up)
            heat = heat + flux_below
        emit(z, temp, cond, heat)
        if z + 1 < layers:
            temp, cond = temp_up, cond_up


def open_kernel(
    temp_ref, kappa_ref, slope_ref, power_ref, flow_ref, wall_ref, dir_ref,
    next_ref, ya_ref, yb_ref, share_ref, tmp_ref, row_ref,
):
    layers, rows, cols = temp_ref.shape
    group = lax.axis_index("grp")
    even = lax.rem(group, 2) == 0

    def emit(z, temp, cond, heat):
        next_ref[z] = temp + time_step * (heat + power_ref[z])

    closed_heat(temp_ref, kappa_ref, slope_ref, emit)
    for q, ref in enumerate((next_ref, temp_ref, kappa_ref, slope_ref)):
        for z in range(layers):
            first = ref[z, 0:1, :]
            last = ref[z, rows - 1 : rows, :]
            at = q * layers + z
            ya_ref[at : at + 1, :] = jnp.where(even, last, first)
            yb_ref[at : at + 1, :] = jnp.where(even, first, last)
    share_ref[0:rows, :] = flow_ref[...]
    share_ref[rows : 2 * rows, :] = wall_ref[...]
    lane = lax.broadcasted_iota(jnp.int32, (rows, TILE), 1)
    left = temp_ref[0, :, 0:TILE]
    right = temp_ref[0, :, cols - TILE : cols]
    tmp_ref[...] = jnp.zeros_like(tmp_ref)
    tmp_ref[0:rows, :] = jnp.where(lane == 0, left, pltpu.roll(right, 2, 1))
    turned = tmp_ref[...].T
    row_ref[...] = jnp.zeros_like(row_ref)
    row_ref[0:8, 0:TILE] = turned[0:8, :]
    row_ref[2:3, 0:rows] = dir_ref[...].astype(F32)
    share_ref[2 * rows :, :] = pltpu.roll(row_ref[...], group * rows, 1)


def edge_kernel(
    first_ref, temp_ref, kappa_ref, slope_ref, ya_ref, yb_ref, share_ref, map_ref,
    next_ref, yo_ref, sa_ref, sb_ref, fw_ref, crow_ref, strip_ref, small_ref,
):
    layers, rows, cols = temp_ref.shape
    span = 2 * rows + 8
    groups = share_ref.shape[0] // span
    group = lax.axis_index("grp")
    even = lax.rem(group, 2) == 0
    place_even = lax.rem(lax.axis_index("loop"), 2) == 0
    ya, yb = ya_ref[...], yb_ref[...]
    low, high = jnp.where(even, yb, ya), jnp.where(even, ya, yb)
    yo_ref[0 : 4 * layers, :] = low
    yo_ref[4 * layers :, :] = high
    low_open = jnp.where(group == 0, 0.0, 1.0)
    high_open = jnp.where(group == groups - 1, 0.0, 1.0)

    flow_all = jnp.concatenate([share_ref[i * span : i * span + rows, :] for i in range(groups)], 0)
    wall_all = jnp.concatenate(
        [share_ref[i * span + rows : i * span + 2 * rows, :] for i in range(groups)], 0
    )
    extra = share_ref[2 * rows : span, :]
    for i in range(1, groups):
        extra = extra + share_ref[i * span + 2 * rows : (i + 1) * span, :]
    chooser = one_hot(map_ref[...], group * rows - 8, rows + 16)
    both = pick(chooser, jnp.concatenate([flow_all, wall_all], 1), ((1,), (0,)))
    flow_y, wall_y = both[:, :cols], both[:, cols:]
    fw_ref[0:rows, :] = flow_y[8 : 8 + rows]
    fw_ref[rows:, :] = wall_y[8 : 8 + rows]
    sink = wall_y[8 : 8 + rows] * (temp_ref[0] - flow_y[8 : 8 + rows])
    temp_low, temp_high = yo_ref[layers : layers + 1, :], yo_ref[5 * layers : 5 * layers + 1, :]
    sink_low = wall_y[7:8] * (temp_low - flow_y[7:8])
    sink_high = wall_y[8 + rows : 9 + rows] * (temp_high - flow_y[8 + rows : 9 + rows])

    row = lax.broadcasted_iota(jnp.int32, (rows, cols), 0)
    lane = lax.broadcasted_iota(jnp.int32, (rows, TILE), 1)
    small_ref[...] = jnp.zeros_like(small_ref)
    lane1 = lax.broadcasted_iota(jnp.int32, (1, TILE), 1)
    for z in range(layers):
        temp, kappa, slope = temp_ref[z], kappa_ref[z], slope_ref[z]
        after = first_ref[z]
        edges = []
        for side, base, at, opened, sunk in (
            (0, 0, 0, low_open, sink_low),
            (1, 4 * layers, rows - 1, high_open, sink_high),
        ):
            temp_h = yo_ref[base + layers + z : base + layers + z + 1, :]
            cond_h = yo_ref[base + 2 * layers + z : base + 2 * layers + z + 1, :] * (
                1.0 + yo_ref[base + 3 * layers + z : base + 3 * layers + z + 1, :] * temp_h
            )
            temp_e = temp[at : at + 1]
            cond_e = kappa[at : at + 1] * (1.0 + slope[at : at + 1] * temp_e)
            flux = opened * face(cond_e, cond_h, temp_e, temp_h)
            halo = yo_ref[base + z : base + z + 1, :] - time_step * flux
            if z == 0:
                halo = halo - time_step * sunk
            yo_ref[base + z : base + z + 1, :] = halo
            edges.append(time_step * flux)
            corner = jnp.where(
                lane1 == 0,
                temp_h[:, 0:TILE],
                jnp.where(
                    lane1 == 1,
                    pltpu.roll(cond_h[:, 0:TILE], 1, 1),
                    jnp.where(
                        lane1 == 4,
                        pltpu.roll(temp_h[:, cols - TILE :], 5, 1),
                        pltpu.roll(cond_h[:, cols - TILE :], 6, 1),
                    ),
                ),
            )
            small_ref[16 * side + z : 16 * side + z + 1, :] = corner
        after = after + jnp.where(row == 0, edges[0], jnp.where(row == rows - 1, edges[1], 0.0))
        if z == 0:
            after = after - time_step * sink
        next_ref[z] = after
        packed = None
        for n, value in enumerate((after, temp, kappa, slope)):
            left = value[:, 0:TILE]
            right = pltpu.roll(value[:, cols - TILE :], n + 5, 1)
            left = pltpu.roll(left, n, 1) if n else left
            packed = left if packed is None else jnp.where(lane == n, left, packed)
            packed = jnp.where(lane == n + 4, right, packed)
        strip_ref[z * rows : (z + 1) * rows, :] = packed
    strips = strip_ref[...].T[0:8, :]
    corners = small_ref[...].T[0:8, :]

    lane_c = lax.broadcasted_iota(jnp.int32, (groups * rows, TILE), 1)
    right_flow = flow_all[:, cols - TILE :]
    pack = jnp.where(lane_c < 2, flow_all[:, 0:TILE], pltpu.roll(right_flow, 4, 1))
    pack = jnp.where(lane_c == 4, pltpu.roll(wall_all[:, 0:TILE], 4, 1), pack)
    pack = jnp.where(lane_c == 5, pltpu.roll(wall_all[:, cols - TILE :], 6, 1), pack)
    turned = pack.T
    flow_0, flow_1 = turned[0:1], turned[1:2]
    flow_m, flow_e = turned[2:3], turned[3:4]
    wall_0, wall_e = turned[4:5], turned[5:6]
    top = pick_rows(extra, one_hot(map_ref[...], 0, groups * rows))
    toward = extra[2:3]
    flux_0 = wall_0 * (top[0:1] - flow_0)
    flux_e = wall_e * (top[1:2] - flow_e)
    part_0 = (1.0 - courant) * flow_0 + courant * (1.0 - toward) * flow_1 + heat_gain * flux_0
    part_e = (1.0 - courant) * flow_e + courant * toward * flow_m + heat_gain * flux_e
    crow_ref[...] = jnp.zeros_like(crow_ref)
    crow_ref[0:1, :] = toward
    crow_ref[1:2, :] = flow_0
    crow_ref[2:3, :] = flow_e
    width = sa_ref.shape[1]
    channels = groups * rows
    for ref, pick_right in ((sa_ref, place_even), (sb_ref, jnp.logical_not(place_even))):
        ref[...] = jnp.zeros_like(ref)
        ref[0:4, :] = jnp.where(pick_right, strips[4:8], strips[0:4])
        ref[4:6, 0:TILE] = jnp.where(pick_right, corners[4:6], corners[0:2])
        ref[6:7, 0:channels] = jnp.where(pick_right, flow_e, flow_0)
        ref[7:8, 0:channels] = jnp.where(pick_right, part_e, part_0)


def close_kernel(
    temp_ref, kappa_ref, slope_ref, power_ref, top_ref, yo_ref, ra_ref, rb_ref, sa_ref, sb_ref,
    fw_ref, crow_ref, map_ref, link_ref,
    out_ref, flow_ref, wide_ref, xt_ref, xc_ref, xf_ref, full_ref,
):
    layers, rows, cols = temp_ref.shape
    group, groups = lax.axis_index("grp"), lax.axis_size("grp")
    place, places = lax.axis_index("loop"), lax.axis_size("loop")
    even = lax.rem(place, 2) == 0
    channels = crow_ref.shape[1]
    low_open = jnp.where(group == 0, 0.0, 1.0)
    high_open = jnp.where(group == groups - 1, 0.0, 1.0)
    got_a, got_b, own_a, own_b = ra_ref[...], rb_ref[...], sa_ref[...], sb_ref[...]
    got = (jnp.where(even, got_b, got_a), jnp.where(even, got_a, got_b))
    own = (jnp.where(even, own_b, own_a), jnp.where(even, own_a, own_b))

    def turn(first, last, ref):
        wide_ref[0:1, 0 : first.shape[1]] = first
        wide_ref[TILE - 1 : TILE, 0 : last.shape[1]] = last
        ref[...] = wide_ref[:, 0 : ref.shape[0]].T

    wide_ref[...] = jnp.zeros_like(wide_ref)
    temps, conds, fluxes = [], [], []
    for side in range(2):
        temp_n, temp_o = got[side][1:2], own[side][1:2]
        cond_n = got[side][2:3] * (1.0 + got[side][3:4] * temp_n)
        cond_o = own[side][2:3] * (1.0 + own[side][3:4] * temp_o)
        flux = time_step * face(cond_o, cond_n, temp_o, temp_n)
        after = got[side][0:1] - flux
        temps.append(after)
        conds.append(got[side][2:3] * (1.0 + got[side][3:4] * after))
        fluxes.append(flux)
    turn(temps[0], temps[1], xt_ref)
    turn(conds[0], conds[1], xc_ref)
    turn(fluxes[0], fluxes[1], xf_ref)

    wide_ref[0:1, 0:TILE] = got[0][4:5, 0:TILE]
    wide_ref[TILE - 1 : TILE, 0:TILE] = got[1][4:5, 0:TILE]
    corner_t = wide_ref[:, 0:TILE].T
    wide_ref[0:1, 0:TILE] = got[0][5:6, 0:TILE]
    wide_ref[TILE - 1 : TILE, 0:TILE] = got[1][5:6, 0:TILE]
    corner_c = wide_ref[:, 0:TILE].T
    lane_l = lax.broadcasted_iota(jnp.int32, (layers, TILE), 1)
    halo = []
    for side in range(2):
        base = 4 * layers * side
        after = yo_ref[base : base + layers, :]
        before = yo_ref[base + layers : base + 2 * layers, :]
        kappa = yo_ref[base + 2 * layers : base + 3 * layers, :]
        slope = yo_ref[base + 3 * layers : base + 4 * layers, :]
        cond = kappa * (1.0 + slope * before)
        c_t, c_c = corner_t[16 * side : 16 * side + layers], corner_c[16 * side : 16 * side + layers]
        tiles = []
        for start, at in ((0, 0), (cols - TILE, TILE - 1)):
            flux = time_step * face(
                cond[:, start : start + TILE], c_c, before[:, start : start + TILE], c_t
            )
            tiles.append(after[:, start : start + TILE] + jnp.where(lane_l == at, flux, 0.0))
        after = jnp.concatenate([tiles[0], after[:, TILE : cols - TILE], tiles[1]], 1) if (
            cols > 2 * TILE
        ) else jnp.concatenate(tiles, 1)
        halo.append((after, kappa * (1.0 + slope * after)))

    lane = lax.broadcasted_iota(jnp.int32, (rows, TILE), 1)
    for z in range(layers):
        add = xf_ref[z * rows : (z + 1) * rows, :]
        full_ref[z] = temp_ref[z]
        full_ref[z, :, 0:TILE] = temp_ref[z, :, 0:TILE] + jnp.where(lane == 0, add, 0.0)
        full_ref[z, :, cols - TILE :] = temp_ref[z, :, cols - TILE :] + jnp.where(
            lane == TILE - 1, add, 0.0
        )

    toward_c = crow_ref[0:1, :]
    first_place = place == 0
    last_place = place == places - 1
    link = one_hot(link_ref[...], 0, channels)
    stack = jnp.concatenate(
        [got[0][6:7, 0:channels], got[1][6:7, 0:channels], crow_ref[1:3, :], crow_ref[4:8, :]], 0
    )
    moved = pick_rows(stack, link)
    own_0 = jnp.where(first_place, moved[2:3], stack[2:3])
    own_e = jnp.where(last_place, moved[3:4], stack[3:4])
    late_l = got[0][7:8, 0:channels] + courant * (1.0 - toward_c) * own_0
    late_r = got[1][7:8, 0:channels] + courant * toward_c * own_e
    late = jnp.concatenate([late_l, late_r, crow_ref[2:8, :]], 0)
    late_moved = pick_rows(late, link)
    edge_rows = (
        (jnp.where(first_place, moved[0:1], stack[0:1]), jnp.where(last_place, moved[1:2], stack[1:2])),
        (jnp.where(first_place, late_moved[0:1], late_l), jnp.where(last_place, late_moved[1:2], late_r)),
    )
    chooser = one_hot(map_ref[...], group * rows, rows)
    wide_row = lax.broadcasted_iota(jnp.int32, (TILE, channels), 0)
    edge_y = [
        pick(chooser, jnp.where(wide_row == 0, pair[0], pair[1]), ((1,), (1,))) for pair in edge_rows
    ]
    toward = pick(chooser, jnp.broadcast_to(toward_c, (TILE, channels)), ((1,), (1,)))
    toward = jnp.concatenate([toward] * (cols // TILE), 1) > 0.5
    lane_w = lax.broadcasted_iota(jnp.int32, (rows, cols), 1)

    def upstream(flow, edge):
        edges = jnp.concatenate([edge] * (cols // TILE), 1)
        before = jnp.where(lane_w == 0, edges, pltpu.roll(flow, 1, 1))
        after = jnp.where(lane_w == cols - 1, edges, pltpu.roll(flow, cols - 1, 1))
        return jnp.where(toward, before, after)

    flow, wall = fw_ref[0:rows, :], fw_ref[rows:, :]
    flux = wall * (top_ref[0] - flow)
    flow = flow - courant * (flow - upstream(flow, edge_y[0])) + heat_gain * flux
    flux = wall * (full_ref[0] - flow)
    flow_ref[...] = flow - courant * (flow - upstream(flow, edge_y[1])) + heat_gain * flux

    row8 = lax.broadcasted_iota(jnp.int32, (8, cols), 0)

    def emit(z, temp, cond, heat):
        result = temp + time_step * (heat + power_ref[z])
        if z == 0:
            result = result - time_step * flux
        halo_t = xt_ref[z * rows : (z + 1) * rows, :]
        halo_c = xc_ref[z * rows : (z + 1) * rows, :]
        sides = []
        for start, at in ((0, 0), (cols - TILE, TILE - 1)):
            part = slice(start, start + TILE)
            extra = time_step * face(cond[:, part], halo_c, temp[:, part], halo_t)
            sides.append(jnp.where(lane == at, extra, 0.0))
        middle = [jnp.zeros((rows, cols - 2 * TILE), F32)] if cols > 2 * TILE else []
        result = result + jnp.concatenate([sides[0]] + middle + [sides[1]], 1)
        out_ref[z] = result
        for side, opened, start, at in ((0, low_open, 0, 0), (1, high_open, rows - 8, 7)):
            part = slice(start, start + 8)
            extra = (time_step * opened) * face(
                cond[part], halo[side][1][z : z + 1], temp[part], halo[side][0][z : z + 1]
            )
            out_ref[z, part, :] = result[part] + jnp.where(row8 == at, extra, 0.0)

    closed_heat(full_ref, kappa_ref, slope_ref, emit)


def return_kernel(flow_ref, map_ref, out_ref, tmp_ref):
    rows = out_ref.shape[0]
    group = lax.axis_index("grp")
    chooser = one_hot(map_ref[...], 0, flow_ref.shape[0])
    tmp_ref[...] = pick(chooser, flow_ref[...], ((0,), (0,)))
    out_ref[...] = tmp_ref[pl.ds(pl.multiple_of(group * rows, 8), rows), :]


def pairs(count, first, closed):
    swaps = []
    for low in range(first, count, 2):
        high = low + 1
        if high == count:
            if not closed:
                continue
            high = 0
        swaps += [(low, high), (high, low)]
    return swaps


def shards(
    solid_temp, kappa, slope, power, coolant_temp, wall_coeff, channel_map, flow_dir, loop_link
):
    groups, places = lax.axis_size("grp"), lax.axis_size("loop")
    layers, rows, cols = solid_temp.shape
    channels = groups * rows
    strip = layers * rows
    params = pltpu.CompilerParams(vmem_limit_bytes=48 * 1024 * 1024)

    def shape(*dims):
        return jax.ShapeDtypeStruct(dims, F32)

    def call(body, outs, scratch, *args):
        return pl.pallas_call(
            body,
            out_shape=outs,
            scratch_shapes=[pltpu.VMEM(dims, F32) for dims in scratch],
            compiler_params=params,
        )(*args)

    link = loop_link.reshape(1, channels)
    first, ya, yb, share = call(
        open_kernel,
        (shape(layers, rows, cols), shape(4 * layers, cols), shape(4 * layers, cols), shape(2 * rows + 8, cols)),
        [(TILE, TILE), (8, cols)],
        solid_temp, kappa, slope, power, coolant_temp, wall_coeff, flow_dir.reshape(1, rows),
    )
    ya = lax.ppermute(ya, "grp", pairs(groups, 0, False))
    yb = lax.ppermute(yb, "grp", pairs(groups, 1, False))
    share = lax.all_gather(share, "grp", axis=0, tiled=True)
    after, yo, sa, sb, fw, crow = call(
        edge_kernel,
        (
            shape(layers, rows, cols), shape(8 * layers, cols), shape(8, strip), shape(8, strip),
            shape(2 * rows, cols), shape(8, channels),
        ),
        [(strip, TILE), (TILE, TILE)],
        first, solid_temp, kappa, slope, ya, yb, share, channel_map,
    )
    ra = lax.ppermute(sa, "loop", pairs(places, 0, True))
    rb = lax.ppermute(sb, "loop", pairs(places, 1, True))
    temp, flow = call(
        close_kernel,
        (shape(layers, rows, cols), shape(rows, cols)),
        [(TILE, strip), (strip, TILE), (strip, TILE), (strip, TILE), (layers, rows, cols)],
        after, kappa, slope, power, solid_temp[0:1], yo, ra, rb, sa, sb, fw, crow, channel_map, link,
    )
    flow = lax.all_gather(flow, "grp", axis=0, tiled=True)
    flow = call(return_kernel, shape(rows, cols), [(channels, cols)], flow, channel_map)
    return (temp, flow)


def solution(mesh):
    block = P(None, "grp", "loop")
    plane = P("grp", "loop")
    return jax.shard_map(
        shards,
        mesh=mesh,
        in_specs=(block, block, block, block, plane, plane, P("loop", None), P("grp"), P()),
        out_specs=(block, plane),
        check_vma=False,
    )
```

time: 761 us -> 41.1 us (0.05)
  local copies, waits for them, and re-layouts: 603 us -> 8.21 us
  waiting for transfers between devices: 67.6 us -> 2.97 us
  starting transfers between devices: 28.6 us -> 6.92 us
  blocking collectives: 33.7 us -> 15.3 us
  between operations: 14.6 us -> 0.69 us
  other arithmetic: 12 us -> 0 us
    gather x10 -> x0, local copies, waits for them, and re-layouts: 595 us -> none  [the longest x4 333 us: shards(): wall_temp = jnp.take_along_axis(top_full, own_map, axis=0)]
    ppermute x20 -> x4, waiting for transfers between devices: 67.6 us -> 2.97 us  [the longest x1 2.97 us: shards(): rb = lax.ppermute(sb, 'loop', pairs(places, 1, True))]
    ppermute x20 -> x4, starting transfers between devices: 28.6 us -> 6.92 us  [the longest x1 3.54 us: shards(): rb = lax.ppermute(sb, 'loop', pairs(places, 1, True))]
    all_gather x6 -> x2, blocking collectives: 33.7 us -> 15.3 us  [the longest x1 9.5 us: shards(): share = lax.all_gather(share, 'grp', axis=0, tiled=True)]
  transfers between devices with their start and end apart: 20 -> 4, of which waited for: 4 -> 1; matrix products, arithmetic and copies ran while one was open for 53% -> 0% of each run, Pallas kernels for 0% -> 0%
where the time goes in v1:
time: 41.1 us; the launch traced here: 40.6 us
  blocking collectives  15.3 us (37%)
  local copies, waits for them, and re-layouts  8.21 us (20%)
  starting transfers between devices  6.92 us (17%)
  Pallas kernels  6.56 us (16%)
  waiting for transfers between devices  2.97 us (7%)
  between operations  0.69 us (2%)
    all_gather x1, blocking collectives, shards(): share = lax.all_gather(share, 'grp', axis=0, tiled=True)  9.5 us
    unnamed x24, local copies, waits for them, and re-layouts  8.21 us
    pallas_call x4, Pallas kernels, call(): pl.pallas_call(body, out_shape=outs, scratch_shapes=[pltpu.VMEM(dims, F32...  6.56 us
    all_gather x1, blocking collectives, shards(): flow = lax.all_gather(flow, 'grp', axis=0, tiled=True)  5.77 us
    ppermute x1, starting transfers between devices, shards(): rb = lax.ppermute(sb, 'loop', pairs(places, 1, True))  3.54 us
    ppermute x1, waiting for transfers between devices, shards(): rb = lax.ppermute(sb, 'loop', pairs(places, 1, True))  2.97 us
    ppermute x1, starting transfers between devices, shards(): ra = lax.ppermute(sa, 'loop', pairs(places, 0, True))  2.21 us
  transfers between devices with their start and end apart: 4, of which 1 were waited for; matrix products, arithmetic and copies ran while one was open for 0% of the time, Pallas kernels for 0%

profile of v1, /device:TPU:0, one launch (start us, length us, event | category | flops | bytes accessed | tf_op | source)
XLA Modules:
  0.0 40.6 jit_solution(1255605956621218575)
XLA Ops:
  0.6 0.0 copy-start.11
  0.6 0.6 %copy-done.11 = s32[64]{0:T(128)S(1)} copy-done((s32[64]{0:T(128)S(1)}, s32[64]{0:T(128)}, u32[]{:S(2)}) %copy-start.11) | copy-done | bytes 280
  1.3 0.0 copy-start
  1.3 1.1 %copy-done = f32[12,64,256]{2,1,0:T(8,128)S(1)} copy-done((f32[12,64,256]{2,1,0:T(8,128)S(1)}, f32[12,64,256]{2,1,0:T(8,128)}, u32[]{:S(2)}) %copy-start) | copy-done | bytes 786456
  2.4 0.0 copy-start.2
  2.4 1.1 %copy-done.2 = f32[12,64,256]{2,1,0:T(8,128)S(1)} copy-done((f32[12,64,256]{2,1,0:T(8,128)S(1)}, f32[12,64,256]{2,1,0:T(8,128)}, u32[]{:S(2)}) %copy-start.2) | copy-done | bytes 786456
  3.6 0.0 copy-start.4
  3.6 1.1 %copy-done.4 = f32[12,64,256]{2,1,0:T(8,128)S(1)} copy-done((f32[12,64,256]{2,1,0:T(8,128)S(1)}, f32[12,64,256]{2,1,0:T(8,128)}, u32[]{:S(2)}) %copy-start.4) | copy-done | bytes 786456
  4.7 0.0 copy-start.5
  4.7 1.1 %copy-done.5 = f32[12,64,256]{2,1,0:T(8,128)S(1)} copy-done((f32[12,64,256]{2,1,0:T(8,128)S(1)}, f32[12,64,256]{2,1,0:T(8,128)}, u32[]{:S(2)}) %copy-start.5) | copy-done | bytes 786456
  5.8 0.0 copy-start.7
  5.8 0.8 %copy-done.7 = f32[64,256]{1,0:T(8,128)S(1)} copy-done((f32[64,256]{1,0:T(8,128)S(1)}, f32[64,256]{1,0:T(8,128)}, u32[]{:S(2)}) %copy-start.7) | copy-done | bytes 65560
  6.7 0.0 copy-start.8
  6.7 0.8 %copy-done.8 = f32[64,256]{1,0:T(8,128)S(1)} copy-done((f32[64,256]{1,0:T(8,128)S(1)}, f32[64,256]{1,0:T(8,128)}, u32[]{:S(2)}) %copy-start.8) | copy-done | bytes 65560
  7.5 1.5 %shard_map.104 = (f32[12,64,256]{2,1,0:T(8,128)S(1)}, f32[48,256]{1,0:T(8,128)S(1)}, f32[48,256]{1,0:T(8,128)S(1)}, f32[136,256]{1,0:T(8,128)S(1)}) custom-call(f32[12,64,256]{2,1,0:T(8,128)S(1)} %copy-done.4, f32[12,64,256]{2,1,0:T(8,128)S(1)} %copy-done, f32[12,64,256]{2,1,0:T(8,128)S(1)} %copy-done.2, f32[12,64,256]{2,1,0:T(8,128)S(1)} %copy-done.5, ...), custom_call_target="tpu_custom_call" | custom-call | tf_op jit(solution)/shard_map/pallas_call | solution.py:395
  9.0 0.5 %collective-permute-start = (f32[48,256]{1,0:T(8,128)S(1)}, f32[48,256]{1,0:T(8,128)S(1)}, u32[]{:S(2)}, u32[]{:S(2)}) collective-permute-start(f32[48,256]{1,0:T(8,128)S(1)} %get-tuple-element.15), channel_id=1, source_target_pairs={{0,8},{8,0},{16,24},{24,16},{1,9},{9,1},{17,25},{25,17},{2,10},{10... | collective-permute-start | bytes 147464 | tf_op jit(solution)/shard_map/ppermute | solution.py:409
  9.5 0.7 %collective-permute-start.1 = (f32[48,256]{1,0:T(8,128)S(1)}, f32[48,256]{1,0:T(8,128)S(1)}, u32[]{:S(2)}, u32[]{:S(2)}) collective-permute-start(f32[48,256]{1,0:T(8,128)S(1)} %get-tuple-element.16), channel_id=1, source_target_pairs={{8,16},{16,8},{9,17},{17,9},{10,18},{18,10},{11,19},{19,11},{12,20... | collective-permute-start | bytes 147464 | tf_op jit(solution)/shard_map/ppermute | solution.py:410
  10.1 9.5 %all_gather.6.share_ref = f32[544,256]{1,0:T(8,128)S(1)} all-gather(f32[136,256]{1,0:T(8,128)S(1)} %get-tuple-element.17), channel_id=1, replica_groups=mesh['grp'=4,'loop'=8] {'grp'}, dimensions={0}, use_global_device_ids=true | all-gather | bytes 696320 | tf_op jit(solution)/shard_map/all_gather | solution.py:411
  19.6 0.0 copy-start.9
  19.6 0.0 collective-permute-done.ya_ref
  19.7 0.0 collective-permute-done.1.yb_ref
  19.7 0.7 %copy-done.9 = s32[1,256]{1,0:T(1,128)S(1)} copy-done((s32[1,256]{1,0:T(1,128)S(1)}, s32[1,256]{1,0:T(1,128)}, u32[]{:S(2)}) %copy-start.9) | copy-done | bytes 1048
  20.3 0.0 copy-start.1
  20.3 0.0 copy-start.3
  20.3 0.0 copy-start.6
  20.3 1.2 %shard_map.105 = (f32[12,64,256]{2,1,0:T(8,128)S(1)}, f32[96,256]{1,0:T(8,128)S(1)}, f32[8,768]{1,0:T(8,128)S(1)}, f32[8,768]{1,0:T(8,128)S(1)}, f32[128,256]{1,0:T(8,128)S(1)}, /*index=5*/f32[8,256]{1,0:T(8,128)S(1)}) custom-call(f32[12,64,256]{2,1,0:T(8,128)S(1)} %get-tuple-element.14.first_ref, f32[12,64,256]{2,1,0:T(8,128)S(1)} %copy-done.4, ...), custom_call_target="tpu_custom_call" | custom-call | tf_op jit(solution)/shard_map/pallas_call | solution.py:395
  21.6 2.2 %collective-permute-start.2 = (f32[8,768]{1,0:T(8,128)S(1)}, f32[8,768]{1,0:T(8,128)S(1)}, u32[]{:S(2)}, u32[]{:S(2)}) collective-permute-start(f32[8,768]{1,0:T(8,128)S(1)} %get-tuple-element.20.sa_ref), channel_id=1, source_target_pairs={{0,1},{1,0},{2,3},{3,2},{4,5},{5,4},{6,7},{7,6},{8,9},{9,8},{10,11... | collective-permute-start | bytes 73736 | tf_op jit(solution)/shard_map/ppermute | solution.py:421
  23.8 3.5 %collective-permute-start.3 = (f32[8,768]{1,0:T(8,128)S(1)}, f32[8,768]{1,0:T(8,128)S(1)}, u32[]{:S(2)}, u32[]{:S(2)}) collective-permute-start(f32[8,768]{1,0:T(8,128)S(1)} %get-tuple-element.21.sb_ref), channel_id=1, source_target_pairs={{1,2},{2,1},{3,4},{4,3},{5,6},{6,5},{7,0},{0,7},{9,10},{10,9},{11,... | collective-permute-start | bytes 73736 | tf_op jit(solution)/shard_map/ppermute | solution.py:422
  27.3 0.0 collective-permute-done.2.ra_ref
  27.4 3.0 %collective-permute-done.3.rb_ref = f32[8,768]{1,0:T(8,128)S(1)} collective-permute-done((f32[8,768]{1,0:T(8,128)S(1)}, f32[8,768]{1,0:T(8,128)S(1)}, u32[]{:S(2)}, u32[]{:S(2)}) %collective-permute-start.3) | collective-permute-done | bytes 24608 | tf_op jit(solution)/shard_map/ppermute | solution.py:422
  30.3 0.0 copy-start.10
  30.3 0.0 copy-done.1
  30.3 0.0 copy-done.3
  30.3 0.0 copy-done.6
  30.3 0.7 %copy-done.10 = s32[256]{0:T(256)S(1)} copy-done((s32[256]{0:T(256)S(1)}, s32[256]{0:T(256)}, u32[]{:S(2)}) %copy-start.10) | copy-done | bytes 1048
  31.0 2.9 %shard_map.106 = (f32[12,64,256]{2,1,0:T(8,128)}, f32[64,256]{1,0:T(8,128)S(1)}) custom-call(f32[12,64,256]{2,1,0:T(8,128)S(1)} %get-tuple-element.18.temp_ref, f32[12,64,256]{2,1,0:T(8,128)S(1)} %copy-done.1, f32[12,64,256]{2,1,0:T(8,128)S(1)} %copy-done.3, f32[12,64,256]{2,1,0:T(8,128)S(1)} %copy-done.6, f32[1,64,256]{2,1,0:T(8,128)S(1)} %slice.3.top_ref, ...), custom_call_target="tpu_custom_call" | custom-call | tf_op jit(solution)/shard_map/pallas_call | solution.py:395
  33.9 5.8 %all_gather.7.flow_ref = f32[256,256]{1,0:T(8,128)S(1)} all-gather(f32[64,256]{1,0:T(8,128)S(1)} %get-tuple-element.25), channel_id=1, replica_groups=mesh['grp'=4,'loop'=8] {'grp'}, dimensions={0}, use_global_device_ids=true | all-gather | bytes 327680 | tf_op jit(solution)/shard_map/all_gather | solution.py:429
  39.7 0.9 %shard_map.107 = f32[64,256]{1,0:T(8,128)} custom-call(f32[256,256]{1,0:T(8,128)S(1)} %all_gather.7.flow_ref, s32[1,256]{1,0:T(1,128)S(1)} %copy-done.9), custom_call_target="tpu_custom_call" | custom-call | tf_op jit(solution)/shard_map/pallas_call | solution.py:395
  (1 shorter events, 0.0 us)
Async XLA Ops:
  0.6 0.7 %copy-start.11 = (s32[64]{0:T(128)S(1)}, s32[64]{0:T(128)}, u32[]{:S(2)}) copy-start(s32[64]{0:T(128)} %param.16) | copy-start | bytes 772
  1.3 1.1 %copy-start = (f32[12,64,256]{2,1,0:T(8,128)S(1)}, f32[12,64,256]{2,1,0:T(8,128)}, u32[]{:S(2)}) copy-start(f32[12,64,256]{2,1,0:T(8,128)} %kappa_ref.5) | copy-start | bytes 2359300
  2.4 1.1 %copy-start.2 = (f32[12,64,256]{2,1,0:T(8,128)S(1)}, f32[12,64,256]{2,1,0:T(8,128)}, u32[]{:S(2)}) copy-start(f32[12,64,256]{2,1,0:T(8,128)} %slope_ref.5) | copy-start | bytes 2359300
  3.6 1.1 %copy-start.4 = (f32[12,64,256]{2,1,0:T(8,128)S(1)}, f32[12,64,256]{2,1,0:T(8,128)}, u32[]{:S(2)}) copy-start(f32[12,64,256]{2,1,0:T(8,128)} %temp_ref.3) | copy-start | bytes 2359300
  4.7 1.1 %copy-start.5 = (f32[12,64,256]{2,1,0:T(8,128)S(1)}, f32[12,64,256]{2,1,0:T(8,128)}, u32[]{:S(2)}) copy-start(f32[12,64,256]{2,1,0:T(8,128)} %power_ref.3) | copy-start | bytes 2359300
  5.8 0.8 %copy-start.7 = (f32[64,256]{1,0:T(8,128)S(1)}, f32[64,256]{1,0:T(8,128)}, u32[]{:S(2)}) copy-start(f32[64,256]{1,0:T(8,128)} %flow_ref.1) | copy-start | bytes 196612
  6.7 0.8 %copy-start.8 = (f32[64,256]{1,0:T(8,128)S(1)}, f32[64,256]{1,0:T(8,128)}, u32[]{:S(2)}) copy-start(f32[64,256]{1,0:T(8,128)} %wall_ref.1) | copy-start | bytes 196612
  9.0 10.7 %collective-permute-start = (f32[48,256]{1,0:T(8,128)S(1)}, f32[48,256]{1,0:T(8,128)S(1)}, u32[]{:S(2)}, u32[]{:S(2)}) collective-permute-start(f32[48,256]{1,0:T(8,128)S(1)} %get-tuple-element.15), channel_id=1, source_target_pairs={{0,8},{8,0},{16,24},{24,16},{1,9},{9,1},{17,25},{25,17},{2,10},{10... | collective-permute-start | bytes 147464 | tf_op jit(solution)/shard_map/ppermute | solution.py:409
  9.5 10.2 %collective-permute-start.1 = (f32[48,256]{1,0:T(8,128)S(1)}, f32[48,256]{1,0:T(8,128)S(1)}, u32[]{:S(2)}, u32[]{:S(2)}) collective-permute-start(f32[48,256]{1,0:T(8,128)S(1)} %get-tuple-element.16), channel_id=1, source_target_pairs={{8,16},{16,8},{9,17},{17,9},{10,18},{18,10},{11,19},{19,11},{12,20... | collective-permute-start | bytes 147464 | tf_op jit(solution)/shard_map/ppermute | solution.py:410
  19.6 0.7 %copy-start.9 = (s32[1,256]{1,0:T(1,128)S(1)}, s32[1,256]{1,0:T(1,128)}, u32[]{:S(2)}) copy-start(s32[1,256]{1,0:T(1,128)} %map_ref.5) | copy-start | bytes 3076
  20.3 10.0 %copy-start.1 = (f32[12,64,256]{2,1,0:T(8,128)S(1)}, f32[12,64,256]{2,1,0:T(8,128)}, u32[]{:S(2)}) copy-start(f32[12,64,256]{2,1,0:T(8,128)} %kappa_ref.5) | copy-start | bytes 2359300
  20.3 10.0 %copy-start.3 = (f32[12,64,256]{2,1,0:T(8,128)S(1)}, f32[12,64,256]{2,1,0:T(8,128)}, u32[]{:S(2)}) copy-start(f32[12,64,256]{2,1,0:T(8,128)} %slope_ref.5) | copy-start | bytes 2359300
  20.3 10.0 %copy-start.6 = (f32[12,64,256]{2,1,0:T(8,128)S(1)}, f32[12,64,256]{2,1,0:T(8,128)}, u32[]{:S(2)}) copy-start(f32[12,64,256]{2,1,0:T(8,128)} %power_ref.3) | copy-start | bytes 2359300
  21.6 5.8 %collective-permute-start.2 = (f32[8,768]{1,0:T(8,128)S(1)}, f32[8,768]{1,0:T(8,128)S(1)}, u32[]{:S(2)}, u32[]{:S(2)}) collective-permute-start(f32[8,768]{1,0:T(8,128)S(1)} %get-tuple-element.20.sa_ref), channel_id=1, source_target_pairs={{0,1},{1,0},{2,3},{3,2},{4,5},{5,4},{6,7},{7,6},{8,9},{9,8},{10,11... | collective-permute-start | bytes 73736 | tf_op jit(solution)/shard_map/ppermute | solution.py:421
  23.8 6.5 %collective-permute-start.3 = (f32[8,768]{1,0:T(8,128)S(1)}, f32[8,768]{1,0:T(8,128)S(1)}, u32[]{:S(2)}, u32[]{:S(2)}) collective-permute-start(f32[8,768]{1,0:T(8,128)S(1)} %get-tuple-element.21.sb_ref), channel_id=1, source_target_pairs={{1,2},{2,1},{3,4},{4,3},{5,6},{6,5},{7,0},{0,7},{9,10},{10,9},{11,... | collective-permute-start | bytes 73736 | tf_op jit(solution)/shard_map/ppermute | solution.py:422
  30.3 0.7 %copy-start.10 = (s32[256]{0:T(256)S(1)}, s32[256]{0:T(256)}, u32[]{:S(2)}) copy-start(s32[256]{0:T(256)} %param.17) | copy-start | bytes 3076

commit v2 on v1

--- a/solution.py
+++ b/solution.py
@@ -9,6 +9,7 @@
 courant = 0.5
 heat_gain = 0.5
 TILE = 128
+CHUNK = 2
 F32 = jnp.float32
 BF16 = jnp.bfloat16
 
@@ -47,14 +48,17 @@
     return 0.5 * (cond_a + cond_b) * (temp_b - temp_a)
 
 
-def closed_heat(temp_ref, kappa_ref, slope_ref, emit):
+def closed_heat(temp_ref, kappa_ref, slope_ref, emit, ready=lambda z: None):
     layers, rows, cols = temp_ref.shape
     lane = lax.broadcasted_iota(jnp.int32, (rows, cols), 1)
     row = lax.broadcasted_iota(jnp.int32, (rows, cols), 0)
+    ready(0)
     temp = temp_ref[0]
     cond = kappa_ref[0] * (1.0 + slope_ref[0] * temp)
     flux_below = None
     for z in range(layers):
+        if z + 1 < layers:
+            ready(z + 1)
         flux_x = face(cond, pltpu.roll(cond, cols - 1, 1), temp, pltpu.roll(temp, cols - 1, 1))
         flux_x = jnp.where(lane == cols - 1, 0.0, flux_x)
         heat = flux_x - pltpu.roll(flux_x, 1, 1)
@@ -74,17 +78,51 @@
 
 
 def open_kernel(
-    temp_ref, kappa_ref, slope_ref, power_ref, flow_ref, wall_ref, dir_ref,
-    next_ref, ya_ref, yb_ref, share_ref, tmp_ref, row_ref,
+    temp_hbm, kappa_hbm, slope_hbm, power_hbm, flow_hbm, wall_hbm, dir_hbm, map_hbm, link_hbm,
+    next_ref, temp_ref, kappa_ref, slope_ref, power_ref, ya_ref, yb_ref, share_ref, map_ref, link_ref,
+    tmp_ref, row_ref, dir_ref, block_sem, small_sem,
 ):
     layers, rows, cols = temp_ref.shape
     group = lax.axis_index("grp")
     even = lax.rem(group, 2) == 0
+    blocks = []
+    for z in range(0, layers, CHUNK):
+        part = pl.ds(z, CHUNK)
+        blocks.append([
+            pltpu.make_async_copy(source.at[part], target.at[part], block_sem.at[n, z // CHUNK])
+            for n, (source, target) in enumerate((
+                (temp_hbm, temp_ref), (kappa_hbm, kappa_ref), (slope_hbm, slope_ref), (power_hbm, power_ref),
+            ))
+        ])
+    smalls = [
+        pltpu.make_async_copy(source, target, small_sem.at[n])
+        for n, (source, target) in enumerate((
+            (flow_hbm, share_ref.at[0:rows]), (wall_hbm, share_ref.at[rows : 2 * rows]),
+            (dir_hbm, dir_ref), (map_hbm, map_ref), (link_hbm, link_ref),
+        ))
+    ]
+    for block in blocks:
+        for copy in block:
+            copy.start()
+    for copy in smalls:
+        copy.start()
+
+    def ready(z):
+        if z % CHUNK == 0:
+            for copy in blocks[z // CHUNK]:
+                copy.wait()
 
     def emit(z, temp, cond, heat):
         next_ref[z] = temp + time_step * (heat + power_ref[z])
-
-    closed_heat(temp_ref, kappa_ref, slope_ref, emit)
+        if z == 0:
+            lane = lax.broadcasted_iota(jnp.int32, (rows, TILE), 1)
+            packed = jnp.where(lane == 0, temp[:, 0:TILE], pltpu.roll(temp[:, cols - TILE :], 2, 1))
+            packed = jnp.where(lane == 3, pltpu.roll(cond[:, 0:TILE], 3, 1), packed)
+            packed = jnp.where(lane == 4, pltpu.roll(cond[:, cols - TILE :], 5, 1), packed)
+            tmp_ref[...] = jnp.zeros_like(tmp_ref)
+            tmp_ref[0:rows, :] = packed
+
+    closed_heat(temp_ref, kappa_ref, slope_ref, emit, ready)
     for q, ref in enumerate((next_ref, temp_ref, kappa_ref, slope_ref)):
         for z in range(layers):
             first = ref[z, 0:1, :]
@@ -92,23 +130,17 @@
             at = q * layers + z
             ya_ref[at : at + 1, :] = jnp.where(even, last, first)
             yb_ref[at : at + 1, :] = jnp.where(even, first, last)
-    share_ref[0:rows, :] = flow_ref[...]
-    share_ref[rows : 2 * rows, :] = wall_ref[...]
-    lane = lax.broadcasted_iota(jnp.int32, (rows, TILE), 1)
-    left = temp_ref[0, :, 0:TILE]
-    right = temp_ref[0, :, cols - TILE : cols]
-    tmp_ref[...] = jnp.zeros_like(tmp_ref)
-    tmp_ref[0:rows, :] = jnp.where(lane == 0, left, pltpu.roll(right, 2, 1))
-    turned = tmp_ref[...].T
+    for copy in smalls:
+        copy.wait()
     row_ref[...] = jnp.zeros_like(row_ref)
-    row_ref[0:8, 0:TILE] = turned[0:8, :]
+    row_ref[0:8, 0:TILE] = tmp_ref[...].T[0:8, :]
     row_ref[2:3, 0:rows] = dir_ref[...].astype(F32)
     share_ref[2 * rows :, :] = pltpu.roll(row_ref[...], group * rows, 1)
 
 
 def edge_kernel(
     first_ref, temp_ref, kappa_ref, slope_ref, ya_ref, yb_ref, share_ref, map_ref,
-    next_ref, yo_ref, sa_ref, sb_ref, fw_ref, crow_ref, strip_ref, small_ref,
+    next_ref, yo_ref, sa_ref, sb_ref, fw_ref, crow_ref, flow_ref, strip_ref, small_ref,
 ):
     layers, rows, cols = temp_ref.shape
     span = 2 * rows + 8
@@ -133,9 +165,8 @@
     chooser = one_hot(map_ref[...], group * rows - 8, rows + 16)
     both = pick(chooser, jnp.concatenate([flow_all, wall_all], 1), ((1,), (0,)))
     flow_y, wall_y = both[:, :cols], both[:, cols:]
-    fw_ref[0:rows, :] = flow_y[8 : 8 + rows]
-    fw_ref[rows:, :] = wall_y[8 : 8 + rows]
-    sink = wall_y[8 : 8 + rows] * (temp_ref[0] - flow_y[8 : 8 + rows])
+    flow, wall = flow_y[8 : 8 + rows], wall_y[8 : 8 + rows]
+    sink = wall * (temp_ref[0] - flow)
     temp_low, temp_high = yo_ref[layers : layers + 1, :], yo_ref[5 * layers : 5 * layers + 1, :]
     sink_low = wall_y[7:8] * (temp_low - flow_y[7:8])
     sink_high = wall_y[8 + rows : 9 + rows] * (temp_high - flow_y[8 + rows : 9 + rows])
@@ -190,6 +221,21 @@
             packed = left if packed is None else jnp.where(lane == n, left, packed)
             packed = jnp.where(lane == n + 4, right, packed)
         strip_ref[z * rows : (z + 1) * rows, :] = packed
+    toward_y = pick(chooser[8 : 8 + rows], jnp.broadcast_to(extra[2:3], (TILE, groups * rows)), ((1,), (1,)))
+    toward_y = jnp.concatenate([toward_y] * (cols // TILE), 1) > 0.5
+    lane_w = lax.broadcasted_iota(jnp.int32, (rows, cols), 1)
+
+    def upstream(values):
+        before = jnp.where(lane_w == 0, 0.0, pltpu.roll(values, 1, 1))
+        after = jnp.where(lane_w == cols - 1, 0.0, pltpu.roll(values, cols - 1, 1))
+        return jnp.where(toward_y, before, after)
+
+    flow = flow - courant * (flow - upstream(flow)) + heat_gain * sink
+    fw_ref[0:rows, :] = flow
+    fw_ref[rows:, :] = wall
+    flux = wall * (next_ref[0] - flow)
+    flow_ref[...] = flow - courant * (flow - upstream(flow)) + heat_gain * flux
+
     strips = strip_ref[...].T[0:8, :]
     corners = small_ref[...].T[0:8, :]
 
@@ -212,20 +258,23 @@
     crow_ref[0:1, :] = toward
     crow_ref[1:2, :] = flow_0
     crow_ref[2:3, :] = flow_e
-    width = sa_ref.shape[1]
+    crow_ref[3:4, :] = wall_0
+    crow_ref[4:5, :] = wall_e
     channels = groups * rows
     for ref, pick_right in ((sa_ref, place_even), (sb_ref, jnp.logical_not(place_even))):
         ref[...] = jnp.zeros_like(ref)
         ref[0:4, :] = jnp.where(pick_right, strips[4:8], strips[0:4])
         ref[4:6, 0:TILE] = jnp.where(pick_right, corners[4:6], corners[0:2])
+        ref[4:5, channels : 2 * channels] = jnp.where(pick_right, extra[1:2], extra[0:1])
+        ref[5:6, channels : 2 * channels] = jnp.where(pick_right, extra[4:5], extra[3:4])
         ref[6:7, 0:channels] = jnp.where(pick_right, flow_e, flow_0)
         ref[7:8, 0:channels] = jnp.where(pick_right, part_e, part_0)
 
 
 def close_kernel(
-    temp_ref, kappa_ref, slope_ref, power_ref, top_ref, yo_ref, ra_ref, rb_ref, sa_ref, sb_ref,
-    fw_ref, crow_ref, map_ref, link_ref,
-    out_ref, flow_ref, wide_ref, xt_ref, xc_ref, xf_ref, full_ref,
+    temp_ref, kappa_ref, slope_ref, power_ref, yo_ref, ra_ref, rb_ref, sa_ref, sb_ref,
+    fw_ref, crow_ref, map_ref, link_ref, all_ref,
+    out_hbm, flow_hbm, wide_ref, xt_ref, xc_ref, xf_ref, full_ref, out_ref, flow_ref, sel_ref, turn_ref, out_sem,
 ):
     layers, rows, cols = temp_ref.shape
     group, groups = lax.axis_index("grp"), lax.axis_size("grp")
@@ -312,26 +361,47 @@
         (jnp.where(first_place, moved[0:1], stack[0:1]), jnp.where(last_place, moved[1:2], stack[1:2])),
         (jnp.where(first_place, late_moved[0:1], late_l), jnp.where(last_place, late_moved[1:2], late_r)),
     )
+    shift_0 = courant * toward_c * edge_rows[0][0]
+    shift_e = courant * (1.0 - toward_c) * edge_rows[0][1]
+    tops = [
+        time_step * face(
+            own[side][5:6, channels : 2 * channels], got[side][5:6, channels : 2 * channels],
+            own[side][4:5, channels : 2 * channels], got[side][4:5, channels : 2 * channels],
+        )
+        for side in range(2)
+    ]
+    every = one_hot(map_ref[...], 0, channels)
+    tops = pick_rows(jnp.concatenate(tops + [crow_ref[2:8, :]], 0), every)
+    wall_0, wall_e = crow_ref[3:4, :], crow_ref[4:5, :]
+    add_0 = (
+        courant * toward_c * edge_rows[1][0]
+        + ((1.0 - courant) - heat_gain * wall_0) * shift_0
+        + heat_gain * wall_0 * tops[0:1]
+    )
+    add_e = (
+        courant * (1.0 - toward_c) * edge_rows[1][1]
+        + ((1.0 - courant) - heat_gain * wall_e) * shift_e
+        + heat_gain * wall_e * tops[1:2]
+    )
+    wide_row = lax.broadcasted_iota(jnp.int32, (TILE, channels), 0)
     chooser = one_hot(map_ref[...], group * rows, rows)
-    wide_row = lax.broadcasted_iota(jnp.int32, (TILE, channels), 0)
-    edge_y = [
-        pick(chooser, jnp.where(wide_row == 0, pair[0], pair[1]), ((1,), (1,))) for pair in edge_rows
-    ]
-    toward = pick(chooser, jnp.broadcast_to(toward_c, (TILE, channels)), ((1,), (1,)))
-    toward = jnp.concatenate([toward] * (cols // TILE), 1) > 0.5
-    lane_w = lax.broadcasted_iota(jnp.int32, (rows, cols), 1)
-
-    def upstream(flow, edge):
-        edges = jnp.concatenate([edge] * (cols // TILE), 1)
-        before = jnp.where(lane_w == 0, edges, pltpu.roll(flow, 1, 1))
-        after = jnp.where(lane_w == cols - 1, edges, pltpu.roll(flow, cols - 1, 1))
-        return jnp.where(toward, before, after)
-
-    flow, wall = fw_ref[0:rows, :], fw_ref[rows:, :]
-    flux = wall * (top_ref[0] - flow)
-    flow = flow - courant * (flow - upstream(flow, edge_y[0])) + heat_gain * flux
-    flux = wall * (full_ref[0] - flow)
-    flow_ref[...] = flow - courant * (flow - upstream(flow, edge_y[1])) + heat_gain * flux
+    edge_y = pick(chooser, jnp.where(wide_row == 0, shift_0, shift_e), ((1,), (1,)))
+    adds = jnp.where(wide_row == 0, add_0, jnp.where(wide_row == 1, courant * toward_c * shift_0, add_e))
+    adds = jnp.where(wide_row == TILE - 2, courant * (1.0 - toward_c) * shift_e, adds)
+    turn_ref[...] = adds.T
+    sel_ref[...] = pick(every, all_ref[...], ((0,), (0,)))
+    mine = pl.ds(pl.multiple_of(group * rows, 8), rows)
+    adds, flow = turn_ref[mine, :], sel_ref[mine, :]
+    pad = [jnp.zeros((rows, cols - 2 * TILE), F32)] if cols > 2 * TILE else []
+    flow_ref[...] = flow + jnp.concatenate(
+        [jnp.where(lane < 2, adds, 0.0)] + pad + [jnp.where(lane >= TILE - 2, adds, 0.0)], 1
+    )
+    flow_copy = pltpu.make_async_copy(flow_ref, flow_hbm, out_sem.at[layers])
+    flow_copy.start()
+    flow = fw_ref[0:rows, :] + jnp.concatenate(
+        [jnp.where(lane == 0, edge_y, 0.0)] + pad + [jnp.where(lane == TILE - 1, edge_y, 0.0)], 1
+    )
+    flux = fw_ref[rows:, :] * (full_ref[0] - flow)
 
     row8 = lax.broadcasted_iota(jnp.int32, (8, cols), 0)
 
@@ -356,15 +426,13 @@
             )
             out_ref[z, part, :] = result[part] + jnp.where(row8 == at, extra, 0.0)
 
+        copies.append(pltpu.make_async_copy(out_ref.at[z], out_hbm.at[z], out_sem.at[z]))
+        copies[-1].start()
+
+    copies = [flow_copy]
     closed_heat(full_ref, kappa_ref, slope_ref, emit)
-
-
-def return_kernel(flow_ref, map_ref, out_ref, tmp_ref):
-    rows = out_ref.shape[0]
-    group = lax.axis_index("grp")
-    chooser = one_hot(map_ref[...], 0, flow_ref.shape[0])
-    tmp_ref[...] = pick(chooser, flow_ref[...], ((0,), (0,)))
-    out_ref[...] = tmp_ref[pl.ds(pl.multiple_of(group * rows, 8), rows), :]
+    for copy in copies:
+        copy.wait()
 
 
 def pairs(count, first, closed):
@@ -391,44 +459,59 @@
     def shape(*dims):
         return jax.ShapeDtypeStruct(dims, F32)
 
-    def call(body, outs, scratch, *args):
+    def call(body, outs, scratch, *args, ins=None, places=None):
         return pl.pallas_call(
             body,
             out_shape=outs,
-            scratch_shapes=[pltpu.VMEM(dims, F32) for dims in scratch],
+            in_specs=[pl.BlockSpec(memory_space=ins or pltpu.VMEM)] * len(args),
+            out_specs=[pl.BlockSpec(memory_space=places or pltpu.VMEM)] * len(outs),
+            scratch_shapes=scratch,
             compiler_params=params,
-        )(*args)
-
-    link = loop_link.reshape(1, channels)
-    first, ya, yb, share = call(
+        )(*[pltpu.with_memory_space_constraint(a, ins) if ins else a for a in args])
+
+    def vmem(*dims):
+        return pltpu.VMEM(dims, F32)
+
+    block = shape(layers, rows, cols)
+    halo = shape(4 * layers, cols)
+    index = jax.ShapeDtypeStruct((1, channels), jnp.int32)
+    first, temp, kappa, slope, power, ya, yb, share, map_row, link_row = call(
         open_kernel,
-        (shape(layers, rows, cols), shape(4 * layers, cols), shape(4 * layers, cols), shape(2 * rows + 8, cols)),
-        [(TILE, TILE), (8, cols)],
+        (block, block, block, block, block, halo, halo, shape(2 * rows + 8, cols), index, index),
+        [
+            vmem(TILE, TILE), vmem(8, cols), pltpu.VMEM((1, rows), jnp.int32),
+            pltpu.SemaphoreType.DMA((4, layers // CHUNK)), pltpu.SemaphoreType.DMA((5,)),
+        ],
         solid_temp, kappa, slope, power, coolant_temp, wall_coeff, flow_dir.reshape(1, rows),
+        channel_map, loop_link.reshape(1, channels),
+        ins=pltpu.HBM,
     )
     ya = lax.ppermute(ya, "grp", pairs(groups, 0, False))
     yb = lax.ppermute(yb, "grp", pairs(groups, 1, False))
     share = lax.all_gather(share, "grp", axis=0, tiled=True)
-    after, yo, sa, sb, fw, crow = call(
+    after, yo, sa, sb, fw, crow, flow = call(
         edge_kernel,
         (
-            shape(layers, rows, cols), shape(8 * layers, cols), shape(8, strip), shape(8, strip),
-            shape(2 * rows, cols), shape(8, channels),
+            block, shape(8 * layers, cols), shape(8, strip), shape(8, strip),
+            shape(2 * rows, cols), shape(8, channels), shape(rows, cols),
         ),
-        [(strip, TILE), (TILE, TILE)],
-        first, solid_temp, kappa, slope, ya, yb, share, channel_map,
+        [vmem(strip, TILE), vmem(TILE, TILE)],
+        first, temp, kappa, slope, ya, yb, share, map_row,
     )
     ra = lax.ppermute(sa, "loop", pairs(places, 0, True))
     rb = lax.ppermute(sb, "loop", pairs(places, 1, True))
-    temp, flow = call(
+    flow = lax.all_gather(flow, "grp", axis=0, tiled=True)
+    return call(
         close_kernel,
-        (shape(layers, rows, cols), shape(rows, cols)),
-        [(TILE, strip), (strip, TILE), (strip, TILE), (strip, TILE), (layers, rows, cols)],
-        after, kappa, slope, power, solid_temp[0:1], yo, ra, rb, sa, sb, fw, crow, channel_map, link,
-    )
-    flow = lax.all_gather(flow, "grp", axis=0, tiled=True)
-    flow = call(return_kernel, shape(rows, cols), [(channels, cols)], flow, channel_map)
-    return (temp, flow)
+        (block, shape(rows, cols)),
+        [
+            vmem(TILE, strip), vmem(strip, TILE), vmem(strip, TILE), vmem(strip, TILE),
+            vmem(layers, rows, cols), vmem(layers, rows, cols), vmem(rows, cols),
+            vmem(channels, cols), vmem(channels, TILE), pltpu.SemaphoreType.DMA((layers + 1,)),
+        ],
+        after, kappa, slope, power, yo, ra, rb, sa, sb, fw, crow, map_row, link_row, flow,
+        places=pltpu.HBM,
+    )
 
 
 def solution(mesh):

time: 41.1 us -> 30.3 us (0.74)
  local copies, waits for them, and re-layouts: 8.21 us -> 0 us
  waiting for transfers between devices: 2.97 us -> 0.01 us
  Pallas kernels: 6.56 us -> 7.29 us
    unnamed x24 -> x0, local copies, waits for them, and re-layouts: 8.21 us -> none
    ppermute x1, waiting for transfers between devices: 2.97 us -> 0.01 us  [shards(): rb = lax.ppermute(sb, 'loop', pairs(places, 1, True))]
    pallas_call x4 -> x3, Pallas kernels: 6.56 us -> 7.29 us  [call(): pl.pallas_call(body, out_shape=outs, in_specs=[pl.BlockSpec(memory_space=...]
  transfers between devices with their start and end apart: 4 -> 4, of which waited for: 1 -> 0; matrix products, arithmetic and copies ran while one was open for 0% -> 0% of each run, Pallas kernels for 0% -> 0%
where the time goes in v2:
time: 30.3 us; the launch traced here: 30.2 us
  blocking collectives  15.3 us (50%)
  Pallas kernels  7.29 us (24%)
  starting transfers between devices  6.92 us (23%)
  between operations  0.66 us (2%)
    all_gather x1, blocking collectives, shards(): share = lax.all_gather(share, 'grp', axis=0, tiled=True)  9.5 us
    pallas_call x3, Pallas kernels, call(): pl.pallas_call(body, out_shape=outs, in_specs=[pl.BlockSpec(memory_space=...  7.29 us
    all_gather x1, blocking collectives, shards(): flow = lax.all_gather(flow, 'grp', axis=0, tiled=True)  5.77 us
    ppermute x1, starting transfers between devices, shards(): rb = lax.ppermute(sb, 'loop', pairs(places, 1, True))  3.55 us
    ppermute x1, starting transfers between devices, shards(): ra = lax.ppermute(sa, 'loop', pairs(places, 0, True))  2.21 us
    ppermute x1, starting transfers between devices, shards(): yb = lax.ppermute(yb, 'grp', pairs(groups, 1, False))  0.65 us
  transfers between devices with their start and end apart: 4, of which 0 were waited for; matrix products, arithmetic and copies ran while one was open for 0% of the time, Pallas kernels for 0%

profile of v2, /device:TPU:0, one launch (start us, length us, event | category | flops | bytes accessed | tf_op | source)
XLA Modules:
  0.0 30.2 jit_solution(14022456824956166793)
XLA Ops:
  0.6 3.1 %shard_map.104 = (f32[12,64,256]{2,1,0:T(8,128)S(1)}, f32[12,64,256]{2,1,0:T(8,128)S(1)}, f32[12,64,256]{2,1,0:T(8,128)S(1)}, f32[12,64,256]{2,1,0:T(8,128)S(1)}...) custom-call(f32[12,64,256]{2,1,0:T(8,128)} %temp_hbm.1, ...), custom_call_target="tpu_custom_call" | custom-call | tf_op jit(solution)/shard_map/pallas_call | solution.py:463
  3.8 0.5 %collective-permute-start = (f32[48,256]{1,0:T(8,128)S(1)}, f32[48,256]{1,0:T(8,128)S(1)}, u32[]{:S(2)}, u32[]{:S(2)}) collective-permute-start(f32[48,256]{1,0:T(8,128)S(1)} %get-tuple-element.23), channel_id=1, source_target_pairs={{0,8},{8,0},{16,24},{24,16},{1,9},{9,1},{17,25},{25,17},{2,10},{10... | collective-permute-start | bytes 147464 | tf_op jit(solution)/shard_map/ppermute | solution.py:489
  4.3 0.7 %collective-permute-start.1 = (f32[48,256]{1,0:T(8,128)S(1)}, f32[48,256]{1,0:T(8,128)S(1)}, u32[]{:S(2)}, u32[]{:S(2)}) collective-permute-start(f32[48,256]{1,0:T(8,128)S(1)} %get-tuple-element.24), channel_id=1, source_target_pairs={{8,16},{16,8},{9,17},{17,9},{10,18},{18,10},{11,19},{19,11},{12,20... | collective-permute-start | bytes 147464 | tf_op jit(solution)/shard_map/ppermute | solution.py:490
  4.9 9.5 %all_gather.6.share_ref = f32[544,256]{1,0:T(8,128)S(1)} all-gather(f32[136,256]{1,0:T(8,128)S(1)} %get-tuple-element.25), channel_id=1, replica_groups=mesh['grp'=4,'loop'=8] {'grp'}, dimensions={0}, use_global_device_ids=true | all-gather | bytes 696320 | tf_op jit(solution)/shard_map/all_gather | solution.py:491
  14.4 0.0 collective-permute-done.ya_ref
  14.4 0.0 collective-permute-done.1.yb_ref
  14.4 1.4 %shard_map.105 = (f32[12,64,256]{2,1,0:T(8,128)S(1)}, f32[96,256]{1,0:T(8,128)S(1)}, f32[8,768]{1,0:T(8,128)S(1)}, f32[8,768]{1,0:T(8,128)S(1)}, f32[128,256]{1,...) custom-call(f32[12,64,256]{2,1,0:T(8,128)S(1)} %get-tuple-element.19.first_ref, ...), custom_call_target="tpu_custom_call" | custom-call | tf_op jit(solution)/shard_map/pallas_call | solution.py:463
  15.9 2.2 %collective-permute-start.2 = (f32[8,768]{1,0:T(8,128)S(1)}, f32[8,768]{1,0:T(8,128)S(1)}, u32[]{:S(2)}, u32[]{:S(2)}) collective-permute-start(f32[8,768]{1,0:T(8,128)S(1)} %get-tuple-element.30.sa_ref), channel_id=1, source_target_pairs={{0,1},{1,0},{2,3},{3,2},{4,5},{5,4},{6,7},{7,6},{8,9},{9,8},{10,11... | collective-permute-start | bytes 73736 | tf_op jit(solution)/shard_map/ppermute | solution.py:501
  18.1 3.5 %collective-permute-start.3 = (f32[8,768]{1,0:T(8,128)S(1)}, f32[8,768]{1,0:T(8,128)S(1)}, u32[]{:S(2)}, u32[]{:S(2)}) collective-permute-start(f32[8,768]{1,0:T(8,128)S(1)} %get-tuple-element.31.sb_ref), channel_id=1, source_target_pairs={{1,2},{2,1},{3,4},{4,3},{5,6},{6,5},{7,0},{0,7},{9,10},{10,9},{11,... | collective-permute-start | bytes 73736 | tf_op jit(solution)/shard_map/ppermute | solution.py:502
  21.6 5.8 %all_gather.7.all_ref = f32[256,256]{1,0:T(8,128)S(1)} all-gather(f32[64,256]{1,0:T(8,128)S(1)} %get-tuple-element.35), channel_id=1, replica_groups=mesh['grp'=4,'loop'=8] {'grp'}, dimensions={0}, use_global_device_ids=true | all-gather | bytes 327680 | tf_op jit(solution)/shard_map/all_gather | solution.py:503
  27.4 0.0 collective-permute-done.2.ra_ref
  27.4 0.0 collective-permute-done.3.rb_ref
  27.4 2.7 %shard_map.106 = (f32[12,64,256]{2,1,0:T(8,128)}, f32[64,256]{1,0:T(8,128)}) custom-call(f32[12,64,256]{2,1,0:T(8,128)S(1)} %get-tuple-element.27.temp_ref, f32[12,64,256]{2,1,0:T(8,128)S(1)} %get-tuple-element.21.kappa_ref, f32[12,64,256]{2,1,0:T(8,128)S(1)} %get-tuple-element.22.slope_ref, f32[12,64,256]{2,1,0:T(8,128)S(1)} %get-tuple-element.28.power_ref, ...), custom_call_target="tpu_custom_call" | custom-call | tf_op jit(solution)/shard_map/pallas_call | solution.py:463
Async XLA Ops:
  3.8 10.7 %collective-permute-start = (f32[48,256]{1,0:T(8,128)S(1)}, f32[48,256]{1,0:T(8,128)S(1)}, u32[]{:S(2)}, u32[]{:S(2)}) collective-permute-start(f32[48,256]{1,0:T(8,128)S(1)} %get-tuple-element.23), channel_id=1, source_target_pairs={{0,8},{8,0},{16,24},{24,16},{1,9},{9,1},{17,25},{25,17},{2,10},{10... | collective-permute-start | bytes 147464 | tf_op jit(solution)/shard_map/ppermute | solution.py:489
  4.3 10.2 %collective-permute-start.1 = (f32[48,256]{1,0:T(8,128)S(1)}, f32[48,256]{1,0:T(8,128)S(1)}, u32[]{:S(2)}, u32[]{:S(2)}) collective-permute-start(f32[48,256]{1,0:T(8,128)S(1)} %get-tuple-element.24), channel_id=1, source_target_pairs={{8,16},{16,8},{9,17},{17,9},{10,18},{18,10},{11,19},{19,11},{12,20... | collective-permute-start | bytes 147464 | tf_op jit(solution)/shard_map/ppermute | solution.py:490
  15.9 11.5 %collective-permute-start.2 = (f32[8,768]{1,0:T(8,128)S(1)}, f32[8,768]{1,0:T(8,128)S(1)}, u32[]{:S(2)}, u32[]{:S(2)}) collective-permute-start(f32[8,768]{1,0:T(8,128)S(1)} %get-tuple-element.30.sa_ref), channel_id=1, source_target_pairs={{0,1},{1,0},{2,3},{3,2},{4,5},{5,4},{6,7},{7,6},{8,9},{9,8},{10,11... | collective-permute-start | bytes 73736 | tf_op jit(solution)/shard_map/ppermute | solution.py:501
  18.1 9.3 %collective-permute-start.3 = (f32[8,768]{1,0:T(8,128)S(1)}, f32[8,768]{1,0:T(8,128)S(1)}, u32[]{:S(2)}, u32[]{:S(2)}) collective-permute-start(f32[8,768]{1,0:T(8,128)S(1)} %get-tuple-element.31.sb_ref), channel_id=1, source_target_pairs={{1,2},{2,1},{3,4},{4,3},{5,6},{6,5},{7,0},{0,7},{9,10},{10,9},{11,... | collective-permute-start | bytes 73736 | tf_op jit(solution)/shard_map/ppermute | solution.py:502

commit v3 on v2

--- a/solution.py
+++ b/solution.py
@@ -9,7 +9,7 @@
 courant = 0.5
 heat_gain = 0.5
 TILE = 128
-CHUNK = 2
+CHUNK = 4
 F32 = jnp.float32
 BF16 = jnp.bfloat16
 
@@ -77,14 +77,73 @@
             temp, cond = temp_up, cond_up
 
 
-def open_kernel(
+def pack_kernel(
     temp_hbm, kappa_hbm, slope_hbm, power_hbm, flow_hbm, wall_hbm, dir_hbm, map_hbm, link_hbm,
-    next_ref, temp_ref, kappa_ref, slope_ref, power_ref, ya_ref, yb_ref, share_ref, map_ref, link_ref,
-    tmp_ref, row_ref, dir_ref, block_sem, small_sem,
+    core_ref, cross_ref, map_ref, link_ref,
+    temp_ref, kappa_ref, slope_ref, power_ref, top_ref, tmp_ref, row_ref, dir_ref,
+    block_sem, top_sem, share_sem, small_sem,
 ):
-    layers, rows, cols = temp_ref.shape
+    layers, rows, cols = temp_hbm.shape
+    share = 2 * rows + 8
     group = lax.axis_index("grp")
     even = lax.rem(group, 2) == 0
+    copies = []
+    for n, (source, target) in enumerate((
+        (temp_hbm, temp_ref), (kappa_hbm, kappa_ref), (slope_hbm, slope_ref), (power_hbm, power_ref),
+    )):
+        copies.append(pltpu.make_async_copy(source.at[:, 0:8], target.at[:, 0:8], block_sem.at[n, 0]))
+        copies.append(
+            pltpu.make_async_copy(source.at[:, rows - 8 : rows], target.at[:, 8:16], block_sem.at[n, 1])
+        )
+    tops = [
+        pltpu.make_async_copy(source.at[0], top_ref.at[n], top_sem.at[n])
+        for n, source in enumerate((temp_hbm, kappa_hbm, slope_hbm))
+    ]
+    smalls = [
+        pltpu.make_async_copy(source, target, small_sem.at[n])
+        for n, (source, target) in enumerate(((dir_hbm, dir_ref), (map_hbm, map_ref), (link_hbm, link_ref)))
+    ]
+    for m, target in enumerate((core_ref, cross_ref)):
+        smalls.append(pltpu.make_async_copy(flow_hbm, target.at[0:rows], share_sem.at[m, 0]))
+        smalls.append(pltpu.make_async_copy(wall_hbm, target.at[rows : 2 * rows], share_sem.at[m, 1]))
+    for copy in copies + tops + smalls:
+        copy.start()
+    tmp_ref[...] = jnp.zeros_like(tmp_ref)
+    row_ref[...] = jnp.zeros_like(row_ref)
+    for copy in copies:
+        copy.wait()
+
+    def emit(z, temp, cond, heat):
+        after = temp + time_step * (heat + power_ref[z])
+        for q, value in enumerate((after, temp, kappa_ref[z], slope_ref[z])):
+            at = share + q * layers + z
+            core_ref[at : at + 1, :] = jnp.where(even, value[15:16], value[0:1])
+            cross_ref[at : at + 1, :] = jnp.where(even, value[0:1], value[15:16])
+
+    closed_heat(temp_ref, kappa_ref, slope_ref, emit)
+    for copy in tops:
+        copy.wait()
+    temp = top_ref[0]
+    cond = top_ref[1] * (1.0 + top_ref[2] * temp)
+    lane = lax.broadcasted_iota(jnp.int32, (rows, TILE), 1)
+    packed = jnp.where(lane == 0, temp[:, 0:TILE], pltpu.roll(temp[:, cols - TILE :], 2, 1))
+    packed = jnp.where(lane == 3, pltpu.roll(cond[:, 0:TILE], 3, 1), packed)
+    packed = jnp.where(lane == 4, pltpu.roll(cond[:, cols - TILE :], 5, 1), packed)
+    tmp_ref[0:rows, :] = packed
+    row_ref[0:8, 0:TILE] = tmp_ref[...].T[0:8, :]
+    for copy in smalls:
+        copy.wait()
+    row_ref[2:3, 0:rows] = dir_ref[...].astype(F32)
+    extra = pltpu.roll(row_ref[...], group * rows, 1)
+    core_ref[2 * rows : share, :] = extra
+    cross_ref[2 * rows : share, :] = extra
+
+
+def open_kernel(
+    temp_hbm, kappa_hbm, slope_hbm, power_hbm, after_ref,
+    next_ref, temp_ref, kappa_ref, slope_ref, power_ref, block_sem,
+):
+    layers = temp_ref.shape[0]
     blocks = []
     for z in range(0, layers, CHUNK):
         part = pl.ds(z, CHUNK)
@@ -94,18 +153,9 @@
                 (temp_hbm, temp_ref), (kappa_hbm, kappa_ref), (slope_hbm, slope_ref), (power_hbm, power_ref),
             ))
         ])
-    smalls = [
-        pltpu.make_async_copy(source, target, small_sem.at[n])
-        for n, (source, target) in enumerate((
-            (flow_hbm, share_ref.at[0:rows]), (wall_hbm, share_ref.at[rows : 2 * rows]),
-            (dir_hbm, dir_ref), (map_hbm, map_ref), (link_hbm, link_ref),
-        ))
-    ]
     for block in blocks:
         for copy in block:
             copy.start()
-    for copy in smalls:
-        copy.start()
 
     def ready(z):
         if z % CHUNK == 0:
@@ -114,56 +164,39 @@
 
     def emit(z, temp, cond, heat):
         next_ref[z] = temp + time_step * (heat + power_ref[z])
-        if z == 0:
-            lane = lax.broadcasted_iota(jnp.int32, (rows, TILE), 1)
-            packed = jnp.where(lane == 0, temp[:, 0:TILE], pltpu.roll(temp[:, cols - TILE :], 2, 1))
-            packed = jnp.where(lane == 3, pltpu.roll(cond[:, 0:TILE], 3, 1), packed)
-            packed = jnp.where(lane == 4, pltpu.roll(cond[:, cols - TILE :], 5, 1), packed)
-            tmp_ref[...] = jnp.zeros_like(tmp_ref)
-            tmp_ref[0:rows, :] = packed
 
     closed_heat(temp_ref, kappa_ref, slope_ref, emit, ready)
-    for q, ref in enumerate((next_ref, temp_ref, kappa_ref, slope_ref)):
-        for z in range(layers):
-            first = ref[z, 0:1, :]
-            last = ref[z, rows - 1 : rows, :]
-            at = q * layers + z
-            ya_ref[at : at + 1, :] = jnp.where(even, last, first)
-            yb_ref[at : at + 1, :] = jnp.where(even, first, last)
-    for copy in smalls:
-        copy.wait()
-    row_ref[...] = jnp.zeros_like(row_ref)
-    row_ref[0:8, 0:TILE] = tmp_ref[...].T[0:8, :]
-    row_ref[2:3, 0:rows] = dir_ref[...].astype(F32)
-    share_ref[2 * rows :, :] = pltpu.roll(row_ref[...], group * rows, 1)
 
 
 def edge_kernel(
-    first_ref, temp_ref, kappa_ref, slope_ref, ya_ref, yb_ref, share_ref, map_ref,
-    next_ref, yo_ref, sa_ref, sb_ref, fw_ref, crow_ref, flow_ref, strip_ref, small_ref,
+    first_ref, temp_ref, kappa_ref, slope_ref, own_ref, core_ref, cross_ref, relay_ref, map_ref,
+    next_ref, yo_ref, sa_ref, sb_ref, fw_ref, crow_ref, flow_ref, strip_ref, small_ref, all_ref,
 ):
     layers, rows, cols = temp_ref.shape
     span = 2 * rows + 8
-    groups = share_ref.shape[0] // span
+    groups = lax.axis_size("grp")
     group = lax.axis_index("grp")
     even = lax.rem(group, 2) == 0
     place_even = lax.rem(lax.axis_index("loop"), 2) == 0
-    ya, yb = ya_ref[...], yb_ref[...]
+    ya, yb = core_ref[span : span + 4 * layers, :], cross_ref[span : span + 4 * layers, :]
     low, high = jnp.where(even, yb, ya), jnp.where(even, ya, yb)
     yo_ref[0 : 4 * layers, :] = low
     yo_ref[4 * layers :, :] = high
     low_open = jnp.where(group == 0, 0.0, 1.0)
     high_open = jnp.where(group == groups - 1, 0.0, 1.0)
 
-    flow_all = jnp.concatenate([share_ref[i * span : i * span + rows, :] for i in range(groups)], 0)
-    wall_all = jnp.concatenate(
-        [share_ref[i * span + rows : i * span + 2 * rows, :] for i in range(groups)], 0
-    )
-    extra = share_ref[2 * rows : span, :]
-    for i in range(1, groups):
-        extra = extra + share_ref[i * span + 2 * rows : (i + 1) * span, :]
+    beside = group + 1 - 2 * lax.rem(group, 2)
+    extra = jnp.zeros((8, cols), F32)
+    for ref, owner in (
+        (own_ref, group), (core_ref, beside), (cross_ref, groups - 1 - group), (relay_ref, groups - 1 - beside),
+    ):
+        part = pl.ds(pl.multiple_of(owner * rows, 8), rows)
+        all_ref[part, 0:cols] = ref[0:rows, :]
+        all_ref[part, cols : 2 * cols] = ref[rows : 2 * rows, :]
+        extra = extra + ref[2 * rows : span, :]
+    flow_all, wall_all = all_ref[:, 0:cols], all_ref[:, cols : 2 * cols]
     chooser = one_hot(map_ref[...], group * rows - 8, rows + 16)
-    both = pick(chooser, jnp.concatenate([flow_all, wall_all], 1), ((1,), (0,)))
+    both = pick(chooser, all_ref[...], ((1,), (0,)))
     flow_y, wall_y = both[:, :cols], both[:, cols:]
     flow, wall = flow_y[8 : 8 + rows], wall_y[8 : 8 + rows]
     sink = wall * (temp_ref[0] - flow)
@@ -459,44 +492,58 @@
     def shape(*dims):
         return jax.ShapeDtypeStruct(dims, F32)
 
-    def call(body, outs, scratch, *args, ins=None, places=None):
+    def call(body, outs, scratch, *args, far=0, places=None, cost=None):
         return pl.pallas_call(
             body,
             out_shape=outs,
-            in_specs=[pl.BlockSpec(memory_space=ins or pltpu.VMEM)] * len(args),
+            in_specs=[pl.BlockSpec(memory_space=pltpu.HBM)] * far + [pl.BlockSpec(memory_space=pltpu.VMEM)] * (len(args) - far),
             out_specs=[pl.BlockSpec(memory_space=places or pltpu.VMEM)] * len(outs),
             scratch_shapes=scratch,
             compiler_params=params,
-        )(*[pltpu.with_memory_space_constraint(a, ins) if ins else a for a in args])
+            cost_estimate=cost,
+        )(*[pltpu.with_memory_space_constraint(arg, pltpu.HBM) for arg in args[:far]], *args[far:])
 
     def vmem(*dims):
         return pltpu.VMEM(dims, F32)
 
     block = shape(layers, rows, cols)
-    halo = shape(4 * layers, cols)
+    share = shape(2 * rows + 8 + 4 * layers, cols)
     index = jax.ShapeDtypeStruct((1, channels), jnp.int32)
-    first, temp, kappa, slope, power, ya, yb, share, map_row, link_row = call(
-        open_kernel,
-        (block, block, block, block, block, halo, halo, shape(2 * rows + 8, cols), index, index),
+    core, cross, map_row, link_row = call(
+        pack_kernel,
+        (share, share, index, index),
         [
-            vmem(TILE, TILE), vmem(8, cols), pltpu.VMEM((1, rows), jnp.int32),
-            pltpu.SemaphoreType.DMA((4, layers // CHUNK)), pltpu.SemaphoreType.DMA((5,)),
+            vmem(layers, 16, cols), vmem(layers, 16, cols), vmem(layers, 16, cols), vmem(layers, 16, cols),
+            vmem(3, rows, cols), vmem(TILE, TILE), vmem(8, cols), pltpu.VMEM((1, rows), jnp.int32),
+            pltpu.SemaphoreType.DMA((4, 2)), pltpu.SemaphoreType.DMA((3,)), pltpu.SemaphoreType.DMA((2, 2)),
+            pltpu.SemaphoreType.DMA((3,)),
         ],
         solid_temp, kappa, slope, power, coolant_temp, wall_coeff, flow_dir.reshape(1, rows),
         channel_map, loop_link.reshape(1, channels),
-        ins=pltpu.HBM,
-    )
-    ya = lax.ppermute(ya, "grp", pairs(groups, 0, False))
-    yb = lax.ppermute(yb, "grp", pairs(groups, 1, False))
-    share = lax.all_gather(share, "grp", axis=0, tiled=True)
+        far=9,
+    )
+    beside = [(i, i + 1 - 2 * (i % 2)) for i in range(groups)]
+    across = [(i, groups - 1 - i) for i in range(groups)]
+    got_cross = lax.ppermute(cross, "grp", across)
+    got_core = lax.ppermute(core, "grp", beside)
+    first, temp, kappa, slope, power = call(
+        open_kernel,
+        (block, block, block, block, block),
+        [pltpu.SemaphoreType.DMA((4, layers // CHUNK))],
+        solid_temp, kappa, slope, power, map_row,
+        far=4,
+        cost=pl.CostEstimate(flops=30 * layers * rows * cols, bytes_accessed=36 * layers * rows * cols, transcendentals=0),
+    )
+    got_cross, first = lax.optimization_barrier((got_cross, first))
+    relay = lax.ppermute(got_cross, "grp", beside)
     after, yo, sa, sb, fw, crow, flow = call(
         edge_kernel,
         (
             block, shape(8 * layers, cols), shape(8, strip), shape(8, strip),
             shape(2 * rows, cols), shape(8, channels), shape(rows, cols),
         ),
-        [vmem(strip, TILE), vmem(TILE, TILE)],
-        first, temp, kappa, slope, ya, yb, share, map_row,
+        [vmem(strip, TILE), vmem(TILE, TILE), vmem(channels, 2 * cols)],
+        first, temp, kappa, slope, core, got_core, got_cross, relay, map_row,
     )
     ra = lax.ppermute(sa, "loop", pairs(places, 0, True))
     rb = lax.ppermute(sb, "loop", pairs(places, 1, True))

time: 30.3 us -> 28 us (0.924)
  blocking collectives: 15.3 us -> 5.77 us
  waiting for transfers between devices: 0.01 us -> 3.05 us
  starting transfers between devices: 6.92 us -> 9.27 us
  Pallas kernels: 7.29 us -> 9.11 us
    all_gather x1 -> x0, blocking collectives: 9.5 us -> none  [shards(): share = lax.all_gather(share, 'grp', axis=0, tiled=True)]
    ppermute x2 -> x3, waiting for transfers between devices: 0.01 us -> 3.04 us  [the longest x1 1.7 us: shards(): got_cross = lax.ppermute(cross, 'grp', across)]
    ppermute x2 -> x3, starting transfers between devices: 1.17 us -> 3.21 us  [the longest x1 2.44 us: shards(): got_cross = lax.ppermute(cross, 'grp', across)]
    pallas_call x3 -> x4, Pallas kernels: 7.29 us -> 9.11 us  [call(): pl.pallas_call(body, out_shape=outs, in_specs=[pl.BlockSpec(memory_space=...]
  transfers between devices with their start and end apart: 4 -> 5, of which waited for: 0 -> 2; matrix products, arithmetic and copies ran while one was open for 0% -> 0% of each run, Pallas kernels for 0% -> 10%
where the time goes in v3:
time: 28 us; the launch traced here: 27.9 us
  starting transfers between devices  9.27 us (33%)
  Pallas kernels  9.11 us (33%)
  blocking collectives  5.77 us (21%)
  waiting for transfers between devices  3.05 us (11%)
  between operations  0.66 us (2%)
    pallas_call x4, Pallas kernels, call(): pl.pallas_call(body, out_shape=outs, in_specs=[pl.BlockSpec(memory_space=...  9.11 us
    all_gather x1, blocking collectives, shards(): flow = lax.all_gather(flow, 'grp', axis=0, tiled=True)  5.77 us
    ppermute x1, starting transfers between devices, shards(): rb = lax.ppermute(sb, 'loop', pairs(places, 1, True))  3.55 us
    ppermute x1, starting transfers between devices, shards(): ra = lax.ppermute(sa, 'loop', pairs(places, 0, True))  2.51 us
    ppermute x1, starting transfers between devices, shards(): got_cross = lax.ppermute(cross, 'grp', across)  2.44 us
    ppermute x1, waiting for transfers between devices, shards(): got_cross = lax.ppermute(cross, 'grp', across)  1.7 us
    ppermute x1, waiting for transfers between devices, shards(): relay = lax.ppermute(got_cross, 'grp', beside)  1.34 us
    ppermute x1, starting transfers between devices, shards(): got_core = lax.ppermute(core, 'grp', beside)  0.68 us
  transfers between devices with their start and end apart: 5, of which 2 were waited for; matrix products, arithmetic and copies ran while one was open for 0% of the time, Pallas kernels for 10%

profile of v3, /device:TPU:0, one launch (start us, length us, event | category | flops | bytes accessed | tf_op | source)
XLA Modules:
  0.0 27.9 jit_solution(9712280248831885439)
XLA Ops:
  0.6 2.1 %shard_map.104 = (f32[184,256]{1,0:T(8,128)S(1)}, f32[184,256]{1,0:T(8,128)S(1)}, s32[1,256]{1,0:T(1,128)S(1)}, s32[1,256]{1,0:T(1,128)S(1)}) custom-call(f32[12,64,256]{2,1,0:T(8,128)} %temp_hbm.3, f32[12,64,256]{2,1,0:T(8,128)} %kappa_hbm.3, f32[12,64,256]{2,1,0:T(8,128)} %slope_hbm.3, f32[12,64,256]{2,1,0:T(8,128)} %power_hbm.3, f32[64,256]{1,0:T(8,128)} %flow_hbm.1, ...), custom_call_target="tpu_custom_call" | custom-call | tf_op jit(solution)/shard_map/pallas_call | solution.py:496
  2.8 2.4 %collective-permute-start = (f32[184,256]{1,0:T(8,128)S(1)}, f32[184,256]{1,0:T(8,128)S(1)}, u32[]{:S(2)}, u32[]{:S(2)}) collective-permute-start(f32[184,256]{1,0:T(8,128)S(1)} %get-tuple-element.20), channel_id=1, source_target_pairs={{0,24},{8,16},{16,8},{24,0},{1,25},{9,17},{17,9},{25,1},{2,26},{10... | collective-permute-start | bytes 565256 | tf_op jit(solution)/shard_map/ppermute | solution.py:527
  5.2 0.7 %collective-permute-start.1 = (f32[184,256]{1,0:T(8,128)S(1)}, f32[184,256]{1,0:T(8,128)S(1)}, u32[]{:S(2)}, u32[]{:S(2)}) collective-permute-start(f32[184,256]{1,0:T(8,128)S(1)} %get-tuple-element.27.own_ref), channel_id=1, source_target_pairs={{0,8},{8,0},{16,24},{24,16},{1,9},{9,1},{17,25},{25,17},{2,10},{10... | collective-permute-start | bytes 565256 | tf_op jit(solution)/shard_map/ppermute | solution.py:528
  5.9 2.7 %shard_map.105 = (f32[12,64,256]{2,1,0:T(8,128)S(1)}, f32[12,64,256]{2,1,0:T(8,128)S(1)}, f32[12,64,256]{2,1,0:T(8,128)S(1)}, f32[12,64,256]{2,1,0:T(8,128)S(1)}, f32[12,64,256]{2,1,0:T(8,128)S(1)}) custom-call(f32[12,64,256]{2,1,0:T(8,128)} %temp_hbm.3, f32[12,64,256]{2,1,0:T(8,128)} %kappa_hbm.3, f32[12,64,256]{2,1,0:T(8,128)} %slope_hbm.3, ...), custom_call_target="tpu_custom_call" | custom-call | flops 5898240 | bytes 7077888 | tf_op jit(solution)/shard_map/pallas_call | solution.py:496
  8.6 1.7 %collective-permute-done.cross_ref = f32[184,256]{1,0:T(8,128)S(1)} collective-permute-done((f32[184,256]{1,0:T(8,128)S(1)}, f32[184,256]{1,0:T(8,128)S(1)}, u32[]{:S(2)}, u32[]{:S(2)}) %collective-permute-start) | collective-permute-done | bytes 188448 | tf_op jit(solution)/shard_map/ppermute | solution.py:527
  10.3 0.1 collective-permute-start.2
  10.4 0.0 collective-permute-done.1.core_ref
  10.4 1.3 %collective-permute-done.2.relay_ref = f32[184,256]{1,0:T(8,128)S(1)} collective-permute-done((f32[184,256]{1,0:T(8,128)S(1)}, f32[184,256]{1,0:T(8,128)S(1)}, u32[]{:S(2)}, u32[]{:S(2)}) %collective-permute-start.2) | collective-permute-done | bytes 188448 | tf_op jit(solution)/shard_map/ppermute | solution.py:538
  11.8 1.5 %shard_map.106 = (f32[12,64,256]{2,1,0:T(8,128)S(1)}, f32[96,256]{1,0:T(8,128)S(1)}, f32[8,768]{1,0:T(8,128)S(1)}, f32[8,768]{1,0:T(8,128)S(1)}, f32[128,256]{1,...) custom-call(f32[12,64,256]{2,1,0:T(8,128)S(1)} %get-tuple-element.23.first_ref, ...), custom_call_target="tpu_custom_call" | custom-call | tf_op jit(solution)/shard_map/pallas_call | solution.py:496
  13.2 2.5 %collective-permute-start.3 = (f32[8,768]{1,0:T(8,128)S(1)}, f32[8,768]{1,0:T(8,128)S(1)}, u32[]{:S(2)}, u32[]{:S(2)}) collective-permute-start(f32[8,768]{1,0:T(8,128)S(1)} %get-tuple-element.32.sa_ref), channel_id=1, source_target_pairs={{0,1},{1,0},{2,3},{3,2},{4,5},{5,4},{6,7},{7,6},{8,9},{9,8},{10,11... | collective-permute-start | bytes 73736 | tf_op jit(solution)/shard_map/ppermute | solution.py:548
  15.8 3.5 %collective-permute-start.4 = (f32[8,768]{1,0:T(8,128)S(1)}, f32[8,768]{1,0:T(8,128)S(1)}, u32[]{:S(2)}, u32[]{:S(2)}) collective-permute-start(f32[8,768]{1,0:T(8,128)S(1)} %get-tuple-element.33.sb_ref), channel_id=1, source_target_pairs={{1,2},{2,1},{3,4},{4,3},{5,6},{6,5},{7,0},{0,7},{9,10},{10,9},{11,... | collective-permute-start | bytes 73736 | tf_op jit(solution)/shard_map/ppermute | solution.py:549
  19.3 5.8 %all_gather.3.all_ref = f32[256,256]{1,0:T(8,128)S(1)} all-gather(f32[64,256]{1,0:T(8,128)S(1)} %get-tuple-element.37), channel_id=1, replica_groups=mesh['grp'=4,'loop'=8] {'grp'}, dimensions={0}, use_global_device_ids=true | all-gather | bytes 327680 | tf_op jit(solution)/shard_map/all_gather | solution.py:550
  25.1 0.0 collective-permute-done.3.ra_ref
  25.1 0.0 collective-permute-done.4.rb_ref
  25.1 2.8 %shard_map.107 = (f32[12,64,256]{2,1,0:T(8,128)}, f32[64,256]{1,0:T(8,128)}) custom-call(f32[12,64,256]{2,1,0:T(8,128)S(1)} %get-tuple-element.29.temp_ref, f32[12,64,256]{2,1,0:T(8,128)S(1)} %get-tuple-element.25.kappa_ref, f32[12,64,256]{2,1,0:T(8,128)S(1)} %get-tuple-element.26.slope_ref, f32[12,64,256]{2,1,0:T(8,128)S(1)} %get-tuple-element.30.power_ref, ...), custom_call_target="tpu_custom_call" | custom-call | tf_op jit(solution)/shard_map/pallas_call | solution.py:496
Async XLA Ops:
  2.8 7.6 %collective-permute-start = (f32[184,256]{1,0:T(8,128)S(1)}, f32[184,256]{1,0:T(8,128)S(1)}, u32[]{:S(2)}, u32[]{:S(2)}) collective-permute-start(f32[184,256]{1,0:T(8,128)S(1)} %get-tuple-element.20), channel_id=1, source_target_pairs={{0,24},{8,16},{16,8},{24,0},{1,25},{9,17},{17,9},{25,1},{2,26},{10... | collective-permute-start | bytes 565256 | tf_op jit(solution)/shard_map/ppermute | solution.py:527
  5.2 5.2 %collective-permute-start.1 = (f32[184,256]{1,0:T(8,128)S(1)}, f32[184,256]{1,0:T(8,128)S(1)}, u32[]{:S(2)}, u32[]{:S(2)}) collective-permute-start(f32[184,256]{1,0:T(8,128)S(1)} %get-tuple-element.27.own_ref), channel_id=1, source_target_pairs={{0,8},{8,0},{16,24},{24,16},{1,9},{9,1},{17,25},{25,17},{2,10},{10... | collective-permute-start | bytes 565256 | tf_op jit(solution)/shard_map/ppermute | solution.py:528
  10.3 1.4 %collective-permute-start.2 = (f32[184,256]{1,0:T(8,128)S(1)}, f32[184,256]{1,0:T(8,128)S(1)}, u32[]{:S(2)}, u32[]{:S(2)}) collective-permute-start(f32[184,256]{1,0:T(8,128)S(1)} %collective-permute-done.cross_ref), channel_id=1, source_target_pairs={{0,8},{8,0},{16,24},{24,16},{1,9},{9,1},{17,25},{25,17},{2,10},{10... | collective-permute-start | bytes 565256 | tf_op jit(solution)/shard_map/ppermute | solution.py:538
  13.2 11.8 %collective-permute-start.3 = (f32[8,768]{1,0:T(8,128)S(1)}, f32[8,768]{1,0:T(8,128)S(1)}, u32[]{:S(2)}, u32[]{:S(2)}) collective-permute-start(f32[8,768]{1,0:T(8,128)S(1)} %get-tuple-element.32.sa_ref), channel_id=1, source_target_pairs={{0,1},{1,0},{2,3},{3,2},{4,5},{5,4},{6,7},{7,6},{8,9},{9,8},{10,11... | collective-permute-start | bytes 73736 | tf_op jit(solution)/shard_map/ppermute | solution.py:548
  15.8 9.3 %collective-permute-start.4 = (f32[8,768]{1,0:T(8,128)S(1)}, f32[8,768]{1,0:T(8,128)S(1)}, u32[]{:S(2)}, u32[]{:S(2)}) collective-permute-start(f32[8,768]{1,0:T(8,128)S(1)} %get-tuple-element.33.sb_ref), channel_id=1, source_target_pairs={{1,2},{2,1},{3,4},{4,3},{5,6},{6,5},{7,0},{0,7},{9,10},{10,9},{11,... | collective-permute-start | bytes 73736 | tf_op jit(solution)/shard_map/ppermute | solution.py:549

commit v4 on v3

--- a/solution.py
+++ b/solution.py
@@ -44,8 +44,12 @@
     return jnp.where(index_row == here, 1.0, 0.0).astype(BF16)
 
 
+def conduct(kappa, slope, temp):
+    return (0.5 * time_step) * kappa * (1.0 + slope * temp)
+
+
 def face(cond_a, cond_b, temp_a, temp_b):
-    return 0.5 * (cond_a + cond_b) * (temp_b - temp_a)
+    return (cond_a + cond_b) * (temp_b - temp_a)
 
 
 def closed_heat(temp_ref, kappa_ref, slope_ref, emit, ready=lambda z: None):
@@ -54,7 +58,7 @@
     row = lax.broadcasted_iota(jnp.int32, (rows, cols), 0)
     ready(0)
     temp = temp_ref[0]
-    cond = kappa_ref[0] * (1.0 + slope_ref[0] * temp)
+    cond = conduct(kappa_ref[0], slope_ref[0], temp)
     flux_below = None
     for z in range(layers):
         if z + 1 < layers:
@@ -69,7 +73,7 @@
             heat = heat - flux_below
         if z + 1 < layers:
             temp_up = temp_ref[z + 1]
-            cond_up = kappa_ref[z + 1] * (1.0 + slope_ref[z + 1] * temp_up)
+            cond_up = conduct(kappa_ref[z + 1], slope_ref[z + 1], temp_up)
             flux_below = face(cond, cond_up, temp, temp_up)
             heat = heat + flux_below
         emit(z, temp, cond, heat)
@@ -79,7 +83,7 @@
 
 def pack_kernel(
     temp_hbm, kappa_hbm, slope_hbm, power_hbm, flow_hbm, wall_hbm, dir_hbm, map_hbm, link_hbm,
-    core_ref, cross_ref, map_ref, link_ref,
+    core_ref, cross_ref, step_ref, map_ref, link_ref,
     temp_ref, kappa_ref, slope_ref, power_ref, top_ref, tmp_ref, row_ref, dir_ref,
     block_sem, top_sem, share_sem, small_sem,
 ):
@@ -114,17 +118,17 @@
         copy.wait()
 
     def emit(z, temp, cond, heat):
-        after = temp + time_step * (heat + power_ref[z])
+        after = temp + heat + time_step * power_ref[z]
         for q, value in enumerate((after, temp, kappa_ref[z], slope_ref[z])):
-            at = share + q * layers + z
-            core_ref[at : at + 1, :] = jnp.where(even, value[15:16], value[0:1])
-            cross_ref[at : at + 1, :] = jnp.where(even, value[0:1], value[15:16])
+            at = q * layers + z
+            core_ref[share + at : share + at + 1, :] = jnp.where(even, value[15:16], value[0:1])
+            step_ref[at : at + 1, :] = jnp.where(even, value[0:1], value[15:16])
 
     closed_heat(temp_ref, kappa_ref, slope_ref, emit)
     for copy in tops:
         copy.wait()
     temp = top_ref[0]
-    cond = top_ref[1] * (1.0 + top_ref[2] * temp)
+    cond = conduct(top_ref[1], top_ref[2], temp)
     lane = lax.broadcasted_iota(jnp.int32, (rows, TILE), 1)
     packed = jnp.where(lane == 0, temp[:, 0:TILE], pltpu.roll(temp[:, cols - TILE :], 2, 1))
     packed = jnp.where(lane == 3, pltpu.roll(cond[:, 0:TILE], 3, 1), packed)
@@ -163,14 +167,14 @@
                 copy.wait()
 
     def emit(z, temp, cond, heat):
-        next_ref[z] = temp + time_step * (heat + power_ref[z])
+        next_ref[z] = temp + heat + time_step * power_ref[z]
 
     closed_heat(temp_ref, kappa_ref, slope_ref, emit, ready)
 
 
 def edge_kernel(
-    first_ref, temp_ref, kappa_ref, slope_ref, own_ref, core_ref, cross_ref, relay_ref, map_ref,
-    next_ref, yo_ref, sa_ref, sb_ref, fw_ref, crow_ref, flow_ref, strip_ref, small_ref, all_ref,
+    first_ref, temp_ref, kappa_ref, slope_ref, own_ref, core_ref, cross_ref, relay_ref, step_ref, map_ref,
+    next_ref, yo_ref, sa_ref, sb_ref, fw_ref, crow_ref, strip_ref, small_ref, all_ref,
 ):
     layers, rows, cols = temp_ref.shape
     span = 2 * rows + 8
@@ -178,7 +182,7 @@
     group = lax.axis_index("grp")
     even = lax.rem(group, 2) == 0
     place_even = lax.rem(lax.axis_index("loop"), 2) == 0
-    ya, yb = core_ref[span : span + 4 * layers, :], cross_ref[span : span + 4 * layers, :]
+    ya, yb = core_ref[span : span + 4 * layers, :], step_ref[...]
     low, high = jnp.where(even, yb, ya), jnp.where(even, ya, yb)
     yo_ref[0 : 4 * layers, :] = low
     yo_ref[4 * layers :, :] = high
@@ -199,6 +203,8 @@
     both = pick(chooser, all_ref[...], ((1,), (0,)))
     flow_y, wall_y = both[:, :cols], both[:, cols:]
     flow, wall = flow_y[8 : 8 + rows], wall_y[8 : 8 + rows]
+    fw_ref[0:rows, :] = flow
+    fw_ref[rows:, :] = wall
     sink = wall * (temp_ref[0] - flow)
     temp_low, temp_high = yo_ref[layers : layers + 1, :], yo_ref[5 * layers : 5 * layers + 1, :]
     sink_low = wall_y[7:8] * (temp_low - flow_y[7:8])
@@ -217,17 +223,19 @@
             (1, 4 * layers, rows - 1, high_open, sink_high),
         ):
             temp_h = yo_ref[base + layers + z : base + layers + z + 1, :]
-            cond_h = yo_ref[base + 2 * layers + z : base + 2 * layers + z + 1, :] * (
-                1.0 + yo_ref[base + 3 * layers + z : base + 3 * layers + z + 1, :] * temp_h
+            cond_h = conduct(
+                yo_ref[base + 2 * layers + z : base + 2 * layers + z + 1, :],
+                yo_ref[base + 3 * layers + z : base + 3 * layers + z + 1, :],
+                temp_h,
             )
             temp_e = temp[at : at + 1]
-            cond_e = kappa[at : at + 1] * (1.0 + slope[at : at + 1] * temp_e)
+            cond_e = conduct(kappa[at : at + 1], slope[at : at + 1], temp_e)
             flux = opened * face(cond_e, cond_h, temp_e, temp_h)
-            halo = yo_ref[base + z : base + z + 1, :] - time_step * flux
+            halo = yo_ref[base + z : base + z + 1, :] - flux
             if z == 0:
                 halo = halo - time_step * sunk
             yo_ref[base + z : base + z + 1, :] = halo
-            edges.append(time_step * flux)
+            edges.append(flux)
             corner = jnp.where(
                 lane1 == 0,
                 temp_h[:, 0:TILE],
@@ -254,21 +262,6 @@
             packed = left if packed is None else jnp.where(lane == n, left, packed)
             packed = jnp.where(lane == n + 4, right, packed)
         strip_ref[z * rows : (z + 1) * rows, :] = packed
-    toward_y = pick(chooser[8 : 8 + rows], jnp.broadcast_to(extra[2:3], (TILE, groups * rows)), ((1,), (1,)))
-    toward_y = jnp.concatenate([toward_y] * (cols // TILE), 1) > 0.5
-    lane_w = lax.broadcasted_iota(jnp.int32, (rows, cols), 1)
-
-    def upstream(values):
-        before = jnp.where(lane_w == 0, 0.0, pltpu.roll(values, 1, 1))
-        after = jnp.where(lane_w == cols - 1, 0.0, pltpu.roll(values, cols - 1, 1))
-        return jnp.where(toward_y, before, after)
-
-    flow = flow - courant * (flow - upstream(flow)) + heat_gain * sink
-    fw_ref[0:rows, :] = flow
-    fw_ref[rows:, :] = wall
-    flux = wall * (next_ref[0] - flow)
-    flow_ref[...] = flow - courant * (flow - upstream(flow)) + heat_gain * flux
-
     strips = strip_ref[...].T[0:8, :]
     corners = small_ref[...].T[0:8, :]
 
@@ -304,10 +297,29 @@
         ref[7:8, 0:channels] = jnp.where(pick_right, part_e, part_0)
 
 
+def coolant_kernel(fw_ref, temp_ref, after_ref, crow_ref, map_ref, first_ref, second_ref):
+    rows, cols = first_ref.shape
+    channels = crow_ref.shape[1]
+    chooser = one_hot(map_ref[...], lax.axis_index("grp") * rows, rows)
+    toward = pick(chooser, jnp.broadcast_to(crow_ref[0:1, :], (TILE, channels)), ((1,), (1,)))
+    toward = jnp.concatenate([toward] * (cols // TILE), 1) > 0.5
+    lane = lax.broadcasted_iota(jnp.int32, (rows, cols), 1)
+
+    def advance(flow, temp):
+        before = jnp.where(lane == 0, 0.0, pltpu.roll(flow, 1, 1))
+        after = jnp.where(lane == cols - 1, 0.0, pltpu.roll(flow, cols - 1, 1))
+        flux = fw_ref[rows:, :] * (temp - flow)
+        return flow - courant * (flow - jnp.where(toward, before, after)) + heat_gain * flux
+
+    first = advance(fw_ref[0:rows, :], temp_ref[0])
+    first_ref[...] = first
+    second_ref[...] = advance(first, after_ref[0])
+
+
 def close_kernel(
     temp_ref, kappa_ref, slope_ref, power_ref, yo_ref, ra_ref, rb_ref, sa_ref, sb_ref,
-    fw_ref, crow_ref, map_ref, link_ref, all_ref,
-    out_hbm, flow_hbm, wide_ref, xt_ref, xc_ref, xf_ref, full_ref, out_ref, flow_ref, sel_ref, turn_ref, out_sem,
+    flow_ref, fw_ref, crow_ref, map_ref, link_ref,
+    out_hbm, tail_ref, add_ref, wide_ref, xt_ref, xc_ref, xf_ref, full_ref, out_ref, turn_ref, out_sem,
 ):
     layers, rows, cols = temp_ref.shape
     group, groups = lax.axis_index("grp"), lax.axis_size("grp")
@@ -329,12 +341,12 @@
     temps, conds, fluxes = [], [], []
     for side in range(2):
         temp_n, temp_o = got[side][1:2], own[side][1:2]
-        cond_n = got[side][2:3] * (1.0 + got[side][3:4] * temp_n)
-        cond_o = own[side][2:3] * (1.0 + own[side][3:4] * temp_o)
-        flux = time_step * face(cond_o, cond_n, temp_o, temp_n)
+        cond_n = conduct(got[side][2:3], got[side][3:4], temp_n)
+        cond_o = conduct(own[side][2:3], own[side][3:4], temp_o)
+        flux = face(cond_o, cond_n, temp_o, temp_n)
         after = got[side][0:1] - flux
         temps.append(after)
-        conds.append(got[side][2:3] * (1.0 + got[side][3:4] * after))
+        conds.append(conduct(got[side][2:3], got[side][3:4], after))
         fluxes.append(flux)
     turn(temps[0], temps[1], xt_ref)
     turn(conds[0], conds[1], xc_ref)
@@ -354,18 +366,18 @@
         before = yo_ref[base + layers : base + 2 * layers, :]
         kappa = yo_ref[base + 2 * layers : base + 3 * layers, :]
         slope = yo_ref[base + 3 * layers : base + 4 * layers, :]
-        cond = kappa * (1.0 + slope * before)
+        cond = conduct(kappa, slope, before)
         c_t, c_c = corner_t[16 * side : 16 * side + layers], corner_c[16 * side : 16 * side + layers]
         tiles = []
         for start, at in ((0, 0), (cols - TILE, TILE - 1)):
-            flux = time_step * face(
+            flux = face(
                 cond[:, start : start + TILE], c_c, before[:, start : start + TILE], c_t
             )
             tiles.append(after[:, start : start + TILE] + jnp.where(lane_l == at, flux, 0.0))
         after = jnp.concatenate([tiles[0], after[:, TILE : cols - TILE], tiles[1]], 1) if (
             cols > 2 * TILE
         ) else jnp.concatenate(tiles, 1)
-        halo.append((after, kappa * (1.0 + slope * after)))
+        halo.append((after, conduct(kappa, slope, after)))
 
     lane = lax.broadcasted_iota(jnp.int32, (rows, TILE), 1)
     for z in range(layers):
@@ -397,7 +409,7 @@
     shift_0 = courant * toward_c * edge_rows[0][0]
     shift_e = courant * (1.0 - toward_c) * edge_rows[0][1]
     tops = [
-        time_step * face(
+        face(
             own[side][5:6, channels : 2 * channels], got[side][5:6, channels : 2 * channels],
             own[side][4:5, channels : 2 * channels], got[side][4:5, channels : 2 * channels],
         )
@@ -421,17 +433,12 @@
     edge_y = pick(chooser, jnp.where(wide_row == 0, shift_0, shift_e), ((1,), (1,)))
     adds = jnp.where(wide_row == 0, add_0, jnp.where(wide_row == 1, courant * toward_c * shift_0, add_e))
     adds = jnp.where(wide_row == TILE - 2, courant * (1.0 - toward_c) * shift_e, adds)
-    turn_ref[...] = adds.T
-    sel_ref[...] = pick(every, all_ref[...], ((0,), (0,)))
-    mine = pl.ds(pl.multiple_of(group * rows, 8), rows)
-    adds, flow = turn_ref[mine, :], sel_ref[mine, :]
+    turn_ref[0:channels, :] = adds.T
+    turn_ref[channels:, :] = jnp.broadcast_to(map_ref[...].astype(F32), (TILE, channels)).T
+    add_ref[0:rows, :] = turn_ref[pl.ds(pl.multiple_of(group * rows, 8), rows), :]
+    add_ref[rows:, :] = turn_ref[pl.ds(pl.multiple_of(channels + group * rows, 8), rows), :]
     pad = [jnp.zeros((rows, cols - 2 * TILE), F32)] if cols > 2 * TILE else []
-    flow_ref[...] = flow + jnp.concatenate(
-        [jnp.where(lane < 2, adds, 0.0)] + pad + [jnp.where(lane >= TILE - 2, adds, 0.0)], 1
-    )
-    flow_copy = pltpu.make_async_copy(flow_ref, flow_hbm, out_sem.at[layers])
-    flow_copy.start()
-    flow = fw_ref[0:rows, :] + jnp.concatenate(
+    flow = flow_ref[...] + jnp.concatenate(
         [jnp.where(lane == 0, edge_y, 0.0)] + pad + [jnp.where(lane == TILE - 1, edge_y, 0.0)], 1
     )
     flux = fw_ref[rows:, :] * (full_ref[0] - flow)
@@ -439,7 +446,7 @@
     row8 = lax.broadcasted_iota(jnp.int32, (8, cols), 0)
 
     def emit(z, temp, cond, heat):
-        result = temp + time_step * (heat + power_ref[z])
+        result = temp + heat + time_step * power_ref[z]
         if z == 0:
             result = result - time_step * flux
         halo_t = xt_ref[z * rows : (z + 1) * rows, :]
@@ -447,25 +454,58 @@
         sides = []
         for start, at in ((0, 0), (cols - TILE, TILE - 1)):
             part = slice(start, start + TILE)
-            extra = time_step * face(cond[:, part], halo_c, temp[:, part], halo_t)
+            extra = face(cond[:, part], halo_c, temp[:, part], halo_t)
             sides.append(jnp.where(lane == at, extra, 0.0))
         middle = [jnp.zeros((rows, cols - 2 * TILE), F32)] if cols > 2 * TILE else []
         result = result + jnp.concatenate([sides[0]] + middle + [sides[1]], 1)
-        out_ref[z] = result
+        early = layers - tail_ref.shape[0]
+        target, at_z = (out_ref, z) if z < early else (tail_ref, z - early)
+        target[at_z] = result
         for side, opened, start, at in ((0, low_open, 0, 0), (1, high_open, rows - 8, 7)):
             part = slice(start, start + 8)
-            extra = (time_step * opened) * face(
+            extra = opened * face(
                 cond[part], halo[side][1][z : z + 1], temp[part], halo[side][0][z : z + 1]
             )
-            out_ref[z, part, :] = result[part] + jnp.where(row8 == at, extra, 0.0)
-
-        copies.append(pltpu.make_async_copy(out_ref.at[z], out_hbm.at[z], out_sem.at[z]))
-        copies[-1].start()
-
-    copies = [flow_copy]
+            target[at_z, part, :] = result[part] + jnp.where(row8 == at, extra, 0.0)
+        if z < early:
+            copies.append(pltpu.make_async_copy(out_ref.at[z], out_hbm.at[z], out_sem.at[z]))
+            copies[-1].start()
+
+    copies = []
     closed_heat(full_ref, kappa_ref, slope_ref, emit)
     for copy in copies:
         copy.wait()
+
+
+def return_kernel(
+    part_hbm, tail_ref, own_ref, core_ref, cross_ref, relay_ref, add_ref,
+    out_hbm, flow_hbm, all_ref, out_ref, sem,
+):
+    rows, cols = out_ref.shape
+    layers, late = out_hbm.shape[0], tail_ref.shape[0]
+    tail = pltpu.make_async_copy(tail_ref, out_hbm.at[layers - late : layers], sem.at[0])
+    tail.start()
+    group, groups = lax.axis_index("grp"), lax.axis_size("grp")
+    beside = group + 1 - 2 * lax.rem(group, 2)
+    for ref, owner in (
+        (own_ref, group), (core_ref, beside), (cross_ref, groups - 1 - group), (relay_ref, groups - 1 - beside),
+    ):
+        all_ref[pl.ds(pl.multiple_of(owner * rows, 8), rows), :] = ref[...]
+    lane = lax.broadcasted_iota(jnp.int32, (rows, TILE), 1)
+    adds, row = add_ref[0:rows, :], add_ref[rows:, :]
+    channels = groups * rows
+    chooser = jnp.concatenate(
+        [jnp.where(row == (lane + start).astype(F32), 1.0, 0.0) for start in range(0, channels, TILE)], 1
+    ).astype(BF16)
+    flow = pick(chooser, all_ref[...], ((1,), (0,)))
+    pad = [jnp.zeros((rows, cols - 2 * TILE), F32)] if cols > 2 * TILE else []
+    out_ref[...] = flow + jnp.concatenate(
+        [jnp.where(lane < 2, adds, 0.0)] + pad + [jnp.where(lane >= TILE - 2, adds, 0.0)], 1
+    )
+    back = pltpu.make_async_copy(out_ref, flow_hbm, sem.at[1])
+    back.start()
+    tail.wait()
+    back.wait()
 
 
 def pairs(count, first, closed):
@@ -492,26 +532,32 @@
     def shape(*dims):
         return jax.ShapeDtypeStruct(dims, F32)
 
-    def call(body, outs, scratch, *args, far=0, places=None, cost=None):
+    def call(body, outs, scratch, *args, far=0, outs_far=0, cost=None, alias={}):
         return pl.pallas_call(
             body,
             out_shape=outs,
             in_specs=[pl.BlockSpec(memory_space=pltpu.HBM)] * far + [pl.BlockSpec(memory_space=pltpu.VMEM)] * (len(args) - far),
-            out_specs=[pl.BlockSpec(memory_space=places or pltpu.VMEM)] * len(outs),
+            out_specs=[pl.BlockSpec(memory_space=pltpu.HBM)] * outs_far
+            + [pl.BlockSpec(memory_space=pltpu.VMEM)] * (len(outs) - outs_far),
             scratch_shapes=scratch,
             compiler_params=params,
             cost_estimate=cost,
+            input_output_aliases=alias,
         )(*[pltpu.with_memory_space_constraint(arg, pltpu.HBM) for arg in args[:far]], *args[far:])
 
     def vmem(*dims):
         return pltpu.VMEM(dims, F32)
 
+    heavy = pl.CostEstimate(
+        flops=30 * layers * rows * cols, bytes_accessed=36 * layers * rows * cols, transcendentals=0
+    )
     block = shape(layers, rows, cols)
-    share = shape(2 * rows + 8 + 4 * layers, cols)
+    share = shape(2 * rows + 8, cols)
+    wide = shape(2 * rows + 8 + 4 * layers, cols)
     index = jax.ShapeDtypeStruct((1, channels), jnp.int32)
-    core, cross, map_row, link_row = call(
+    core, cross, step, map_row, link_row = call(
         pack_kernel,
-        (share, share, index, index),
+        (wide, share, shape(4 * layers, cols), index, index),
         [
             vmem(layers, 16, cols), vmem(layers, 16, cols), vmem(layers, 16, cols), vmem(layers, 16, cols),
             vmem(3, rows, cols), vmem(TILE, TILE), vmem(8, cols), pltpu.VMEM((1, rows), jnp.int32),
@@ -525,6 +571,7 @@
     beside = [(i, i + 1 - 2 * (i % 2)) for i in range(groups)]
     across = [(i, groups - 1 - i) for i in range(groups)]
     got_cross = lax.ppermute(cross, "grp", across)
+    got_step = lax.ppermute(step, "grp", pairs(groups, 1, False))
     got_core = lax.ppermute(core, "grp", beside)
     first, temp, kappa, slope, power = call(
         open_kernel,
@@ -532,32 +579,48 @@
         [pltpu.SemaphoreType.DMA((4, layers // CHUNK))],
         solid_temp, kappa, slope, power, map_row,
         far=4,
-        cost=pl.CostEstimate(flops=30 * layers * rows * cols, bytes_accessed=36 * layers * rows * cols, transcendentals=0),
-    )
-    got_cross, first = lax.optimization_barrier((got_cross, first))
+        cost=heavy,
+    )
+    got_cross, got_step, first = lax.optimization_barrier((got_cross, got_step, first))
     relay = lax.ppermute(got_cross, "grp", beside)
-    after, yo, sa, sb, fw, crow, flow = call(
+    after, yo, sa, sb, fw, crow = call(
         edge_kernel,
         (
-            block, shape(8 * layers, cols), shape(8, strip), shape(8, strip),
-            shape(2 * rows, cols), shape(8, channels), shape(rows, cols),
+            block, shape(8 * layers, cols), shape(24, strip), shape(24, strip),
+            shape(2 * rows, cols), shape(8, channels),
         ),
         [vmem(strip, TILE), vmem(TILE, TILE), vmem(channels, 2 * cols)],
-        first, temp, kappa, slope, core, got_core, got_cross, relay, map_row,
+        first, temp, kappa, slope, core, got_core, got_cross, relay, got_step, map_row,
     )
     ra = lax.ppermute(sa, "loop", pairs(places, 0, True))
     rb = lax.ppermute(sb, "loop", pairs(places, 1, True))
-    flow = lax.all_gather(flow, "grp", axis=0, tiled=True)
-    return call(
+    flow1, flow = call(
+        coolant_kernel, (shape(rows, cols), shape(rows, cols)), [], fw, temp, after, crow, map_row,
+    )
+    got_across = lax.ppermute(flow, "grp", across)
+    got_over = lax.ppermute(flow, "grp", [(i, (i + groups // 2) % groups) for i in range(groups)])
+    got_beside = lax.ppermute(flow, "grp", beside)
+    late = layers // 3
+    out, tail, adds = call(
         close_kernel,
-        (block, shape(rows, cols)),
+        (block, shape(late, rows, cols), shape(2 * rows, TILE)),
         [
             vmem(TILE, strip), vmem(strip, TILE), vmem(strip, TILE), vmem(strip, TILE),
-            vmem(layers, rows, cols), vmem(layers, rows, cols), vmem(rows, cols),
-            vmem(channels, cols), vmem(channels, TILE), pltpu.SemaphoreType.DMA((layers + 1,)),
+            vmem(layers, rows, cols), vmem(layers - late, rows, cols), vmem(2 * channels, TILE),
+            pltpu.SemaphoreType.DMA((layers - late,)),
         ],
-        after, kappa, slope, power, yo, ra, rb, sa, sb, fw, crow, map_row, link_row, flow,
-        places=pltpu.HBM,
+        after, kappa, slope, power, yo, ra, rb, sa, sb, flow1, fw, crow, map_row, link_row,
+        outs_far=1,
+        cost=heavy,
+    )
+    return call(
+        return_kernel,
+        (block, shape(rows, cols)),
+        [vmem(channels, cols), vmem(rows, cols), pltpu.SemaphoreType.DMA((2,))],
+        out, tail, flow, got_beside, got_across, got_over, adds,
+        far=1,
+        outs_far=2,
+        alias={0: 0},
     )
 
 

time: 28 us -> 25.8 us (0.921)
  blocking collectives: 5.77 us -> 0 us
  starting transfers between devices: 9.27 us -> 13.1 us
  waiting for transfers between devices: 3.05 us -> 2.07 us
  Pallas kernels: 9.11 us -> 9.74 us
    all_gather x1 -> x0, blocking collectives: 5.77 us -> none  [shards(): flow = lax.all_gather(flow, 'grp', axis=0, tiled=True)]
    ppermute x0 -> x4, starting transfers between devices: none -> 2.86 us  [the longest x1 1.58 us: shards(): lax.ppermute(flow, 'grp', [(i, (i + groups // 2) % groups) for i in range...]
    ppermute x1, waiting for transfers between devices: 1.7 us -> 0.01 us  [shards(): got_cross = lax.ppermute(cross, 'grp', across)]
    ppermute x1, starting transfers between devices: 0.68 us -> 2.01 us  [shards(): got_core = lax.ppermute(core, 'grp', beside)]
    ppermute x1, waiting for transfers between devices: 0.01 us -> 0.98 us  [shards(): rb = lax.ppermute(sb, 'loop', pairs(places, 1, True))]
    ppermute x1, starting transfers between devices: 2.51 us -> 1.6 us  [shards(): ra = lax.ppermute(sa, 'loop', pairs(places, 0, True))]
    pallas_call x4 -> x6, Pallas kernels: 9.11 us -> 9.74 us  [call(): pl.pallas_call(body, out_shape=outs, in_specs=[pl.BlockSpec(memory_space=...]
    ppermute x1, starting transfers between devices: 0.09 us -> 0.67 us  [shards(): relay = lax.ppermute(got_cross, 'grp', beside)]
  transfers between devices with their start and end apart: 5 -> 9, of which waited for: 2 -> 3; matrix products, arithmetic and copies ran while one was open for 0% -> 0% of each run, Pallas kernels for 10% -> 21%
where the time goes in v4:
time: 25.8 us; the launch traced here: 25.6 us
  starting transfers between devices  13.1 us (51%)
  Pallas kernels  9.74 us (38%)
  waiting for transfers between devices  2.07 us (8%)
  between operations  0.71 us (3%)
    pallas_call x6, Pallas kernels, call(): pl.pallas_call(body, out_shape=outs, in_specs=[pl.BlockSpec(memory_space=...  9.74 us
    ppermute x1, starting transfers between devices, shards(): rb = lax.ppermute(sb, 'loop', pairs(places, 1, True))  3.54 us
    ppermute x1, starting transfers between devices, shards(): got_cross = lax.ppermute(cross, 'grp', across)  2.44 us
    ppermute x1, starting transfers between devices, shards(): got_core = lax.ppermute(core, 'grp', beside)  2.01 us
    ppermute x1, starting transfers between devices, shards(): ra = lax.ppermute(sa, 'loop', pairs(places, 0, True))  1.6 us
    ppermute x1, starting transfers between devices, shards(): lax.ppermute(flow, 'grp', [(i, (i + groups // 2) % groups) for i in range...  1.58 us
    ppermute x1, waiting for transfers between devices, shards(): relay = lax.ppermute(got_cross, 'grp', beside)  0.99 us
    ppermute x1, waiting for transfers between devices, shards(): rb = lax.ppermute(sb, 'loop', pairs(places, 1, True))  0.98 us
  transfers between devices with their start and end apart: 9, of which 3 were waited for; matrix products, arithmetic and copies ran while one was open for 0% of the time, Pallas kernels for 21%

profile of v4, /device:TPU:0, one launch (start us, length us, event | category | flops | bytes accessed | tf_op | source)
XLA Modules:
  0.0 25.6 jit_solution(3479050530984284913)
XLA Ops:
  0.6 2.1 %shard_map.104 = (f32[184,256]{1,0:T(8,128)S(1)}, f32[136,256]{1,0:T(8,128)S(1)}, f32[48,256]{1,0:T(8,128)S(1)}, s32[1,256]{1,0:T(1,128)S(1)}, s32[1,256]{1,0:T(1,128)S(1)}) custom-call(f32[12,64,256]{2,1,0:T(8,128)} %temp_hbm.3, f32[12,64,256]{2,1,0:T(8,128)} %kappa_hbm.3, f32[12,64,256]{2,1,0:T(8,128)} %slope_hbm.3, f32[12,64,256]{2,1,0:T(8,128)} %power_hbm.3, ...), custom_call_target="tpu_custom_call" | custom-call | tf_op jit(solution)/shard_map/pallas_call | solution.py:536
  2.7 2.4 %collective-permute-start = (f32[136,256]{1,0:T(8,128)S(1)}, f32[136,256]{1,0:T(8,128)S(1)}, u32[]{:S(2)}, u32[]{:S(2)}) collective-permute-start(f32[136,256]{1,0:T(8,128)S(1)} %get-tuple-element.26), channel_id=1, source_target_pairs={{0,24},{8,16},{16,8},{24,0},{1,25},{9,17},{17,9},{25,1},{2,26},{10... | collective-permute-start | bytes 417800 | tf_op jit(solution)/shard_map/ppermute | solution.py:573
  5.2 0.7 %collective-permute-start.1 = (f32[48,256]{1,0:T(8,128)S(1)}, f32[48,256]{1,0:T(8,128)S(1)}, u32[]{:S(2)}, u32[]{:S(2)}) collective-permute-start(f32[48,256]{1,0:T(8,128)S(1)} %get-tuple-element.27), channel_id=1, source_target_pairs={{8,16},{16,8},{9,17},{17,9},{10,18},{18,10},{11,19},{19,11},{12,20... | collective-permute-start | bytes 147464 | tf_op jit(solution)/shard_map/ppermute | solution.py:574
  5.8 2.0 %collective-permute-start.2 = (f32[184,256]{1,0:T(8,128)S(1)}, f32[184,256]{1,0:T(8,128)S(1)}, u32[]{:S(2)}, u32[]{:S(2)}) collective-permute-start(f32[184,256]{1,0:T(8,128)S(1)} %get-tuple-element.34.own_ref), channel_id=1, source_target_pairs={{0,8},{8,0},{16,24},{24,16},{1,9},{9,1},{17,25},{25,17},{2,10},{10... | collective-permute-start | bytes 565256 | tf_op jit(solution)/shard_map/ppermute | solution.py:575
  7.9 2.7 %shard_map.105 = (f32[12,64,256]{2,1,0:T(8,128)S(1)}, f32[12,64,256]{2,1,0:T(8,128)S(1)}, f32[12,64,256]{2,1,0:T(8,128)S(1)}, f32[12,64,256]{2,1,0:T(8,128)S(1)}, f32[12,64,256]{2,1,0:T(8,128)S(1)}) custom-call(f32[12,64,256]{2,1,0:T(8,128)} %temp_hbm.3, f32[12,64,256]{2,1,0:T(8,128)} %kappa_hbm.3, f32[12,64,256]{2,1,0:T(8,128)} %slope_hbm.3, ...), custom_call_target="tpu_custom_call" | custom-call | flops 5898240 | bytes 7077888 | tf_op jit(solution)/shard_map/pallas_call | solution.py:536
  10.6 0.0 collective-permute-done.1.step_ref
  10.6 0.0 collective-permute-done.cross_ref
  10.6 0.7 %collective-permute-start.3 = (f32[136,256]{1,0:T(8,128)S(1)}, f32[136,256]{1,0:T(8,128)S(1)}, u32[]{:S(2)}, u32[]{:S(2)}) collective-permute-start(f32[136,256]{1,0:T(8,128)S(1)} %collective-permute-done.cross_ref), channel_id=1, source_target_pairs={{0,8},{8,0},{16,24},{24,16},{1,9},{9,1},{17,25},{25,17},{2,10},{10... | collective-permute-start | bytes 417800 | tf_op jit(solution)/shard_map/ppermute | solution.py:585
  11.3 0.0 collective-permute-done.2.core_ref
  11.3 1.0 %collective-permute-done.3.relay_ref = f32[136,256]{1,0:T(8,128)S(1)} collective-permute-done((f32[136,256]{1,0:T(8,128)S(1)}, f32[136,256]{1,0:T(8,128)S(1)}, u32[]{:S(2)}, u32[]{:S(2)}) %collective-permute-start.3) | collective-permute-done | bytes 139296 | tf_op jit(solution)/shard_map/ppermute | solution.py:585
  12.3 1.3 %shard_map.106 = (f32[12,64,256]{2,1,0:T(8,128)S(1)}, f32[96,256]{1,0:T(8,128)S(1)}, f32[24,768]{1,0:T(8,128)S(1)}, f32[24,768]{1,0:T(8,128)S(1)}, f32[128,256]{1,0:T(8,128)S(1)}, /*index=5*/f32[8,256]{1,0:T(8,128)S(1)}) custom-call(f32[12,64,256]{2,1,0:T(8,128)S(1)} %get-tuple-element.30.first_ref, f32[12,64,256]{2,1,0:T(8,128)S(1)} %get-tuple-element.31.temp_ref, ...), custom_call_target="tpu_custom_call" | custom-call | tf_op jit(solution)/shard_map/pallas_call | solution.py:536
  13.6 1.6 %collective-permute-start.4 = (f32[24,768]{1,0:T(8,128)S(1)}, f32[24,768]{1,0:T(8,128)S(1)}, u32[]{:S(2)}, u32[]{:S(2)}) collective-permute-start(f32[24,768]{1,0:T(8,128)S(1)} %get-tuple-element.40.sa_ref), channel_id=1, source_target_pairs={{0,1},{1,0},{2,3},{3,2},{4,5},{5,4},{6,7},{7,6},{8,9},{9,8},{10,11... | collective-permute-start | bytes 221192 | tf_op jit(solution)/shard_map/ppermute | solution.py:595
  15.2 3.5 %collective-permute-start.5 = (f32[24,768]{1,0:T(8,128)S(1)}, f32[24,768]{1,0:T(8,128)S(1)}, u32[]{:S(2)}, u32[]{:S(2)}) collective-permute-start(f32[24,768]{1,0:T(8,128)S(1)} %get-tuple-element.41.sb_ref), channel_id=1, source_target_pairs={{1,2},{2,1},{3,4},{4,3},{5,6},{6,5},{7,0},{0,7},{9,10},{10,9},{11,... | collective-permute-start | bytes 221192 | tf_op jit(solution)/shard_map/ppermute | solution.py:596
  18.7 0.3 %shard_map.107 = (f32[64,256]{1,0:T(8,128)S(1)}, f32[64,256]{1,0:T(8,128)S(1)}) custom-call(f32[128,256]{1,0:T(8,128)S(1)} %get-tuple-element.42.fw_ref, f32[12,64,256]{2,1,0:T(8,128)S(1)} %get-tuple-element.31.temp_ref, f32[12,64,256]{2,1,0:T(8,128)S(1)} %get-tuple-element.37.after_ref.temp_ref, f32[8,256]{1,0:T(8,128)S(1)} %get-tuple-element.43.crow_ref, ...), custom_call_target="tpu_custom_call" | custom-call | tf_op jit(solution)/shard_map/pallas_call | solution.py:536
  19.0 1.6 %collective-permute-start.8 = (f32[64,256]{1,0:T(8,128)S(1)}, f32[64,256]{1,0:T(8,128)S(1)}, u32[]{:S(2)}, u32[]{:S(2)}) collective-permute-start(f32[64,256]{1,0:T(8,128)S(1)} %get-tuple-element.48.own_ref), channel_id=1, source_target_pairs={{0,16},{8,24},{16,0},{24,8},{1,17},{9,25},{17,1},{25,9},{2,18},{10... | collective-permute-start | bytes 196616 | tf_op jit(solution)/shard_map/ppermute | solution.py:601
  20.6 0.0 collective-permute-start.7
  20.6 0.6 %collective-permute-start.6 = (f32[64,256]{1,0:T(8,128)S(1)}, f32[64,256]{1,0:T(8,128)S(1)}, u32[]{:S(2)}, u32[]{:S(2)}) collective-permute-start(f32[64,256]{1,0:T(8,128)S(1)} %get-tuple-element.48.own_ref), channel_id=1, source_target_pairs={{0,8},{8,0},{16,24},{24,16},{1,9},{9,1},{17,25},{25,17},{2,10},{10... | collective-permute-start | bytes 196616 | tf_op jit(solution)/shard_map/ppermute | solution.py:602
  21.2 0.0 collective-permute-done.4.ra_ref
  21.2 1.0 %collective-permute-done.5.rb_ref = f32[24,768]{1,0:T(8,128)S(1)} collective-permute-done((f32[24,768]{1,0:T(8,128)S(1)}, f32[24,768]{1,0:T(8,128)S(1)}, u32[]{:S(2)}, u32[]{:S(2)}) %collective-permute-start.5) | collective-permute-done | bytes 73760 | tf_op jit(solution)/shard_map/ppermute | solution.py:596
  22.2 2.4 %shard_map.108 = (f32[12,64,256]{2,1,0:T(8,128)}, f32[4,64,256]{2,1,0:T(8,128)S(1)}, f32[128,128]{1,0:T(8,128)S(1)}) custom-call(f32[12,64,256]{2,1,0:T(8,128)S(1)} %get-tuple-element.37.after_ref.temp_ref, f32[12,64,256]{2,1,0:T(8,128)S(1)} %get-tuple-element.32.kappa_ref, f32[12,64,256]{2,1,0:T(8,128)S(1)} %get-tuple-element.33.slope_ref, ...), custom_call_target="tpu_custom_call" | custom-call | flops 5898240 | bytes 7077888 | tf_op jit(solution)/shard_map/pallas_call | solution.py:536
  24.7 0.0 collective-permute-done.8.relay_ref
  24.7 0.1 collective-permute-done.7.cross_ref
  24.8 0.0 collective-permute-done.6.core_ref
  24.8 0.9 %shard_map.109 = (f32[12,64,256]{2,1,0:T(8,128)}, f32[64,256]{1,0:T(8,128)}) custom-call(f32[12,64,256]{2,1,0:T(8,128)} %get-tuple-element.46.part_hbm, f32[4,64,256]{2,1,0:T(8,128)S(1)} %get-tuple-element.47.tail_ref, f32[64,256]{1,0:T(8,128)S(1)} %get-tuple-element.48.own_ref, ...), custom_call_target="tpu_custom_call", output_to_operand_aliasing={{0}: (0, {})} | custom-call | tf_op jit(solution)/shard_map/pallas_call | solution.py:536
Async XLA Ops:
  2.7 7.8 %collective-permute-start = (f32[136,256]{1,0:T(8,128)S(1)}, f32[136,256]{1,0:T(8,128)S(1)}, u32[]{:S(2)}, u32[]{:S(2)}) collective-permute-start(f32[136,256]{1,0:T(8,128)S(1)} %get-tuple-element.26), channel_id=1, source_target_pairs={{0,24},{8,16},{16,8},{24,0},{1,25},{9,17},{17,9},{25,1},{2,26},{10... | collective-permute-start | bytes 417800 | tf_op jit(solution)/shard_map/ppermute | solution.py:573
  5.2 5.4 %collective-permute-start.1 = (f32[48,256]{1,0:T(8,128)S(1)}, f32[48,256]{1,0:T(8,128)S(1)}, u32[]{:S(2)}, u32[]{:S(2)}) collective-permute-start(f32[48,256]{1,0:T(8,128)S(1)} %get-tuple-element.27), channel_id=1, source_target_pairs={{8,16},{16,8},{9,17},{17,9},{10,18},{18,10},{11,19},{19,11},{12,20... | collective-permute-start | bytes 147464 | tf_op jit(solution)/shard_map/ppermute | solution.py:574
  5.8 5.4 %collective-permute-start.2 = (f32[184,256]{1,0:T(8,128)S(1)}, f32[184,256]{1,0:T(8,128)S(1)}, u32[]{:S(2)}, u32[]{:S(2)}) collective-permute-start(f32[184,256]{1,0:T(8,128)S(1)} %get-tuple-element.34.own_ref), channel_id=1, source_target_pairs={{0,8},{8,0},{16,24},{24,16},{1,9},{9,1},{17,25},{25,17},{2,10},{10... | collective-permute-start | bytes 565256 | tf_op jit(solution)/shard_map/ppermute | solution.py:575
  10.6 1.7 %collective-permute-start.3 = (f32[136,256]{1,0:T(8,128)S(1)}, f32[136,256]{1,0:T(8,128)S(1)}, u32[]{:S(2)}, u32[]{:S(2)}) collective-permute-start(f32[136,256]{1,0:T(8,128)S(1)} %collective-permute-done.cross_ref), channel_id=1, source_target_pairs={{0,8},{8,0},{16,24},{24,16},{1,9},{9,1},{17,25},{25,17},{2,10},{10... | collective-permute-start | bytes 417800 | tf_op jit(solution)/shard_map/ppermute | solution.py:585
  13.6 7.7 %collective-permute-start.4 = (f32[24,768]{1,0:T(8,128)S(1)}, f32[24,768]{1,0:T(8,128)S(1)}, u32[]{:S(2)}, u32[]{:S(2)}) collective-permute-start(f32[24,768]{1,0:T(8,128)S(1)} %get-tuple-element.40.sa_ref), channel_id=1, source_target_pairs={{0,1},{1,0},{2,3},{3,2},{4,5},{5,4},{6,7},{7,6},{8,9},{9,8},{10,11... | collective-permute-start | bytes 221192 | tf_op jit(solution)/shard_map/ppermute | solution.py:595
  15.2 7.0 %collective-permute-start.5 = (f32[24,768]{1,0:T(8,128)S(1)}, f32[24,768]{1,0:T(8,128)S(1)}, u32[]{:S(2)}, u32[]{:S(2)}) collective-permute-start(f32[24,768]{1,0:T(8,128)S(1)} %get-tuple-element.41.sb_ref), channel_id=1, source_target_pairs={{1,2},{2,1},{3,4},{4,3},{5,6},{6,5},{7,0},{0,7},{9,10},{10,9},{11,... | collective-permute-start | bytes 221192 | tf_op jit(solution)/shard_map/ppermute | solution.py:596
  19.0 5.6 %collective-permute-start.8 = (f32[64,256]{1,0:T(8,128)S(1)}, f32[64,256]{1,0:T(8,128)S(1)}, u32[]{:S(2)}, u32[]{:S(2)}) collective-permute-start(f32[64,256]{1,0:T(8,128)S(1)} %get-tuple-element.48.own_ref), channel_id=1, source_target_pairs={{0,16},{8,24},{16,0},{24,8},{1,17},{9,25},{17,1},{25,9},{2,18},{10... | collective-permute-start | bytes 196616 | tf_op jit(solution)/shard_map/ppermute | solution.py:601
  20.6 4.2 %collective-permute-start.7 = (f32[64,256]{1,0:T(8,128)S(1)}, f32[64,256]{1,0:T(8,128)S(1)}, u32[]{:S(2)}, u32[]{:S(2)}) collective-permute-start(f32[64,256]{1,0:T(8,128)S(1)} %get-tuple-element.48.own_ref), channel_id=1, source_target_pairs={{0,24},{8,16},{16,8},{24,0},{1,25},{9,17},{17,9},{25,1},{2,26},{10... | collective-permute-start | bytes 196616 | tf_op jit(solution)/shard_map/ppermute | solution.py:600
  20.6 4.2 %collective-permute-start.6 = (f32[64,256]{1,0:T(8,128)S(1)}, f32[64,256]{1,0:T(8,128)S(1)}, u32[]{:S(2)}, u32[]{:S(2)}) collective-permute-start(f32[64,256]{1,0:T(8,128)S(1)} %get-tuple-element.48.own_ref), channel_id=1, source_target_pairs={{0,8},{8,0},{16,24},{24,16},{1,9},{9,1},{17,25},{25,17},{2,10},{10... | collective-permute-start | bytes 196616 | tf_op jit(solution)/shard_map/ppermute | solution.py:602

commit v5 on v4

--- a/solution.py
+++ b/solution.py
@@ -173,15 +173,13 @@
 
 
 def edge_kernel(
-    first_ref, temp_ref, kappa_ref, slope_ref, own_ref, core_ref, cross_ref, relay_ref, step_ref, map_ref,
-    next_ref, yo_ref, sa_ref, sb_ref, fw_ref, crow_ref, strip_ref, small_ref, all_ref,
+    first_ref, temp_ref, kappa_ref, slope_ref, core_ref, step_ref,
+    next_ref, yo_ref, line_ref, strip_ref, small_ref,
 ):
     layers, rows, cols = temp_ref.shape
     span = 2 * rows + 8
-    groups = lax.axis_size("grp")
-    group = lax.axis_index("grp")
+    group, groups = lax.axis_index("grp"), lax.axis_size("grp")
     even = lax.rem(group, 2) == 0
-    place_even = lax.rem(lax.axis_index("loop"), 2) == 0
     ya, yb = core_ref[span : span + 4 * layers, :], step_ref[...]
     low, high = jnp.where(even, yb, ya), jnp.where(even, ya, yb)
     yo_ref[0 : 4 * layers, :] = low
@@ -189,6 +187,64 @@
     low_open = jnp.where(group == 0, 0.0, 1.0)
     high_open = jnp.where(group == groups - 1, 0.0, 1.0)
 
+    row = lax.broadcasted_iota(jnp.int32, (rows, cols), 0)
+    lane = lax.broadcasted_iota(jnp.int32, (rows, TILE), 1)
+    small_ref[...] = jnp.zeros_like(small_ref)
+    lane1 = lax.broadcasted_iota(jnp.int32, (1, TILE), 1)
+    for z in range(layers):
+        temp, kappa, slope = temp_ref[z], kappa_ref[z], slope_ref[z]
+        after = first_ref[z]
+        edges = []
+        for side, base, at, opened in ((0, 0, 0, low_open), (1, 4 * layers, rows - 1, high_open)):
+            temp_h = yo_ref[base + layers + z : base + layers + z + 1, :]
+            cond_h = conduct(
+                yo_ref[base + 2 * layers + z : base + 2 * layers + z + 1, :],
+                yo_ref[base + 3 * layers + z : base + 3 * layers + z + 1, :],
+                temp_h,
+            )
+            temp_e = temp[at : at + 1]
+            cond_e = conduct(kappa[at : at + 1], slope[at : at + 1], temp_e)
+            flux = opened * face(cond_e, cond_h, temp_e, temp_h)
+            halo = yo_ref[base + z : base + z + 1, :] - flux
+            yo_ref[base + z : base + z + 1, :] = halo
+            edges.append(flux)
+            corner = jnp.where(
+                lane1 == 0,
+                temp_h[:, 0:TILE],
+                jnp.where(
+                    lane1 == 1,
+                    pltpu.roll(cond_h[:, 0:TILE], 1, 1),
+                    jnp.where(
+                        lane1 == 4,
+                        pltpu.roll(temp_h[:, cols - TILE :], 5, 1),
+                        pltpu.roll(cond_h[:, cols - TILE :], 6, 1),
+                    ),
+                ),
+            )
+            small_ref[16 * side + z : 16 * side + z + 1, :] = corner
+        after = after + jnp.where(row == 0, edges[0], jnp.where(row == rows - 1, edges[1], 0.0))
+        next_ref[z] = after
+        packed = None
+        for n, value in enumerate((after, temp, kappa, slope)):
+            left = value[:, 0:TILE]
+            right = pltpu.roll(value[:, cols - TILE :], n + 5, 1)
+            left = pltpu.roll(left, n, 1) if n else left
+            packed = left if packed is None else jnp.where(lane == n, left, packed)
+            packed = jnp.where(lane == n + 4, right, packed)
+        strip_ref[z * rows : (z + 1) * rows, :] = packed
+    line_ref[0:8, :] = strip_ref[...].T[0:8, :]
+    line_ref[8:16, 0:TILE] = small_ref[...].T[0:8, :]
+
+
+def select_kernel(
+    old_ref, halo_ref, line_ref, temp_ref, own_ref, core_ref, cross_ref, relay_ref, map_ref,
+    top_ref, yo_ref, sa_ref, sb_ref, fw_ref, crow_ref, all_ref, tmp_ref,
+):
+    rows, cols = old_ref.shape[1:]
+    layers = temp_ref.shape[0]
+    span = 2 * rows + 8
+    group, groups = lax.axis_index("grp"), lax.axis_size("grp")
+    place_even = lax.rem(lax.axis_index("loop"), 2) == 0
     beside = group + 1 - 2 * lax.rem(group, 2)
     extra = jnp.zeros((8, cols), F32)
     for ref, owner in (
@@ -206,65 +262,16 @@
     fw_ref[0:rows, :] = flow
     fw_ref[rows:, :] = wall
     sink = wall * (temp_ref[0] - flow)
-    temp_low, temp_high = yo_ref[layers : layers + 1, :], yo_ref[5 * layers : 5 * layers + 1, :]
-    sink_low = wall_y[7:8] * (temp_low - flow_y[7:8])
-    sink_high = wall_y[8 + rows : 9 + rows] * (temp_high - flow_y[8 + rows : 9 + rows])
-
-    row = lax.broadcasted_iota(jnp.int32, (rows, cols), 0)
+    for base, at in ((0, 7), (4 * layers, 8 + rows)):
+        temp = halo_ref[base + layers : base + layers + 1, :]
+        heat = wall_y[at : at + 1] * (temp - flow_y[at : at + 1])
+        yo_ref[base : base + 8, :] = halo_ref[base : base + 8, :]
+        yo_ref[base : base + 1, :] = halo_ref[base : base + 1, :] - time_step * heat
+    top_ref[0] = old_ref[0] - time_step * sink
     lane = lax.broadcasted_iota(jnp.int32, (rows, TILE), 1)
-    small_ref[...] = jnp.zeros_like(small_ref)
-    lane1 = lax.broadcasted_iota(jnp.int32, (1, TILE), 1)
-    for z in range(layers):
-        temp, kappa, slope = temp_ref[z], kappa_ref[z], slope_ref[z]
-        after = first_ref[z]
-        edges = []
-        for side, base, at, opened, sunk in (
-            (0, 0, 0, low_open, sink_low),
-            (1, 4 * layers, rows - 1, high_open, sink_high),
-        ):
-            temp_h = yo_ref[base + layers + z : base + layers + z + 1, :]
-            cond_h = conduct(
-                yo_ref[base + 2 * layers + z : base + 2 * layers + z + 1, :],
-                yo_ref[base + 3 * layers + z : base + 3 * layers + z + 1, :],
-                temp_h,
-            )
-            temp_e = temp[at : at + 1]
-            cond_e = conduct(kappa[at : at + 1], slope[at : at + 1], temp_e)
-            flux = opened * face(cond_e, cond_h, temp_e, temp_h)
-            halo = yo_ref[base + z : base + z + 1, :] - flux
-            if z == 0:
-                halo = halo - time_step * sunk
-            yo_ref[base + z : base + z + 1, :] = halo
-            edges.append(flux)
-            corner = jnp.where(
-                lane1 == 0,
-                temp_h[:, 0:TILE],
-                jnp.where(
-                    lane1 == 1,
-                    pltpu.roll(cond_h[:, 0:TILE], 1, 1),
-                    jnp.where(
-                        lane1 == 4,
-                        pltpu.roll(temp_h[:, cols - TILE :], 5, 1),
-                        pltpu.roll(cond_h[:, cols - TILE :], 6, 1),
-                    ),
-                ),
-            )
-            small_ref[16 * side + z : 16 * side + z + 1, :] = corner
-        after = after + jnp.where(row == 0, edges[0], jnp.where(row == rows - 1, edges[1], 0.0))
-        if z == 0:
-            after = after - time_step * sink
-        next_ref[z] = after
-        packed = None
-        for n, value in enumerate((after, temp, kappa, slope)):
-            left = value[:, 0:TILE]
-            right = pltpu.roll(value[:, cols - TILE :], n + 5, 1)
-            left = pltpu.roll(left, n, 1) if n else left
-            packed = left if packed is None else jnp.where(lane == n, left, packed)
-            packed = jnp.where(lane == n + 4, right, packed)
-        strip_ref[z * rows : (z + 1) * rows, :] = packed
-    strips = strip_ref[...].T[0:8, :]
-    corners = small_ref[...].T[0:8, :]
-
+    tmp_ref[...] = jnp.zeros_like(tmp_ref)
+    tmp_ref[0:rows, :] = jnp.where(lane == 0, sink[:, 0:TILE], pltpu.roll(sink[:, cols - TILE :], 2, 1))
+    sunk = tmp_ref[...].T[0:8, :]
     lane_c = lax.broadcasted_iota(jnp.int32, (groups * rows, TILE), 1)
     right_flow = flow_all[:, cols - TILE :]
     pack = jnp.where(lane_c < 2, flow_all[:, 0:TILE], pltpu.roll(right_flow, 4, 1))
@@ -289,8 +296,11 @@
     channels = groups * rows
     for ref, pick_right in ((sa_ref, place_even), (sb_ref, jnp.logical_not(place_even))):
         ref[...] = jnp.zeros_like(ref)
-        ref[0:4, :] = jnp.where(pick_right, strips[4:8], strips[0:4])
-        ref[4:6, 0:TILE] = jnp.where(pick_right, corners[4:6], corners[0:2])
+        ref[0:4, :] = jnp.where(pick_right, line_ref[4:8, :], line_ref[0:4, :])
+        ref[0:1, 0:rows] = ref[0:1, 0:rows] - time_step * jnp.where(
+            pick_right, sunk[1:2, 0:rows], sunk[0:1, 0:rows]
+        )
+        ref[4:6, 0:TILE] = jnp.where(pick_right, line_ref[12:14, 0:TILE], line_ref[8:10, 0:TILE])
         ref[4:5, channels : 2 * channels] = jnp.where(pick_right, extra[1:2], extra[0:1])
         ref[5:6, channels : 2 * channels] = jnp.where(pick_right, extra[4:5], extra[3:4])
         ref[6:7, 0:channels] = jnp.where(pick_right, flow_e, flow_0)
@@ -583,14 +593,22 @@
     )
     got_cross, got_step, first = lax.optimization_barrier((got_cross, got_step, first))
     relay = lax.ppermute(got_cross, "grp", beside)
+    after, yo, line = call(
+        edge_kernel,
+        (block, shape(8 * layers, cols), shape(16, strip)),
+        [vmem(strip, TILE), vmem(TILE, TILE)],
+        first, temp, kappa, slope, got_core, got_step,
+        cost=heavy,
+    )
     after, yo, sa, sb, fw, crow = call(
-        edge_kernel,
+        select_kernel,
         (
             block, shape(8 * layers, cols), shape(24, strip), shape(24, strip),
             shape(2 * rows, cols), shape(8, channels),
         ),
-        [vmem(strip, TILE), vmem(TILE, TILE), vmem(channels, 2 * cols)],
-        first, temp, kappa, slope, core, got_core, got_cross, relay, got_step, map_row,
+        [vmem(channels, 2 * cols), vmem(TILE, TILE)],
+        after, yo, line, temp, core, got_core, got_cross, relay, map_row,
+        alias={0: 0, 1: 1},
     )
     ra = lax.ppermute(sa, "loop", pairs(places, 0, True))
     rb = lax.ppermute(sb, "loop", pairs(places, 1, True))

time: 25.8 us -> 25.1 us (0.973)
  waiting for transfers between devices: 2.07 us -> 1.08 us
    ppermute x1, starting transfers between devices: 0.67 us -> 2.01 us  [shards(): relay = lax.ppermute(got_cross, 'grp', beside)]
    ppermute x1, starting transfers between devices: 2.01 us -> 0.68 us  [shards(): got_core = lax.ppermute(core, 'grp', beside)]
    ppermute x1, waiting for transfers between devices: 0.99 us -> 0.01 us  [shards(): relay = lax.ppermute(got_cross, 'grp', beside)]
    pallas_call x6 -> x7, Pallas kernels: 9.74 us -> 9.98 us  [call(): pl.pallas_call(body, out_shape=outs, in_specs=[pl.BlockSpec(memory_space=...]
  transfers between devices with their start and end apart: 9 -> 9, of which waited for: 3 -> 2; matrix products, arithmetic and copies ran while one was open for 0% -> 0% of each run, Pallas kernels for 21% -> 26%
where the time goes in v5:
time: 25.1 us; the launch traced here: 24.9 us
  starting transfers between devices  13.1 us (52%)
  Pallas kernels  9.98 us (40%)
  waiting for transfers between devices  1.08 us (4%)
  between operations  0.71 us (3%)
    pallas_call x7, Pallas kernels, call(): pl.pallas_call(body, out_shape=outs, in_specs=[pl.BlockSpec(memory_space=...  9.98 us
    ppermute x1, starting transfers between devices, shards(): rb = lax.ppermute(sb, 'loop', pairs(places, 1, True))  3.54 us
    ppermute x1, starting transfers between devices, shards(): got_cross = lax.ppermute(cross, 'grp', across)  2.44 us
    ppermute x1, starting transfers between devices, shards(): relay = lax.ppermute(got_cross, 'grp', beside)  2.01 us
    ppermute x1, starting transfers between devices, shards(): ra = lax.ppermute(sa, 'loop', pairs(places, 0, True))  1.59 us
    ppermute x1, starting transfers between devices, shards(): lax.ppermute(flow, 'grp', [(i, (i + groups // 2) % groups) for i in range...  1.39 us
    ppermute x1, waiting for transfers between devices, shards(): rb = lax.ppermute(sb, 'loop', pairs(places, 1, True))  0.98 us
    ppermute x1, starting transfers between devices, shards(): got_beside = lax.ppermute(flow, 'grp', beside)  0.81 us
  transfers between devices with their start and end apart: 9, of which 2 were waited for; matrix products, arithmetic and copies ran while one was open for 0% of the time, Pallas kernels for 26%

profile of v5, /device:TPU:0, one launch (start us, length us, event | category | flops | bytes accessed | tf_op | source)
XLA Modules:
  0.0 24.9 jit_solution(5251095244496561632)
XLA Ops:
  0.6 2.1 %shard_map.104 = (f32[184,256]{1,0:T(8,128)S(1)}, f32[136,256]{1,0:T(8,128)S(1)}, f32[48,256]{1,0:T(8,128)S(1)}, s32[1,256]{1,0:T(1,128)S(1)}, s32[1,256]{1,0:T(1,128)S(1)}) custom-call(f32[12,64,256]{2,1,0:T(8,128)} %temp_hbm.3, f32[12,64,256]{2,1,0:T(8,128)} %kappa_hbm.3, f32[12,64,256]{2,1,0:T(8,128)} %slope_hbm.3, f32[12,64,256]{2,1,0:T(8,128)} %power_hbm.3, ...), custom_call_target="tpu_custom_call" | custom-call | tf_op jit(solution)/shard_map/pallas_call | solution.py:546
  2.7 2.4 %collective-permute-start = (f32[136,256]{1,0:T(8,128)S(1)}, f32[136,256]{1,0:T(8,128)S(1)}, u32[]{:S(2)}, u32[]{:S(2)}) collective-permute-start(f32[136,256]{1,0:T(8,128)S(1)} %get-tuple-element.29), channel_id=1, source_target_pairs={{0,24},{8,16},{16,8},{24,0},{1,25},{9,17},{17,9},{25,1},{2,26},{10... | collective-permute-start | bytes 417800 | tf_op jit(solution)/shard_map/ppermute | solution.py:583
  5.2 0.7 %collective-permute-start.2 = (f32[184,256]{1,0:T(8,128)S(1)}, f32[184,256]{1,0:T(8,128)S(1)}, u32[]{:S(2)}, u32[]{:S(2)}) collective-permute-start(f32[184,256]{1,0:T(8,128)S(1)} %get-tuple-element.37.own_ref), channel_id=1, source_target_pairs={{0,8},{8,0},{16,24},{24,16},{1,9},{9,1},{17,25},{25,17},{2,10},{10... | collective-permute-start | bytes 565256 | tf_op jit(solution)/shard_map/ppermute | solution.py:585
  5.9 0.7 %collective-permute-start.1 = (f32[48,256]{1,0:T(8,128)S(1)}, f32[48,256]{1,0:T(8,128)S(1)}, u32[]{:S(2)}, u32[]{:S(2)}) collective-permute-start(f32[48,256]{1,0:T(8,128)S(1)} %get-tuple-element.30), channel_id=1, source_target_pairs={{8,16},{16,8},{9,17},{17,9},{10,18},{18,10},{11,19},{19,11},{12,20... | collective-permute-start | bytes 147464 | tf_op jit(solution)/shard_map/ppermute | solution.py:584
  6.5 2.7 %shard_map.105 = (f32[12,64,256]{2,1,0:T(8,128)S(1)}, f32[12,64,256]{2,1,0:T(8,128)S(1)}, f32[12,64,256]{2,1,0:T(8,128)S(1)}, f32[12,64,256]{2,1,0:T(8,128)S(1)}, f32[12,64,256]{2,1,0:T(8,128)S(1)}) custom-call(f32[12,64,256]{2,1,0:T(8,128)} %temp_hbm.3, f32[12,64,256]{2,1,0:T(8,128)} %kappa_hbm.3, f32[12,64,256]{2,1,0:T(8,128)} %slope_hbm.3, ...), custom_call_target="tpu_custom_call" | custom-call | flops 5898240 | bytes 7077888 | tf_op jit(solution)/shard_map/pallas_call | solution.py:546
  9.2 0.0 collective-permute-done.1.step_ref
  9.3 0.0 collective-permute-done.cross_ref
  9.3 2.0 %collective-permute-start.3 = (f32[136,256]{1,0:T(8,128)S(1)}, f32[136,256]{1,0:T(8,128)S(1)}, u32[]{:S(2)}, u32[]{:S(2)}) collective-permute-start(f32[136,256]{1,0:T(8,128)S(1)} %collective-permute-done.cross_ref), channel_id=1, source_target_pairs={{0,8},{8,0},{16,24},{24,16},{1,9},{9,1},{17,25},{25,17},{2,10},{10... | collective-permute-start | bytes 417800 | tf_op jit(solution)/shard_map/ppermute | solution.py:595
  11.3 0.0 collective-permute-done.2.core_ref
  11.3 1.0 %shard_map.106 = (f32[12,64,256]{2,1,0:T(8,128)S(1)}, f32[96,256]{1,0:T(8,128)S(1)}, f32[16,768]{1,0:T(8,128)S(1)}) custom-call(f32[12,64,256]{2,1,0:T(8,128)S(1)} %get-tuple-element.33.first_ref, f32[12,64,256]{2,1,0:T(8,128)S(1)} %get-tuple-element.34.temp_ref, f32[12,64,256]{2,1,0:T(8,128)S(1)} %get-tuple-element.35.kappa_ref, ...), custom_call_target="tpu_custom_call" | custom-call | flops 5898240 | bytes 7077888 | tf_op jit(solution)/shard_map/pallas_call | solution.py:546
  12.3 0.0 collective-permute-done.3.relay_ref
  12.3 0.6 %shard_map.107 = (f32[12,64,256]{2,1,0:T(8,128)S(1)}, f32[96,256]{1,0:T(8,128)S(1)}, f32[24,768]{1,0:T(8,128)S(1)}, f32[24,768]{1,0:T(8,128)S(1)}, f32[128,256]{1,0:T(8,128)S(1)}, /*index=5*/f32[8,256]{1,0:T(8,128)S(1)}) custom-call(f32[12,64,256]{2,1,0:T(8,128)S(1)} %get-tuple-element.39.old_ref, ...), custom_call_target="tpu_custom_call", output_to_operand_aliasing={{0}: (0, {}), {1}: (1, {})} | custom-call | tf_op jit(solution)/shard_map/pallas_call | solution.py:546
  12.8 1.6 %collective-permute-start.4 = (f32[24,768]{1,0:T(8,128)S(1)}, f32[24,768]{1,0:T(8,128)S(1)}, u32[]{:S(2)}, u32[]{:S(2)}) collective-permute-start(f32[24,768]{1,0:T(8,128)S(1)} %get-tuple-element.46.sa_ref), channel_id=1, source_target_pairs={{0,1},{1,0},{2,3},{3,2},{4,5},{5,4},{6,7},{7,6},{8,9},{9,8},{10,11... | collective-permute-start | bytes 221192 | tf_op jit(solution)/shard_map/ppermute | solution.py:613
  14.4 3.5 %collective-permute-start.5 = (f32[24,768]{1,0:T(8,128)S(1)}, f32[24,768]{1,0:T(8,128)S(1)}, u32[]{:S(2)}, u32[]{:S(2)}) collective-permute-start(f32[24,768]{1,0:T(8,128)S(1)} %get-tuple-element.47.sb_ref), channel_id=1, source_target_pairs={{1,2},{2,1},{3,4},{4,3},{5,6},{6,5},{7,0},{0,7},{9,10},{10,9},{11,... | collective-permute-start | bytes 221192 | tf_op jit(solution)/shard_map/ppermute | solution.py:614
  18.0 0.3 %shard_map.108 = (f32[64,256]{1,0:T(8,128)S(1)}, f32[64,256]{1,0:T(8,128)S(1)}) custom-call(f32[128,256]{1,0:T(8,128)S(1)} %get-tuple-element.48.fw_ref, f32[12,64,256]{2,1,0:T(8,128)S(1)} %get-tuple-element.34.temp_ref, f32[12,64,256]{2,1,0:T(8,128)S(1)} %get-tuple-element.43.after_ref.temp_ref, f32[8,256]{1,0:T(8,128)S(1)} %get-tuple-element.49.crow_ref, ...), custom_call_target="tpu_custom_call" | custom-call | tf_op jit(solution)/shard_map/pallas_call | solution.py:546
  18.3 1.4 %collective-permute-start.8 = (f32[64,256]{1,0:T(8,128)S(1)}, f32[64,256]{1,0:T(8,128)S(1)}, u32[]{:S(2)}, u32[]{:S(2)}) collective-permute-start(f32[64,256]{1,0:T(8,128)S(1)} %get-tuple-element.54.own_ref), channel_id=1, source_target_pairs={{0,16},{8,24},{16,0},{24,8},{1,17},{9,25},{17,1},{25,9},{2,18},{10... | collective-permute-start | bytes 196616 | tf_op jit(solution)/shard_map/ppermute | solution.py:619
  19.7 0.0 collective-permute-start.7
  19.7 0.8 %collective-permute-start.6 = (f32[64,256]{1,0:T(8,128)S(1)}, f32[64,256]{1,0:T(8,128)S(1)}, u32[]{:S(2)}, u32[]{:S(2)}) collective-permute-start(f32[64,256]{1,0:T(8,128)S(1)} %get-tuple-element.54.own_ref), channel_id=1, source_target_pairs={{0,8},{8,0},{16,24},{24,16},{1,9},{9,1},{17,25},{25,17},{2,10},{10... | collective-permute-start | bytes 196616 | tf_op jit(solution)/shard_map/ppermute | solution.py:620
  20.5 0.0 collective-permute-done.4.ra_ref
  20.5 1.0 %collective-permute-done.5.rb_ref = f32[24,768]{1,0:T(8,128)S(1)} collective-permute-done((f32[24,768]{1,0:T(8,128)S(1)}, f32[24,768]{1,0:T(8,128)S(1)}, u32[]{:S(2)}, u32[]{:S(2)}) %collective-permute-start.5) | collective-permute-done | bytes 73760 | tf_op jit(solution)/shard_map/ppermute | solution.py:614
  21.5 2.4 %shard_map.109 = (f32[12,64,256]{2,1,0:T(8,128)}, f32[4,64,256]{2,1,0:T(8,128)S(1)}, f32[128,128]{1,0:T(8,128)S(1)}) custom-call(f32[12,64,256]{2,1,0:T(8,128)S(1)} %get-tuple-element.43.after_ref.temp_ref, f32[12,64,256]{2,1,0:T(8,128)S(1)} %get-tuple-element.35.kappa_ref, f32[12,64,256]{2,1,0:T(8,128)S(1)} %get-tuple-element.36.slope_ref, ...), custom_call_target="tpu_custom_call" | custom-call | flops 5898240 | bytes 7077888 | tf_op jit(solution)/shard_map/pallas_call | solution.py:546
  23.9 0.0 collective-permute-done.8.relay_ref
  23.9 0.1 collective-permute-done.7.cross_ref
  24.0 0.0 collective-permute-done.6.core_ref
  24.0 0.9 %shard_map.110 = (f32[12,64,256]{2,1,0:T(8,128)}, f32[64,256]{1,0:T(8,128)}) custom-call(f32[12,64,256]{2,1,0:T(8,128)} %get-tuple-element.52.part_hbm, f32[4,64,256]{2,1,0:T(8,128)S(1)} %get-tuple-element.53.tail_ref, f32[64,256]{1,0:T(8,128)S(1)} %get-tuple-element.54.own_ref, ...), custom_call_target="tpu_custom_call", output_to_operand_aliasing={{0}: (0, {})} | custom-call | tf_op jit(solution)/shard_map/pallas_call | solution.py:546
Async XLA Ops:
  2.7 6.5 %collective-permute-start = (f32[136,256]{1,0:T(8,128)S(1)}, f32[136,256]{1,0:T(8,128)S(1)}, u32[]{:S(2)}, u32[]{:S(2)}) collective-permute-start(f32[136,256]{1,0:T(8,128)S(1)} %get-tuple-element.29), channel_id=1, source_target_pairs={{0,24},{8,16},{16,8},{24,0},{1,25},{9,17},{17,9},{25,1},{2,26},{10... | collective-permute-start | bytes 417800 | tf_op jit(solution)/shard_map/ppermute | solution.py:583
  5.2 6.1 %collective-permute-start.2 = (f32[184,256]{1,0:T(8,128)S(1)}, f32[184,256]{1,0:T(8,128)S(1)}, u32[]{:S(2)}, u32[]{:S(2)}) collective-permute-start(f32[184,256]{1,0:T(8,128)S(1)} %get-tuple-element.37.own_ref), channel_id=1, source_target_pairs={{0,8},{8,0},{16,24},{24,16},{1,9},{9,1},{17,25},{25,17},{2,10},{10... | collective-permute-start | bytes 565256 | tf_op jit(solution)/shard_map/ppermute | solution.py:585
  5.9 3.4 %collective-permute-start.1 = (f32[48,256]{1,0:T(8,128)S(1)}, f32[48,256]{1,0:T(8,128)S(1)}, u32[]{:S(2)}, u32[]{:S(2)}) collective-permute-start(f32[48,256]{1,0:T(8,128)S(1)} %get-tuple-element.30), channel_id=1, source_target_pairs={{8,16},{16,8},{9,17},{17,9},{10,18},{18,10},{11,19},{19,11},{12,20... | collective-permute-start | bytes 147464 | tf_op jit(solution)/shard_map/ppermute | solution.py:584
  9.3 3.0 %collective-permute-start.3 = (f32[136,256]{1,0:T(8,128)S(1)}, f32[136,256]{1,0:T(8,128)S(1)}, u32[]{:S(2)}, u32[]{:S(2)}) collective-permute-start(f32[136,256]{1,0:T(8,128)S(1)} %collective-permute-done.cross_ref), channel_id=1, source_target_pairs={{0,8},{8,0},{16,24},{24,16},{1,9},{9,1},{17,25},{25,17},{2,10},{10... | collective-permute-start | bytes 417800 | tf_op jit(solution)/shard_map/ppermute | solution.py:595
  12.8 7.7 %collective-permute-start.4 = (f32[24,768]{1,0:T(8,128)S(1)}, f32[24,768]{1,0:T(8,128)S(1)}, u32[]{:S(2)}, u32[]{:S(2)}) collective-permute-start(f32[24,768]{1,0:T(8,128)S(1)} %get-tuple-element.46.sa_ref), channel_id=1, source_target_pairs={{0,1},{1,0},{2,3},{3,2},{4,5},{5,4},{6,7},{7,6},{8,9},{9,8},{10,11... | collective-permute-start | bytes 221192 | tf_op jit(solution)/shard_map/ppermute | solution.py:613
  14.4 7.0 %collective-permute-start.5 = (f32[24,768]{1,0:T(8,128)S(1)}, f32[24,768]{1,0:T(8,128)S(1)}, u32[]{:S(2)}, u32[]{:S(2)}) collective-permute-start(f32[24,768]{1,0:T(8,128)S(1)} %get-tuple-element.47.sb_ref), channel_id=1, source_target_pairs={{1,2},{2,1},{3,4},{4,3},{5,6},{6,5},{7,0},{0,7},{9,10},{10,9},{11,... | collective-permute-start | bytes 221192 | tf_op jit(solution)/shard_map/ppermute | solution.py:614
  18.3 5.6 %collective-permute-start.8 = (f32[64,256]{1,0:T(8,128)S(1)}, f32[64,256]{1,0:T(8,128)S(1)}, u32[]{:S(2)}, u32[]{:S(2)}) collective-permute-start(f32[64,256]{1,0:T(8,128)S(1)} %get-tuple-element.54.own_ref), channel_id=1, source_target_pairs={{0,16},{8,24},{16,0},{24,8},{1,17},{9,25},{17,1},{25,9},{2,18},{10... | collective-permute-start | bytes 196616 | tf_op jit(solution)/shard_map/ppermute | solution.py:619
  19.7 4.3 %collective-permute-start.7 = (f32[64,256]{1,0:T(8,128)S(1)}, f32[64,256]{1,0:T(8,128)S(1)}, u32[]{:S(2)}, u32[]{:S(2)}) collective-permute-start(f32[64,256]{1,0:T(8,128)S(1)} %get-tuple-element.54.own_ref), channel_id=1, source_target_pairs={{0,24},{8,16},{16,8},{24,0},{1,25},{9,17},{17,9},{25,1},{2,26},{10... | collective-permute-start | bytes 196616 | tf_op jit(solution)/shard_map/ppermute | solution.py:618
  19.7 4.3 %collective-permute-start.6 = (f32[64,256]{1,0:T(8,128)S(1)}, f32[64,256]{1,0:T(8,128)S(1)}, u32[]{:S(2)}, u32[]{:S(2)}) collective-permute-start(f32[64,256]{1,0:T(8,128)S(1)} %get-tuple-element.54.own_ref), channel_id=1, source_target_pairs={{0,8},{8,0},{16,24},{24,16},{1,9},{9,1},{17,25},{25,17},{2,10},{10... | collective-permute-start | bytes 196616 | tf_op jit(solution)/shard_map/ppermute | solution.py:620

commit v6 on v5

--- a/solution.py
+++ b/solution.py
@@ -95,9 +95,9 @@
     for n, (source, target) in enumerate((
         (temp_hbm, temp_ref), (kappa_hbm, kappa_ref), (slope_hbm, slope_ref), (power_hbm, power_ref),
     )):
-        copies.append(pltpu.make_async_copy(source.at[:, 0:8], target.at[:, 0:8], block_sem.at[n, 0]))
+        copies.append(pltpu.make_async_copy(source.at[:, 0:2], target.at[:, 0:2], block_sem.at[n, 0]))
         copies.append(
-            pltpu.make_async_copy(source.at[:, rows - 8 : rows], target.at[:, 8:16], block_sem.at[n, 1])
+            pltpu.make_async_copy(source.at[:, rows - 2 : rows], target.at[:, 6:8], block_sem.at[n, 1])
         )
     tops = [
         pltpu.make_async_copy(source.at[0], top_ref.at[n], top_sem.at[n])
@@ -107,9 +107,8 @@
         pltpu.make_async_copy(source, target, small_sem.at[n])
         for n, (source, target) in enumerate(((dir_hbm, dir_ref), (map_hbm, map_ref), (link_hbm, link_ref)))
     ]
-    for m, target in enumerate((core_ref, cross_ref)):
-        smalls.append(pltpu.make_async_copy(flow_hbm, target.at[0:rows], share_sem.at[m, 0]))
-        smalls.append(pltpu.make_async_copy(wall_hbm, target.at[rows : 2 * rows], share_sem.at[m, 1]))
+    smalls.append(pltpu.make_async_copy(flow_hbm, cross_ref.at[0:rows], share_sem.at[0]))
+    smalls.append(pltpu.make_async_copy(wall_hbm, cross_ref.at[rows : 2 * rows], share_sem.at[1]))
     for copy in copies + tops + smalls:
         copy.start()
     tmp_ref[...] = jnp.zeros_like(tmp_ref)
@@ -121,8 +120,8 @@
         after = temp + heat + time_step * power_ref[z]
         for q, value in enumerate((after, temp, kappa_ref[z], slope_ref[z])):
             at = q * layers + z
-            core_ref[share + at : share + at + 1, :] = jnp.where(even, value[15:16], value[0:1])
-            step_ref[at : at + 1, :] = jnp.where(even, value[0:1], value[15:16])
+            core_ref[share + at : share + at + 1, :] = jnp.where(even, value[7:8], value[0:1])
+            step_ref[at : at + 1, :] = jnp.where(even, value[0:1], value[7:8])
 
     closed_heat(temp_ref, kappa_ref, slope_ref, emit)
     for copy in tops:
@@ -139,8 +138,9 @@
         copy.wait()
     row_ref[2:3, 0:rows] = dir_ref[...].astype(F32)
     extra = pltpu.roll(row_ref[...], group * rows, 1)
+    cross_ref[2 * rows : share, :] = extra
     core_ref[2 * rows : share, :] = extra
-    cross_ref[2 * rows : share, :] = extra
+    core_ref[0 : 2 * rows, :] = cross_ref[0 : 2 * rows, :]
 
 
 def open_kernel(
@@ -296,7 +296,7 @@
     channels = groups * rows
     for ref, pick_right in ((sa_ref, place_even), (sb_ref, jnp.logical_not(place_even))):
         ref[...] = jnp.zeros_like(ref)
-        ref[0:4, :] = jnp.where(pick_right, line_ref[4:8, :], line_ref[0:4, :])
+        ref[0:4, 0 : layers * rows] = jnp.where(pick_right, line_ref[4:8, :], line_ref[0:4, :])
         ref[0:1, 0:rows] = ref[0:1, 0:rows] - time_step * jnp.where(
             pick_right, sunk[1:2, 0:rows], sunk[0:1, 0:rows]
         )
@@ -338,7 +338,7 @@
     channels = crow_ref.shape[1]
     low_open = jnp.where(group == 0, 0.0, 1.0)
     high_open = jnp.where(group == groups - 1, 0.0, 1.0)
-    got_a, got_b, own_a, own_b = ra_ref[...], rb_ref[...], sa_ref[...], sb_ref[...]
+    got_a, got_b, own_a, own_b = (ref[0:8, 0 : layers * rows] for ref in (ra_ref, rb_ref, sa_ref, sb_ref))
     got = (jnp.where(even, got_b, got_a), jnp.where(even, got_a, got_b))
     own = (jnp.where(even, own_b, own_a), jnp.where(even, own_a, own_b))
 
@@ -569,9 +569,9 @@
         pack_kernel,
         (wide, share, shape(4 * layers, cols), index, index),
         [
-            vmem(layers, 16, cols), vmem(layers, 16, cols), vmem(layers, 16, cols), vmem(layers, 16, cols),
+            vmem(layers, 8, cols), vmem(layers, 8, cols), vmem(layers, 8, cols), vmem(layers, 8, cols),
             vmem(3, rows, cols), vmem(TILE, TILE), vmem(8, cols), pltpu.VMEM((1, rows), jnp.int32),
-            pltpu.SemaphoreType.DMA((4, 2)), pltpu.SemaphoreType.DMA((3,)), pltpu.SemaphoreType.DMA((2, 2)),
+            pltpu.SemaphoreType.DMA((4, 2)), pltpu.SemaphoreType.DMA((3,)), pltpu.SemaphoreType.DMA((2,)),
             pltpu.SemaphoreType.DMA((3,)),
         ],
         solid_temp, kappa, slope, power, coolant_temp, wall_coeff, flow_dir.reshape(1, rows),
@@ -603,7 +603,7 @@
     after, yo, sa, sb, fw, crow = call(
         select_kernel,
         (
-            block, shape(8 * layers, cols), shape(24, strip), shape(24, strip),
+            block, shape(8 * layers, cols), shape(16, strip + strip // 3), shape(16, strip + strip // 3),
             shape(2 * rows, cols), shape(8, channels),
         ),
         [vmem(channels, 2 * cols), vmem(TILE, TILE)],

time: 25.1 us -> 24.5 us (0.976)
  Pallas kernels: 9.98 us -> 9.39 us
    pallas_call x7, Pallas kernels: 9.98 us -> 9.39 us  [call(): pl.pallas_call(body, out_shape=outs, in_specs=[pl.BlockSpec(memory_space=...]
where the time goes in v6:
time: 24.5 us; the launch traced here: 24.3 us
  starting transfers between devices  13.1 us (53%)
  Pallas kernels  9.39 us (38%)
  waiting for transfers between devices  1.08 us (4%)
  between operations  0.71 us (3%)
    pallas_call x7, Pallas kernels, call(): pl.pallas_call(body, out_shape=outs, in_specs=[pl.BlockSpec(memory_space=...  9.39 us
    ppermute x1, starting transfers between devices, shards(): rb = lax.ppermute(sb, 'loop', pairs(places, 1, True))  3.54 us
    ppermute x1, starting transfers between devices, shards(): got_cross = lax.ppermute(cross, 'grp', across)  2.44 us
    ppermute x1, starting transfers between devices, shards(): relay = lax.ppermute(got_cross, 'grp', beside)  2.01 us
    ppermute x1, starting transfers between devices, shards(): ra = lax.ppermute(sa, 'loop', pairs(places, 0, True))  1.59 us
    ppermute x1, starting transfers between devices, shards(): lax.ppermute(flow, 'grp', [(i, (i + groups // 2) % groups) for i in range...  1.39 us
    ppermute x1, waiting for transfers between devices, shards(): rb = lax.ppermute(sb, 'loop', pairs(places, 1, True))  0.9 us
    ppermute x1, starting transfers between devices, shards(): got_beside = lax.ppermute(flow, 'grp', beside)  0.81 us
  transfers between devices with their start and end apart: 9, of which 2 were waited for; matrix products, arithmetic and copies ran while one was open for 0% of the time, Pallas kernels for 26%

profile of v6, /device:TPU:0, one launch (start us, length us, event | category | flops | bytes accessed | tf_op | source)
XLA Modules:
  0.0 24.3 jit_solution(1496172224197274163)
XLA Ops:
  0.6 1.5 %shard_map.104 = (f32[184,256]{1,0:T(8,128)S(1)}, f32[136,256]{1,0:T(8,128)S(1)}, f32[48,256]{1,0:T(8,128)S(1)}, s32[1,256]{1,0:T(1,128)S(1)}, s32[1,256]{1,0:T(1,128)S(1)}) custom-call(f32[12,64,256]{2,1,0:T(8,128)} %temp_hbm.3, f32[12,64,256]{2,1,0:T(8,128)} %kappa_hbm.3, f32[12,64,256]{2,1,0:T(8,128)} %slope_hbm.3, f32[12,64,256]{2,1,0:T(8,128)} %power_hbm.3, ...), custom_call_target="tpu_custom_call" | custom-call | tf_op jit(solution)/shard_map/pallas_call | solution.py:546
  2.2 2.4 %collective-permute-start = (f32[136,256]{1,0:T(8,128)S(1)}, f32[136,256]{1,0:T(8,128)S(1)}, u32[]{:S(2)}, u32[]{:S(2)}) collective-permute-start(f32[136,256]{1,0:T(8,128)S(1)} %get-tuple-element.29), channel_id=1, source_target_pairs={{0,24},{8,16},{16,8},{24,0},{1,25},{9,17},{17,9},{25,1},{2,26},{10... | collective-permute-start | bytes 417800 | tf_op jit(solution)/shard_map/ppermute | solution.py:583
  4.6 0.7 %collective-permute-start.2 = (f32[184,256]{1,0:T(8,128)S(1)}, f32[184,256]{1,0:T(8,128)S(1)}, u32[]{:S(2)}, u32[]{:S(2)}) collective-permute-start(f32[184,256]{1,0:T(8,128)S(1)} %get-tuple-element.37.own_ref), channel_id=1, source_target_pairs={{0,8},{8,0},{16,24},{24,16},{1,9},{9,1},{17,25},{25,17},{2,10},{10... | collective-permute-start | bytes 565256 | tf_op jit(solution)/shard_map/ppermute | solution.py:585
  5.3 0.7 %collective-permute-start.1 = (f32[48,256]{1,0:T(8,128)S(1)}, f32[48,256]{1,0:T(8,128)S(1)}, u32[]{:S(2)}, u32[]{:S(2)}) collective-permute-start(f32[48,256]{1,0:T(8,128)S(1)} %get-tuple-element.30), channel_id=1, source_target_pairs={{8,16},{16,8},{9,17},{17,9},{10,18},{18,10},{11,19},{19,11},{12,20... | collective-permute-start | bytes 147464 | tf_op jit(solution)/shard_map/ppermute | solution.py:584
  5.9 2.7 %shard_map.105 = (f32[12,64,256]{2,1,0:T(8,128)S(1)}, f32[12,64,256]{2,1,0:T(8,128)S(1)}, f32[12,64,256]{2,1,0:T(8,128)S(1)}, f32[12,64,256]{2,1,0:T(8,128)S(1)}, f32[12,64,256]{2,1,0:T(8,128)S(1)}) custom-call(f32[12,64,256]{2,1,0:T(8,128)} %temp_hbm.3, f32[12,64,256]{2,1,0:T(8,128)} %kappa_hbm.3, f32[12,64,256]{2,1,0:T(8,128)} %slope_hbm.3, ...), custom_call_target="tpu_custom_call" | custom-call | flops 5898240 | bytes 7077888 | tf_op jit(solution)/shard_map/pallas_call | solution.py:546
  8.7 0.0 collective-permute-done.1.step_ref
  8.7 0.0 collective-permute-done.cross_ref
  8.7 2.0 %collective-permute-start.3 = (f32[136,256]{1,0:T(8,128)S(1)}, f32[136,256]{1,0:T(8,128)S(1)}, u32[]{:S(2)}, u32[]{:S(2)}) collective-permute-start(f32[136,256]{1,0:T(8,128)S(1)} %collective-permute-done.cross_ref), channel_id=1, source_target_pairs={{0,8},{8,0},{16,24},{24,16},{1,9},{9,1},{17,25},{25,17},{2,10},{10... | collective-permute-start | bytes 417800 | tf_op jit(solution)/shard_map/ppermute | solution.py:595
  10.7 0.0 collective-permute-done.2.core_ref
  10.7 1.0 %shard_map.106 = (f32[12,64,256]{2,1,0:T(8,128)S(1)}, f32[96,256]{1,0:T(8,128)S(1)}, f32[16,768]{1,0:T(8,128)S(1)}) custom-call(f32[12,64,256]{2,1,0:T(8,128)S(1)} %get-tuple-element.33.first_ref, f32[12,64,256]{2,1,0:T(8,128)S(1)} %get-tuple-element.34.temp_ref, f32[12,64,256]{2,1,0:T(8,128)S(1)} %get-tuple-element.35.kappa_ref, ...), custom_call_target="tpu_custom_call" | custom-call | flops 5898240 | bytes 7077888 | tf_op jit(solution)/shard_map/pallas_call | solution.py:546
  11.7 0.0 collective-permute-done.3.relay_ref
  11.7 0.6 %shard_map.107 = (f32[12,64,256]{2,1,0:T(8,128)S(1)}, f32[96,256]{1,0:T(8,128)S(1)}, f32[16,1024]{1,0:T(8,128)S(1)}, f32[16,1024]{1,0:T(8,128)S(1)}, f32[128,256]{1,0:T(8,128)S(1)}, /*index=5*/f32[8,256]{1,0:T(8,128)S(1)}) custom-call(f32[12,64,256]{2,1,0:T(8,128)S(1)} %get-tuple-element.39.old_ref, ...), custom_call_target="tpu_custom_call", output_to_operand_aliasing={{0}: (0, {}), {1}: (1, {})} | custom-call | tf_op jit(solution)/shard_map/pallas_call | solution.py:546
  12.2 1.6 %collective-permute-start.4 = (f32[16,1024]{1,0:T(8,128)S(1)}, f32[16,1024]{1,0:T(8,128)S(1)}, u32[]{:S(2)}, u32[]{:S(2)}) collective-permute-start(f32[16,1024]{1,0:T(8,128)S(1)} %get-tuple-element.46.sa_ref), channel_id=1, source_target_pairs={{0,1},{1,0},{2,3},{3,2},{4,5},{5,4},{6,7},{7,6},{8,9},{9,8},{10,11... | collective-permute-start | bytes 196616 | tf_op jit(solution)/shard_map/ppermute | solution.py:613
  13.8 3.5 %collective-permute-start.5 = (f32[16,1024]{1,0:T(8,128)S(1)}, f32[16,1024]{1,0:T(8,128)S(1)}, u32[]{:S(2)}, u32[]{:S(2)}) collective-permute-start(f32[16,1024]{1,0:T(8,128)S(1)} %get-tuple-element.47.sb_ref), channel_id=1, source_target_pairs={{1,2},{2,1},{3,4},{4,3},{5,6},{6,5},{7,0},{0,7},{9,10},{10,9},{11,... | collective-permute-start | bytes 196616 | tf_op jit(solution)/shard_map/ppermute | solution.py:614
  17.4 0.3 %shard_map.108 = (f32[64,256]{1,0:T(8,128)S(1)}, f32[64,256]{1,0:T(8,128)S(1)}) custom-call(f32[128,256]{1,0:T(8,128)S(1)} %get-tuple-element.48.fw_ref, f32[12,64,256]{2,1,0:T(8,128)S(1)} %get-tuple-element.34.temp_ref, f32[12,64,256]{2,1,0:T(8,128)S(1)} %get-tuple-element.43.after_ref.temp_ref, f32[8,256]{1,0:T(8,128)S(1)} %get-tuple-element.49.crow_ref, ...), custom_call_target="tpu_custom_call" | custom-call | tf_op jit(solution)/shard_map/pallas_call | solution.py:546
  17.7 1.4 %collective-permute-start.8 = (f32[64,256]{1,0:T(8,128)S(1)}, f32[64,256]{1,0:T(8,128)S(1)}, u32[]{:S(2)}, u32[]{:S(2)}) collective-permute-start(f32[64,256]{1,0:T(8,128)S(1)} %get-tuple-element.54.own_ref), channel_id=1, source_target_pairs={{0,16},{8,24},{16,0},{24,8},{1,17},{9,25},{17,1},{25,9},{2,18},{10... | collective-permute-start | bytes 196616 | tf_op jit(solution)/shard_map/ppermute | solution.py:619
  19.1 0.0 collective-permute-start.7
  19.1 0.8 %collective-permute-start.6 = (f32[64,256]{1,0:T(8,128)S(1)}, f32[64,256]{1,0:T(8,128)S(1)}, u32[]{:S(2)}, u32[]{:S(2)}) collective-permute-start(f32[64,256]{1,0:T(8,128)S(1)} %get-tuple-element.54.own_ref), channel_id=1, source_target_pairs={{0,8},{8,0},{16,24},{24,16},{1,9},{9,1},{17,25},{25,17},{2,10},{10... | collective-permute-start | bytes 196616 | tf_op jit(solution)/shard_map/ppermute | solution.py:620
  19.9 0.0 collective-permute-done.4.ra_ref
  19.9 0.9 %collective-permute-done.5.rb_ref = f32[16,1024]{1,0:T(8,128)S(1)} collective-permute-done((f32[16,1024]{1,0:T(8,128)S(1)}, f32[16,1024]{1,0:T(8,128)S(1)}, u32[]{:S(2)}, u32[]{:S(2)}) %collective-permute-start.5) | collective-permute-done | bytes 65568 | tf_op jit(solution)/shard_map/ppermute | solution.py:614
  20.8 2.4 %shard_map.109 = (f32[12,64,256]{2,1,0:T(8,128)}, f32[4,64,256]{2,1,0:T(8,128)S(1)}, f32[128,128]{1,0:T(8,128)S(1)}) custom-call(f32[12,64,256]{2,1,0:T(8,128)S(1)} %get-tuple-element.43.after_ref.temp_ref, f32[12,64,256]{2,1,0:T(8,128)S(1)} %get-tuple-element.35.kappa_ref, f32[12,64,256]{2,1,0:T(8,128)S(1)} %get-tuple-element.36.slope_ref, ...), custom_call_target="tpu_custom_call" | custom-call | flops 5898240 | bytes 7077888 | tf_op jit(solution)/shard_map/pallas_call | solution.py:546
  23.2 0.0 collective-permute-done.8.relay_ref
  23.2 0.2 collective-permute-done.7.cross_ref
  23.4 0.0 collective-permute-done.6.core_ref
  23.4 0.9 %shard_map.110 = (f32[12,64,256]{2,1,0:T(8,128)}, f32[64,256]{1,0:T(8,128)}) custom-call(f32[12,64,256]{2,1,0:T(8,128)} %get-tuple-element.52.part_hbm, f32[4,64,256]{2,1,0:T(8,128)S(1)} %get-tuple-element.53.tail_ref, f32[64,256]{1,0:T(8,128)S(1)} %get-tuple-element.54.own_ref, ...), custom_call_target="tpu_custom_call", output_to_operand_aliasing={{0}: (0, {})} | custom-call | tf_op jit(solution)/shard_map/pallas_call | solution.py:546
Async XLA Ops:
  2.2 6.5 %collective-permute-start = (f32[136,256]{1,0:T(8,128)S(1)}, f32[136,256]{1,0:T(8,128)S(1)}, u32[]{:S(2)}, u32[]{:S(2)}) collective-permute-start(f32[136,256]{1,0:T(8,128)S(1)} %get-tuple-element.29), channel_id=1, source_target_pairs={{0,24},{8,16},{16,8},{24,0},{1,25},{9,17},{17,9},{25,1},{2,26},{10... | collective-permute-start | bytes 417800 | tf_op jit(solution)/shard_map/ppermute | solution.py:583
  4.6 6.1 %collective-permute-start.2 = (f32[184,256]{1,0:T(8,128)S(1)}, f32[184,256]{1,0:T(8,128)S(1)}, u32[]{:S(2)}, u32[]{:S(2)}) collective-permute-start(f32[184,256]{1,0:T(8,128)S(1)} %get-tuple-element.37.own_ref), channel_id=1, source_target_pairs={{0,8},{8,0},{16,24},{24,16},{1,9},{9,1},{17,25},{25,17},{2,10},{10... | collective-permute-start | bytes 565256 | tf_op jit(solution)/shard_map/ppermute | solution.py:585
  5.3 3.4 %collective-permute-start.1 = (f32[48,256]{1,0:T(8,128)S(1)}, f32[48,256]{1,0:T(8,128)S(1)}, u32[]{:S(2)}, u32[]{:S(2)}) collective-permute-start(f32[48,256]{1,0:T(8,128)S(1)} %get-tuple-element.30), channel_id=1, source_target_pairs={{8,16},{16,8},{9,17},{17,9},{10,18},{18,10},{11,19},{19,11},{12,20... | collective-permute-start | bytes 147464 | tf_op jit(solution)/shard_map/ppermute | solution.py:584
  8.7 3.0 %collective-permute-start.3 = (f32[136,256]{1,0:T(8,128)S(1)}, f32[136,256]{1,0:T(8,128)S(1)}, u32[]{:S(2)}, u32[]{:S(2)}) collective-permute-start(f32[136,256]{1,0:T(8,128)S(1)} %collective-permute-done.cross_ref), channel_id=1, source_target_pairs={{0,8},{8,0},{16,24},{24,16},{1,9},{9,1},{17,25},{25,17},{2,10},{10... | collective-permute-start | bytes 417800 | tf_op jit(solution)/shard_map/ppermute | solution.py:595
  12.2 7.7 %collective-permute-start.4 = (f32[16,1024]{1,0:T(8,128)S(1)}, f32[16,1024]{1,0:T(8,128)S(1)}, u32[]{:S(2)}, u32[]{:S(2)}) collective-permute-start(f32[16,1024]{1,0:T(8,128)S(1)} %get-tuple-element.46.sa_ref), channel_id=1, source_target_pairs={{0,1},{1,0},{2,3},{3,2},{4,5},{5,4},{6,7},{7,6},{8,9},{9,8},{10,11... | collective-permute-start | bytes 196616 | tf_op jit(solution)/shard_map/ppermute | solution.py:613
  13.8 7.0 %collective-permute-start.5 = (f32[16,1024]{1,0:T(8,128)S(1)}, f32[16,1024]{1,0:T(8,128)S(1)}, u32[]{:S(2)}, u32[]{:S(2)}) collective-permute-start(f32[16,1024]{1,0:T(8,128)S(1)} %get-tuple-element.47.sb_ref), channel_id=1, source_target_pairs={{1,2},{2,1},{3,4},{4,3},{5,6},{6,5},{7,0},{0,7},{9,10},{10,9},{11,... | collective-permute-start | bytes 196616 | tf_op jit(solution)/shard_map/ppermute | solution.py:614
  17.7 5.6 %collective-permute-start.8 = (f32[64,256]{1,0:T(8,128)S(1)}, f32[64,256]{1,0:T(8,128)S(1)}, u32[]{:S(2)}, u32[]{:S(2)}) collective-permute-start(f32[64,256]{1,0:T(8,128)S(1)} %get-tuple-element.54.own_ref), channel_id=1, source_target_pairs={{0,16},{8,24},{16,0},{24,8},{1,17},{9,25},{17,1},{25,9},{2,18},{10... | collective-permute-start | bytes 196616 | tf_op jit(solution)/shard_map/ppermute | solution.py:619
  19.1 4.3 %collective-permute-start.7 = (f32[64,256]{1,0:T(8,128)S(1)}, f32[64,256]{1,0:T(8,128)S(1)}, u32[]{:S(2)}, u32[]{:S(2)}) collective-permute-start(f32[64,256]{1,0:T(8,128)S(1)} %get-tuple-element.54.own_ref), channel_id=1, source_target_pairs={{0,24},{8,16},{16,8},{24,0},{1,25},{9,17},{17,9},{25,1},{2,26},{10... | collective-permute-start | bytes 196616 | tf_op jit(solution)/shard_map/ppermute | solution.py:618
  19.1 4.3 %collective-permute-start.6 = (f32[64,256]{1,0:T(8,128)S(1)}, f32[64,256]{1,0:T(8,128)S(1)}, u32[]{:S(2)}, u32[]{:S(2)}) collective-permute-start(f32[64,256]{1,0:T(8,128)S(1)} %get-tuple-element.54.own_ref), channel_id=1, source_target_pairs={{0,8},{8,0},{16,24},{24,16},{1,9},{9,1},{17,25},{25,17},{2,10},{10... | collective-permute-start | bytes 196616 | tf_op jit(solution)/shard_map/ppermute | solution.py:620

commit v7 on v6

--- a/solution.py
+++ b/solution.py
@@ -311,7 +311,10 @@
     rows, cols = first_ref.shape
     channels = crow_ref.shape[1]
     chooser = one_hot(map_ref[...], lax.axis_index("grp") * rows, rows)
-    toward = pick(chooser, jnp.broadcast_to(crow_ref[0:1, :], (TILE, channels)), ((1,), (1,)))
+    toward = lax.dot_general(
+        chooser, jnp.broadcast_to(crow_ref[0:1, :], (TILE, channels)).astype(BF16), (((1,), (1,)), ((), ())),
+        preferred_element_type=F32,
+    )
     toward = jnp.concatenate([toward] * (cols // TILE), 1) > 0.5
     lane = lax.broadcasted_iota(jnp.int32, (rows, cols), 1)
 

time: 24.5 us -> 24.4 us (level)
  no operation moved by 1% of the time
where the time goes in v7:
time: 24.4 us; the launch traced here: 24.3 us
  starting transfers between devices  13.1 us (54%)
  Pallas kernels  9.35 us (38%)
  waiting for transfers between devices  1.08 us (4%)
  between operations  0.71 us (3%)
    pallas_call x7, Pallas kernels, call(): pl.pallas_call(body, out_shape=outs, in_specs=[pl.BlockSpec(memory_space=...  9.35 us
    ppermute x1, starting transfers between devices, shards(): rb = lax.ppermute(sb, 'loop', pairs(places, 1, True))  3.54 us
    ppermute x1, starting transfers between devices, shards(): got_cross = lax.ppermute(cross, 'grp', across)  2.44 us
    ppermute x1, starting transfers between devices, shards(): relay = lax.ppermute(got_cross, 'grp', beside)  2.01 us
    ppermute x1, starting transfers between devices, shards(): ra = lax.ppermute(sa, 'loop', pairs(places, 0, True))  1.59 us
    ppermute x1, starting transfers between devices, shards(): lax.ppermute(flow, 'grp', [(i, (i + groups // 2) % groups) for i in range...  1.39 us
    ppermute x1, waiting for transfers between devices, shards(): rb = lax.ppermute(sb, 'loop', pairs(places, 1, True))  0.94 us
    ppermute x1, starting transfers between devices, shards(): got_beside = lax.ppermute(flow, 'grp', beside)  0.81 us
  transfers between devices with their start and end apart: 9, of which 2 were waited for; matrix products, arithmetic and copies ran while one was open for 0% of the time, Pallas kernels for 26%

profile of v7, /device:TPU:0, one launch (start us, length us, event | category | flops | bytes accessed | tf_op | source)
XLA Modules:
  0.0 24.3 jit_solution(16905030366354092351)
XLA Ops:
  0.6 1.5 %shard_map.104 = (f32[184,256]{1,0:T(8,128)S(1)}, f32[136,256]{1,0:T(8,128)S(1)}, f32[48,256]{1,0:T(8,128)S(1)}, s32[1,256]{1,0:T(1,128)S(1)}, s32[1,256]{1,0:T(1,128)S(1)}) custom-call(f32[12,64,256]{2,1,0:T(8,128)} %temp_hbm.3, f32[12,64,256]{2,1,0:T(8,128)} %kappa_hbm.3, f32[12,64,256]{2,1,0:T(8,128)} %slope_hbm.3, f32[12,64,256]{2,1,0:T(8,128)} %power_hbm.3, ...), custom_call_target="tpu_custom_call" | custom-call | tf_op jit(solution)/shard_map/pallas_call | solution.py:549
  2.2 2.4 %collective-permute-start = (f32[136,256]{1,0:T(8,128)S(1)}, f32[136,256]{1,0:T(8,128)S(1)}, u32[]{:S(2)}, u32[]{:S(2)}) collective-permute-start(f32[136,256]{1,0:T(8,128)S(1)} %get-tuple-element.29), channel_id=1, source_target_pairs={{0,24},{8,16},{16,8},{24,0},{1,25},{9,17},{17,9},{25,1},{2,26},{10... | collective-permute-start | bytes 417800 | tf_op jit(solution)/shard_map/ppermute | solution.py:586
  4.6 0.7 %collective-permute-start.2 = (f32[184,256]{1,0:T(8,128)S(1)}, f32[184,256]{1,0:T(8,128)S(1)}, u32[]{:S(2)}, u32[]{:S(2)}) collective-permute-start(f32[184,256]{1,0:T(8,128)S(1)} %get-tuple-element.37.own_ref), channel_id=1, source_target_pairs={{0,8},{8,0},{16,24},{24,16},{1,9},{9,1},{17,25},{25,17},{2,10},{10... | collective-permute-start | bytes 565256 | tf_op jit(solution)/shard_map/ppermute | solution.py:588
  5.3 0.7 %collective-permute-start.1 = (f32[48,256]{1,0:T(8,128)S(1)}, f32[48,256]{1,0:T(8,128)S(1)}, u32[]{:S(2)}, u32[]{:S(2)}) collective-permute-start(f32[48,256]{1,0:T(8,128)S(1)} %get-tuple-element.30), channel_id=1, source_target_pairs={{8,16},{16,8},{9,17},{17,9},{10,18},{18,10},{11,19},{19,11},{12,20... | collective-permute-start | bytes 147464 | tf_op jit(solution)/shard_map/ppermute | solution.py:587
  5.9 2.7 %shard_map.105 = (f32[12,64,256]{2,1,0:T(8,128)S(1)}, f32[12,64,256]{2,1,0:T(8,128)S(1)}, f32[12,64,256]{2,1,0:T(8,128)S(1)}, f32[12,64,256]{2,1,0:T(8,128)S(1)}, f32[12,64,256]{2,1,0:T(8,128)S(1)}) custom-call(f32[12,64,256]{2,1,0:T(8,128)} %temp_hbm.3, f32[12,64,256]{2,1,0:T(8,128)} %kappa_hbm.3, f32[12,64,256]{2,1,0:T(8,128)} %slope_hbm.3, ...), custom_call_target="tpu_custom_call" | custom-call | flops 5898240 | bytes 7077888 | tf_op jit(solution)/shard_map/pallas_call | solution.py:549
  8.7 0.0 collective-permute-done.1.step_ref
  8.7 0.0 collective-permute-done.cross_ref
  8.7 2.0 %collective-permute-start.3 = (f32[136,256]{1,0:T(8,128)S(1)}, f32[136,256]{1,0:T(8,128)S(1)}, u32[]{:S(2)}, u32[]{:S(2)}) collective-permute-start(f32[136,256]{1,0:T(8,128)S(1)} %collective-permute-done.cross_ref), channel_id=1, source_target_pairs={{0,8},{8,0},{16,24},{24,16},{1,9},{9,1},{17,25},{25,17},{2,10},{10... | collective-permute-start | bytes 417800 | tf_op jit(solution)/shard_map/ppermute | solution.py:598
  10.7 0.0 collective-permute-done.2.core_ref
  10.7 1.0 %shard_map.106 = (f32[12,64,256]{2,1,0:T(8,128)S(1)}, f32[96,256]{1,0:T(8,128)S(1)}, f32[16,768]{1,0:T(8,128)S(1)}) custom-call(f32[12,64,256]{2,1,0:T(8,128)S(1)} %get-tuple-element.33.first_ref, f32[12,64,256]{2,1,0:T(8,128)S(1)} %get-tuple-element.34.temp_ref, f32[12,64,256]{2,1,0:T(8,128)S(1)} %get-tuple-element.35.kappa_ref, ...), custom_call_target="tpu_custom_call" | custom-call | flops 5898240 | bytes 7077888 | tf_op jit(solution)/shard_map/pallas_call | solution.py:549
  11.7 0.0 collective-permute-done.3.relay_ref
  11.7 0.6 %shard_map.107 = (f32[12,64,256]{2,1,0:T(8,128)S(1)}, f32[96,256]{1,0:T(8,128)S(1)}, f32[16,1024]{1,0:T(8,128)S(1)}, f32[16,1024]{1,0:T(8,128)S(1)}, f32[128,256]{1,0:T(8,128)S(1)}, /*index=5*/f32[8,256]{1,0:T(8,128)S(1)}) custom-call(f32[12,64,256]{2,1,0:T(8,128)S(1)} %get-tuple-element.39.old_ref, ...), custom_call_target="tpu_custom_call", output_to_operand_aliasing={{0}: (0, {}), {1}: (1, {})} | custom-call | tf_op jit(solution)/shard_map/pallas_call | solution.py:549
  12.2 1.6 %collective-permute-start.4 = (f32[16,1024]{1,0:T(8,128)S(1)}, f32[16,1024]{1,0:T(8,128)S(1)}, u32[]{:S(2)}, u32[]{:S(2)}) collective-permute-start(f32[16,1024]{1,0:T(8,128)S(1)} %get-tuple-element.46.sa_ref), channel_id=1, source_target_pairs={{0,1},{1,0},{2,3},{3,2},{4,5},{5,4},{6,7},{7,6},{8,9},{9,8},{10,11... | collective-permute-start | bytes 196616 | tf_op jit(solution)/shard_map/ppermute | solution.py:616
  13.8 3.5 %collective-permute-start.5 = (f32[16,1024]{1,0:T(8,128)S(1)}, f32[16,1024]{1,0:T(8,128)S(1)}, u32[]{:S(2)}, u32[]{:S(2)}) collective-permute-start(f32[16,1024]{1,0:T(8,128)S(1)} %get-tuple-element.47.sb_ref), channel_id=1, source_target_pairs={{1,2},{2,1},{3,4},{4,3},{5,6},{6,5},{7,0},{0,7},{9,10},{10,9},{11,... | collective-permute-start | bytes 196616 | tf_op jit(solution)/shard_map/ppermute | solution.py:617
  17.4 0.3 %shard_map.108 = (f32[64,256]{1,0:T(8,128)S(1)}, f32[64,256]{1,0:T(8,128)S(1)}) custom-call(f32[128,256]{1,0:T(8,128)S(1)} %get-tuple-element.48.fw_ref, f32[12,64,256]{2,1,0:T(8,128)S(1)} %get-tuple-element.34.temp_ref, f32[12,64,256]{2,1,0:T(8,128)S(1)} %get-tuple-element.43.after_ref.temp_ref, f32[8,256]{1,0:T(8,128)S(1)} %get-tuple-element.49.crow_ref, ...), custom_call_target="tpu_custom_call" | custom-call | tf_op jit(solution)/shard_map/pallas_call | solution.py:549
  17.6 1.4 %collective-permute-start.8 = (f32[64,256]{1,0:T(8,128)S(1)}, f32[64,256]{1,0:T(8,128)S(1)}, u32[]{:S(2)}, u32[]{:S(2)}) collective-permute-start(f32[64,256]{1,0:T(8,128)S(1)} %get-tuple-element.54.own_ref), channel_id=1, source_target_pairs={{0,16},{8,24},{16,0},{24,8},{1,17},{9,25},{17,1},{25,9},{2,18},{10... | collective-permute-start | bytes 196616 | tf_op jit(solution)/shard_map/ppermute | solution.py:622
  19.0 0.0 collective-permute-start.7
  19.0 0.8 %collective-permute-start.6 = (f32[64,256]{1,0:T(8,128)S(1)}, f32[64,256]{1,0:T(8,128)S(1)}, u32[]{:S(2)}, u32[]{:S(2)}) collective-permute-start(f32[64,256]{1,0:T(8,128)S(1)} %get-tuple-element.54.own_ref), channel_id=1, source_target_pairs={{0,8},{8,0},{16,24},{24,16},{1,9},{9,1},{17,25},{25,17},{2,10},{10... | collective-permute-start | bytes 196616 | tf_op jit(solution)/shard_map/ppermute | solution.py:623
  19.8 0.0 collective-permute-done.4.ra_ref
  19.8 0.9 %collective-permute-done.5.rb_ref = f32[16,1024]{1,0:T(8,128)S(1)} collective-permute-done((f32[16,1024]{1,0:T(8,128)S(1)}, f32[16,1024]{1,0:T(8,128)S(1)}, u32[]{:S(2)}, u32[]{:S(2)}) %collective-permute-start.5) | collective-permute-done | bytes 65568 | tf_op jit(solution)/shard_map/ppermute | solution.py:617
  20.8 2.4 %shard_map.109 = (f32[12,64,256]{2,1,0:T(8,128)}, f32[4,64,256]{2,1,0:T(8,128)S(1)}, f32[128,128]{1,0:T(8,128)S(1)}) custom-call(f32[12,64,256]{2,1,0:T(8,128)S(1)} %get-tuple-element.43.after_ref.temp_ref, f32[12,64,256]{2,1,0:T(8,128)S(1)} %get-tuple-element.35.kappa_ref, f32[12,64,256]{2,1,0:T(8,128)S(1)} %get-tuple-element.36.slope_ref, ...), custom_call_target="tpu_custom_call" | custom-call | flops 5898240 | bytes 7077888 | tf_op jit(solution)/shard_map/pallas_call | solution.py:549
  23.2 0.0 collective-permute-done.8.relay_ref
  23.2 0.1 collective-permute-done.7.cross_ref
  23.4 0.0 collective-permute-done.6.core_ref
  23.4 0.9 %shard_map.110 = (f32[12,64,256]{2,1,0:T(8,128)}, f32[64,256]{1,0:T(8,128)}) custom-call(f32[12,64,256]{2,1,0:T(8,128)} %get-tuple-element.52.part_hbm, f32[4,64,256]{2,1,0:T(8,128)S(1)} %get-tuple-element.53.tail_ref, f32[64,256]{1,0:T(8,128)S(1)} %get-tuple-element.54.own_ref, ...), custom_call_target="tpu_custom_call", output_to_operand_aliasing={{0}: (0, {})} | custom-call | tf_op jit(solution)/shard_map/pallas_call | solution.py:549
Async XLA Ops:
  2.2 6.5 %collective-permute-start = (f32[136,256]{1,0:T(8,128)S(1)}, f32[136,256]{1,0:T(8,128)S(1)}, u32[]{:S(2)}, u32[]{:S(2)}) collective-permute-start(f32[136,256]{1,0:T(8,128)S(1)} %get-tuple-element.29), channel_id=1, source_target_pairs={{0,24},{8,16},{16,8},{24,0},{1,25},{9,17},{17,9},{25,1},{2,26},{10... | collective-permute-start | bytes 417800 | tf_op jit(solution)/shard_map/ppermute | solution.py:586
  4.6 6.1 %collective-permute-start.2 = (f32[184,256]{1,0:T(8,128)S(1)}, f32[184,256]{1,0:T(8,128)S(1)}, u32[]{:S(2)}, u32[]{:S(2)}) collective-permute-start(f32[184,256]{1,0:T(8,128)S(1)} %get-tuple-element.37.own_ref), channel_id=1, source_target_pairs={{0,8},{8,0},{16,24},{24,16},{1,9},{9,1},{17,25},{25,17},{2,10},{10... | collective-permute-start | bytes 565256 | tf_op jit(solution)/shard_map/ppermute | solution.py:588
  5.3 3.4 %collective-permute-start.1 = (f32[48,256]{1,0:T(8,128)S(1)}, f32[48,256]{1,0:T(8,128)S(1)}, u32[]{:S(2)}, u32[]{:S(2)}) collective-permute-start(f32[48,256]{1,0:T(8,128)S(1)} %get-tuple-element.30), channel_id=1, source_target_pairs={{8,16},{16,8},{9,17},{17,9},{10,18},{18,10},{11,19},{19,11},{12,20... | collective-permute-start | bytes 147464 | tf_op jit(solution)/shard_map/ppermute | solution.py:587
  8.7 3.0 %collective-permute-start.3 = (f32[136,256]{1,0:T(8,128)S(1)}, f32[136,256]{1,0:T(8,128)S(1)}, u32[]{:S(2)}, u32[]{:S(2)}) collective-permute-start(f32[136,256]{1,0:T(8,128)S(1)} %collective-permute-done.cross_ref), channel_id=1, source_target_pairs={{0,8},{8,0},{16,24},{24,16},{1,9},{9,1},{17,25},{25,17},{2,10},{10... | collective-permute-start | bytes 417800 | tf_op jit(solution)/shard_map/ppermute | solution.py:598
  12.2 7.6 %collective-permute-start.4 = (f32[16,1024]{1,0:T(8,128)S(1)}, f32[16,1024]{1,0:T(8,128)S(1)}, u32[]{:S(2)}, u32[]{:S(2)}) collective-permute-start(f32[16,1024]{1,0:T(8,128)S(1)} %get-tuple-element.46.sa_ref), channel_id=1, source_target_pairs={{0,1},{1,0},{2,3},{3,2},{4,5},{5,4},{6,7},{7,6},{8,9},{9,8},{10,11... | collective-permute-start | bytes 196616 | tf_op jit(solution)/shard_map/ppermute | solution.py:616
  13.8 7.0 %collective-permute-start.5 = (f32[16,1024]{1,0:T(8,128)S(1)}, f32[16,1024]{1,0:T(8,128)S(1)}, u32[]{:S(2)}, u32[]{:S(2)}) collective-permute-start(f32[16,1024]{1,0:T(8,128)S(1)} %get-tuple-element.47.sb_ref), channel_id=1, source_target_pairs={{1,2},{2,1},{3,4},{4,3},{5,6},{6,5},{7,0},{0,7},{9,10},{10,9},{11,... | collective-permute-start | bytes 196616 | tf_op jit(solution)/shard_map/ppermute | solution.py:617
  17.6 5.6 %collective-permute-start.8 = (f32[64,256]{1,0:T(8,128)S(1)}, f32[64,256]{1,0:T(8,128)S(1)}, u32[]{:S(2)}, u32[]{:S(2)}) collective-permute-start(f32[64,256]{1,0:T(8,128)S(1)} %get-tuple-element.54.own_ref), channel_id=1, source_target_pairs={{0,16},{8,24},{16,0},{24,8},{1,17},{9,25},{17,1},{25,9},{2,18},{10... | collective-permute-start | bytes 196616 | tf_op jit(solution)/shard_map/ppermute | solution.py:622
  19.0 4.3 %collective-permute-start.7 = (f32[64,256]{1,0:T(8,128)S(1)}, f32[64,256]{1,0:T(8,128)S(1)}, u32[]{:S(2)}, u32[]{:S(2)}) collective-permute-start(f32[64,256]{1,0:T(8,128)S(1)} %get-tuple-element.54.own_ref), channel_id=1, source_target_pairs={{0,24},{8,16},{16,8},{24,0},{1,25},{9,17},{17,9},{25,1},{2,26},{10... | collective-permute-start | bytes 196616 | tf_op jit(solution)/shard_map/ppermute | solution.py:621
  19.0 4.3 %collective-permute-start.6 = (f32[64,256]{1,0:T(8,128)S(1)}, f32[64,256]{1,0:T(8,128)S(1)}, u32[]{:S(2)}, u32[]{:S(2)}) collective-permute-start(f32[64,256]{1,0:T(8,128)S(1)} %get-tuple-element.54.own_ref), channel_id=1, source_target_pairs={{0,8},{8,0},{16,24},{24,16},{1,9},{9,1},{17,25},{25,17},{2,10},{10... | collective-permute-start | bytes 196616 | tf_op jit(solution)/shard_map/ppermute | solution.py:623

commit v8 on v7

--- a/solution.py
+++ b/solution.py
@@ -491,7 +491,7 @@
 
 
 def return_kernel(
-    part_hbm, tail_ref, own_ref, core_ref, cross_ref, relay_ref, add_ref,
+    part_hbm, tail_ref, own_ref, cross_ref, core_ref, relay_ref, add_ref,
     out_hbm, flow_hbm, all_ref, out_ref, sem,
 ):
     rows, cols = out_ref.shape
@@ -638,7 +638,7 @@
         return_kernel,
         (block, shape(rows, cols)),
         [vmem(channels, cols), vmem(rows, cols), pltpu.SemaphoreType.DMA((2,))],
-        out, tail, flow, got_beside, got_across, got_over, adds,
+        out, tail, flow, got_across, got_beside, got_over, adds,
         far=1,
         outs_far=2,
         alias={0: 0},

time: 24.4 us -> 24.3 us (level)
    ppermute x1, starting transfers between devices: 0.81 us -> 0.01 us  [shards(): got_beside = lax.ppermute(flow, 'grp', beside)]
    ppermute x1, starting transfers between devices: 0.01 us -> 0.81 us  [shards(): got_across = lax.ppermute(flow, 'grp', across)]
  transfers between devices with their start and end apart: 9 -> 9, of which waited for: 2 -> 1; matrix products, arithmetic and copies ran while one was open for 0% -> 0% of each run, Pallas kernels for 26% -> 26%
where the time goes in v8:
time: 24.3 us; the launch traced here: 24.2 us
  starting transfers between devices  13.1 us (54%)
  Pallas kernels  9.35 us (38%)
  waiting for transfers between devices  0.96 us (4%)
  between operations  0.72 us (3%)
    pallas_call x7, Pallas kernels, call(): pl.pallas_call(body, out_shape=outs, in_specs=[pl.BlockSpec(memory_space=...  9.35 us
    ppermute x1, starting transfers between devices, shards(): rb = lax.ppermute(sb, 'loop', pairs(places, 1, True))  3.54 us
    ppermute x1, starting transfers between devices, shards(): got_cross = lax.ppermute(cross, 'grp', across)  2.44 us
    ppermute x1, starting transfers between devices, shards(): relay = lax.ppermute(got_cross, 'grp', beside)  2.01 us
    ppermute x1, starting transfers between devices, shards(): ra = lax.ppermute(sa, 'loop', pairs(places, 0, True))  1.59 us
    ppermute x1, starting transfers between devices, shards(): lax.ppermute(flow, 'grp', [(i, (i + groups // 2) % groups) for i in range...  1.39 us
    ppermute x1, waiting for transfers between devices, shards(): rb = lax.ppermute(sb, 'loop', pairs(places, 1, True))  0.94 us
    ppermute x1, starting transfers between devices, shards(): got_across = lax.ppermute(flow, 'grp', across)  0.81 us
  transfers between devices with their start and end apart: 9, of which 1 were waited for; matrix products, arithmetic and copies ran while one was open for 0% of the time, Pallas kernels for 26%

profile of v8, /device:TPU:0, one launch (start us, length us, event | category | flops | bytes accessed | tf_op | source)
XLA Modules:
  0.0 24.2 jit_solution(10959631065612927289)
XLA Ops:
  0.6 1.5 %shard_map.104 = (f32[184,256]{1,0:T(8,128)S(1)}, f32[136,256]{1,0:T(8,128)S(1)}, f32[48,256]{1,0:T(8,128)S(1)}, s32[1,256]{1,0:T(1,128)S(1)}, s32[1,256]{1,0:T(1,128)S(1)}) custom-call(f32[12,64,256]{2,1,0:T(8,128)} %temp_hbm.3, f32[12,64,256]{2,1,0:T(8,128)} %kappa_hbm.3, f32[12,64,256]{2,1,0:T(8,128)} %slope_hbm.3, f32[12,64,256]{2,1,0:T(8,128)} %power_hbm.3, ...), custom_call_target="tpu_custom_call" | custom-call | tf_op jit(solution)/shard_map/pallas_call | solution.py:549
  2.2 2.4 %collective-permute-start = (f32[136,256]{1,0:T(8,128)S(1)}, f32[136,256]{1,0:T(8,128)S(1)}, u32[]{:S(2)}, u32[]{:S(2)}) collective-permute-start(f32[136,256]{1,0:T(8,128)S(1)} %get-tuple-element.29), channel_id=1, source_target_pairs={{0,24},{8,16},{16,8},{24,0},{1,25},{9,17},{17,9},{25,1},{2,26},{10... | collective-permute-start | bytes 417800 | tf_op jit(solution)/shard_map/ppermute | solution.py:586
  4.6 0.7 %collective-permute-start.2 = (f32[184,256]{1,0:T(8,128)S(1)}, f32[184,256]{1,0:T(8,128)S(1)}, u32[]{:S(2)}, u32[]{:S(2)}) collective-permute-start(f32[184,256]{1,0:T(8,128)S(1)} %get-tuple-element.37.own_ref), channel_id=1, source_target_pairs={{0,8},{8,0},{16,24},{24,16},{1,9},{9,1},{17,25},{25,17},{2,10},{10... | collective-permute-start | bytes 565256 | tf_op jit(solution)/shard_map/ppermute | solution.py:588
  5.3 0.7 %collective-permute-start.1 = (f32[48,256]{1,0:T(8,128)S(1)}, f32[48,256]{1,0:T(8,128)S(1)}, u32[]{:S(2)}, u32[]{:S(2)}) collective-permute-start(f32[48,256]{1,0:T(8,128)S(1)} %get-tuple-element.30), channel_id=1, source_target_pairs={{8,16},{16,8},{9,17},{17,9},{10,18},{18,10},{11,19},{19,11},{12,20... | collective-permute-start | bytes 147464 | tf_op jit(solution)/shard_map/ppermute | solution.py:587
  5.9 2.7 %shard_map.105 = (f32[12,64,256]{2,1,0:T(8,128)S(1)}, f32[12,64,256]{2,1,0:T(8,128)S(1)}, f32[12,64,256]{2,1,0:T(8,128)S(1)}, f32[12,64,256]{2,1,0:T(8,128)S(1)}, f32[12,64,256]{2,1,0:T(8,128)S(1)}) custom-call(f32[12,64,256]{2,1,0:T(8,128)} %temp_hbm.3, f32[12,64,256]{2,1,0:T(8,128)} %kappa_hbm.3, f32[12,64,256]{2,1,0:T(8,128)} %slope_hbm.3, ...), custom_call_target="tpu_custom_call" | custom-call | flops 5898240 | bytes 7077888 | tf_op jit(solution)/shard_map/pallas_call | solution.py:549
  8.7 0.0 collective-permute-done.1.step_ref
  8.7 0.0 collective-permute-done.cross_ref
  8.7 2.0 %collective-permute-start.3 = (f32[136,256]{1,0:T(8,128)S(1)}, f32[136,256]{1,0:T(8,128)S(1)}, u32[]{:S(2)}, u32[]{:S(2)}) collective-permute-start(f32[136,256]{1,0:T(8,128)S(1)} %collective-permute-done.cross_ref), channel_id=1, source_target_pairs={{0,8},{8,0},{16,24},{24,16},{1,9},{9,1},{17,25},{25,17},{2,10},{10... | collective-permute-start | bytes 417800 | tf_op jit(solution)/shard_map/ppermute | solution.py:598
  10.7 0.0 collective-permute-done.2.core_ref
  10.7 1.0 %shard_map.106 = (f32[12,64,256]{2,1,0:T(8,128)S(1)}, f32[96,256]{1,0:T(8,128)S(1)}, f32[16,768]{1,0:T(8,128)S(1)}) custom-call(f32[12,64,256]{2,1,0:T(8,128)S(1)} %get-tuple-element.33.first_ref, f32[12,64,256]{2,1,0:T(8,128)S(1)} %get-tuple-element.34.temp_ref, f32[12,64,256]{2,1,0:T(8,128)S(1)} %get-tuple-element.35.kappa_ref, ...), custom_call_target="tpu_custom_call" | custom-call | flops 5898240 | bytes 7077888 | tf_op jit(solution)/shard_map/pallas_call | solution.py:549
  11.7 0.0 collective-permute-done.3.relay_ref
  11.7 0.6 %shard_map.107 = (f32[12,64,256]{2,1,0:T(8,128)S(1)}, f32[96,256]{1,0:T(8,128)S(1)}, f32[16,1024]{1,0:T(8,128)S(1)}, f32[16,1024]{1,0:T(8,128)S(1)}, f32[128,256]{1,0:T(8,128)S(1)}, /*index=5*/f32[8,256]{1,0:T(8,128)S(1)}) custom-call(f32[12,64,256]{2,1,0:T(8,128)S(1)} %get-tuple-element.39.old_ref, ...), custom_call_target="tpu_custom_call", output_to_operand_aliasing={{0}: (0, {}), {1}: (1, {})} | custom-call | tf_op jit(solution)/shard_map/pallas_call | solution.py:549
  12.2 1.6 %collective-permute-start.4 = (f32[16,1024]{1,0:T(8,128)S(1)}, f32[16,1024]{1,0:T(8,128)S(1)}, u32[]{:S(2)}, u32[]{:S(2)}) collective-permute-start(f32[16,1024]{1,0:T(8,128)S(1)} %get-tuple-element.46.sa_ref), channel_id=1, source_target_pairs={{0,1},{1,0},{2,3},{3,2},{4,5},{5,4},{6,7},{7,6},{8,9},{9,8},{10,11... | collective-permute-start | bytes 196616 | tf_op jit(solution)/shard_map/ppermute | solution.py:616
  13.8 3.5 %collective-permute-start.5 = (f32[16,1024]{1,0:T(8,128)S(1)}, f32[16,1024]{1,0:T(8,128)S(1)}, u32[]{:S(2)}, u32[]{:S(2)}) collective-permute-start(f32[16,1024]{1,0:T(8,128)S(1)} %get-tuple-element.47.sb_ref), channel_id=1, source_target_pairs={{1,2},{2,1},{3,4},{4,3},{5,6},{6,5},{7,0},{0,7},{9,10},{10,9},{11,... | collective-permute-start | bytes 196616 | tf_op jit(solution)/shard_map/ppermute | solution.py:617
  17.4 0.3 %shard_map.108 = (f32[64,256]{1,0:T(8,128)S(1)}, f32[64,256]{1,0:T(8,128)S(1)}) custom-call(f32[128,256]{1,0:T(8,128)S(1)} %get-tuple-element.48.fw_ref, f32[12,64,256]{2,1,0:T(8,128)S(1)} %get-tuple-element.34.temp_ref, f32[12,64,256]{2,1,0:T(8,128)S(1)} %get-tuple-element.43.after_ref.temp_ref, f32[8,256]{1,0:T(8,128)S(1)} %get-tuple-element.49.crow_ref, ...), custom_call_target="tpu_custom_call" | custom-call | tf_op jit(solution)/shard_map/pallas_call | solution.py:549
  17.6 1.4 %collective-permute-start.8 = (f32[64,256]{1,0:T(8,128)S(1)}, f32[64,256]{1,0:T(8,128)S(1)}, u32[]{:S(2)}, u32[]{:S(2)}) collective-permute-start(f32[64,256]{1,0:T(8,128)S(1)} %get-tuple-element.54.own_ref), channel_id=1, source_target_pairs={{0,16},{8,24},{16,0},{24,8},{1,17},{9,25},{17,1},{25,9},{2,18},{10... | collective-permute-start | bytes 196616 | tf_op jit(solution)/shard_map/ppermute | solution.py:622
  19.0 0.0 collective-permute-start.7
  19.0 0.8 %collective-permute-start.6 = (f32[64,256]{1,0:T(8,128)S(1)}, f32[64,256]{1,0:T(8,128)S(1)}, u32[]{:S(2)}, u32[]{:S(2)}) collective-permute-start(f32[64,256]{1,0:T(8,128)S(1)} %get-tuple-element.54.own_ref), channel_id=1, source_target_pairs={{0,24},{8,16},{16,8},{24,0},{1,25},{9,17},{17,9},{25,1},{2,26},{10... | collective-permute-start | bytes 196616 | tf_op jit(solution)/shard_map/ppermute | solution.py:621
  19.8 0.0 collective-permute-done.4.ra_ref
  19.8 0.9 %collective-permute-done.5.rb_ref = f32[16,1024]{1,0:T(8,128)S(1)} collective-permute-done((f32[16,1024]{1,0:T(8,128)S(1)}, f32[16,1024]{1,0:T(8,128)S(1)}, u32[]{:S(2)}, u32[]{:S(2)}) %collective-permute-start.5) | collective-permute-done | bytes 65568 | tf_op jit(solution)/shard_map/ppermute | solution.py:617
  20.8 2.4 %shard_map.109 = (f32[12,64,256]{2,1,0:T(8,128)}, f32[4,64,256]{2,1,0:T(8,128)S(1)}, f32[128,128]{1,0:T(8,128)S(1)}) custom-call(f32[12,64,256]{2,1,0:T(8,128)S(1)} %get-tuple-element.43.after_ref.temp_ref, f32[12,64,256]{2,1,0:T(8,128)S(1)} %get-tuple-element.35.kappa_ref, f32[12,64,256]{2,1,0:T(8,128)S(1)} %get-tuple-element.36.slope_ref, ...), custom_call_target="tpu_custom_call" | custom-call | flops 5898240 | bytes 7077888 | tf_op jit(solution)/shard_map/pallas_call | solution.py:549
  23.2 0.0 collective-permute-done.8.relay_ref
  23.2 0.0 collective-permute-done.7.core_ref
  23.3 0.0 collective-permute-done.6.cross_ref
  23.3 0.9 %shard_map.110 = (f32[12,64,256]{2,1,0:T(8,128)}, f32[64,256]{1,0:T(8,128)}) custom-call(f32[12,64,256]{2,1,0:T(8,128)} %get-tuple-element.52.part_hbm, f32[4,64,256]{2,1,0:T(8,128)S(1)} %get-tuple-element.53.tail_ref, f32[64,256]{1,0:T(8,128)S(1)} %get-tuple-element.54.own_ref, ...), custom_call_target="tpu_custom_call", output_to_operand_aliasing={{0}: (0, {})} | custom-call | tf_op jit(solution)/shard_map/pallas_call | solution.py:549
Async XLA Ops:
  2.2 6.5 %collective-permute-start = (f32[136,256]{1,0:T(8,128)S(1)}, f32[136,256]{1,0:T(8,128)S(1)}, u32[]{:S(2)}, u32[]{:S(2)}) collective-permute-start(f32[136,256]{1,0:T(8,128)S(1)} %get-tuple-element.29), channel_id=1, source_target_pairs={{0,24},{8,16},{16,8},{24,0},{1,25},{9,17},{17,9},{25,1},{2,26},{10... | collective-permute-start | bytes 417800 | tf_op jit(solution)/shard_map/ppermute | solution.py:586
  4.6 6.1 %collective-permute-start.2 = (f32[184,256]{1,0:T(8,128)S(1)}, f32[184,256]{1,0:T(8,128)S(1)}, u32[]{:S(2)}, u32[]{:S(2)}) collective-permute-start(f32[184,256]{1,0:T(8,128)S(1)} %get-tuple-element.37.own_ref), channel_id=1, source_target_pairs={{0,8},{8,0},{16,24},{24,16},{1,9},{9,1},{17,25},{25,17},{2,10},{10... | collective-permute-start | bytes 565256 | tf_op jit(solution)/shard_map/ppermute | solution.py:588
  5.3 3.4 %collective-permute-start.1 = (f32[48,256]{1,0:T(8,128)S(1)}, f32[48,256]{1,0:T(8,128)S(1)}, u32[]{:S(2)}, u32[]{:S(2)}) collective-permute-start(f32[48,256]{1,0:T(8,128)S(1)} %get-tuple-element.30), channel_id=1, source_target_pairs={{8,16},{16,8},{9,17},{17,9},{10,18},{18,10},{11,19},{19,11},{12,20... | collective-permute-start | bytes 147464 | tf_op jit(solution)/shard_map/ppermute | solution.py:587
  8.7 3.0 %collective-permute-start.3 = (f32[136,256]{1,0:T(8,128)S(1)}, f32[136,256]{1,0:T(8,128)S(1)}, u32[]{:S(2)}, u32[]{:S(2)}) collective-permute-start(f32[136,256]{1,0:T(8,128)S(1)} %collective-permute-done.cross_ref), channel_id=1, source_target_pairs={{0,8},{8,0},{16,24},{24,16},{1,9},{9,1},{17,25},{25,17},{2,10},{10... | collective-permute-start | bytes 417800 | tf_op jit(solution)/shard_map/ppermute | solution.py:598
  12.2 7.6 %collective-permute-start.4 = (f32[16,1024]{1,0:T(8,128)S(1)}, f32[16,1024]{1,0:T(8,128)S(1)}, u32[]{:S(2)}, u32[]{:S(2)}) collective-permute-start(f32[16,1024]{1,0:T(8,128)S(1)} %get-tuple-element.46.sa_ref), channel_id=1, source_target_pairs={{0,1},{1,0},{2,3},{3,2},{4,5},{5,4},{6,7},{7,6},{8,9},{9,8},{10,11... | collective-permute-start | bytes 196616 | tf_op jit(solution)/shard_map/ppermute | solution.py:616
  13.8 7.0 %collective-permute-start.5 = (f32[16,1024]{1,0:T(8,128)S(1)}, f32[16,1024]{1,0:T(8,128)S(1)}, u32[]{:S(2)}, u32[]{:S(2)}) collective-permute-start(f32[16,1024]{1,0:T(8,128)S(1)} %get-tuple-element.47.sb_ref), channel_id=1, source_target_pairs={{1,2},{2,1},{3,4},{4,3},{5,6},{6,5},{7,0},{0,7},{9,10},{10,9},{11,... | collective-permute-start | bytes 196616 | tf_op jit(solution)/shard_map/ppermute | solution.py:617
  17.6 5.6 %collective-permute-start.8 = (f32[64,256]{1,0:T(8,128)S(1)}, f32[64,256]{1,0:T(8,128)S(1)}, u32[]{:S(2)}, u32[]{:S(2)}) collective-permute-start(f32[64,256]{1,0:T(8,128)S(1)} %get-tuple-element.54.own_ref), channel_id=1, source_target_pairs={{0,16},{8,24},{16,0},{24,8},{1,17},{9,25},{17,1},{25,9},{2,18},{10... | collective-permute-start | bytes 196616 | tf_op jit(solution)/shard_map/ppermute | solution.py:622
  19.0 4.2 %collective-permute-start.7 = (f32[64,256]{1,0:T(8,128)S(1)}, f32[64,256]{1,0:T(8,128)S(1)}, u32[]{:S(2)}, u32[]{:S(2)}) collective-permute-start(f32[64,256]{1,0:T(8,128)S(1)} %get-tuple-element.54.own_ref), channel_id=1, source_target_pairs={{0,8},{8,0},{16,24},{24,16},{1,9},{9,1},{17,25},{25,17},{2,10},{10... | collective-permute-start | bytes 196616 | tf_op jit(solution)/shard_map/ppermute | solution.py:623
  19.0 4.2 %collective-permute-start.6 = (f32[64,256]{1,0:T(8,128)S(1)}, f32[64,256]{1,0:T(8,128)S(1)}, u32[]{:S(2)}, u32[]{:S(2)}) collective-permute-start(f32[64,256]{1,0:T(8,128)S(1)} %get-tuple-element.54.own_ref), channel_id=1, source_target_pairs={{0,24},{8,16},{16,8},{24,0},{1,25},{9,17},{17,9},{25,1},{2,26},{10... | collective-permute-start | bytes 196616 | tf_op jit(solution)/shard_map/ppermute | solution.py:621

commit v9 on v8

--- a/solution.py
+++ b/solution.py
@@ -621,7 +621,7 @@
     got_across = lax.ppermute(flow, "grp", across)
     got_over = lax.ppermute(flow, "grp", [(i, (i + groups // 2) % groups) for i in range(groups)])
     got_beside = lax.ppermute(flow, "grp", beside)
-    late = layers // 3
+    late = layers // 2
     out, tail, adds = call(
         close_kernel,
         (block, shape(late, rows, cols), shape(2 * rows, TILE)),

time: 24.3 us -> 24.1 us (level)
  no operation moved by 1% of the time
where the time goes in v9:
time: 24.1 us; the launch traced here: 23.9 us
  starting transfers between devices  13.1 us (54%)
  Pallas kernels  9.11 us (38%)
  waiting for transfers between devices  0.96 us (4%)
  between operations  0.72 us (3%)
    pallas_call x7, Pallas kernels, call(): pl.pallas_call(body, out_shape=outs, in_specs=[pl.BlockSpec(memory_space=...  9.11 us
    ppermute x1, starting transfers between devices, shards(): rb = lax.ppermute(sb, 'loop', pairs(places, 1, True))  3.55 us
    ppermute x1, starting transfers between devices, shards(): got_cross = lax.ppermute(cross, 'grp', across)  2.44 us
    ppermute x1, starting transfers between devices, shards(): relay = lax.ppermute(got_cross, 'grp', beside)  2.01 us
    ppermute x1, starting transfers between devices, shards(): ra = lax.ppermute(sa, 'loop', pairs(places, 0, True))  1.59 us
    ppermute x1, starting transfers between devices, shards(): lax.ppermute(flow, 'grp', [(i, (i + groups // 2) % groups) for i in range...  1.37 us
    ppermute x1, waiting for transfers between devices, shards(): rb = lax.ppermute(sb, 'loop', pairs(places, 1, True))  0.94 us
    ppermute x1, starting transfers between devices, shards(): got_across = lax.ppermute(flow, 'grp', across)  0.83 us
  transfers between devices with their start and end apart: 9, of which 1 were waited for; matrix products, arithmetic and copies ran while one was open for 0% of the time, Pallas kernels for 26%

profile of v9, /device:TPU:0, one launch (start us, length us, event | category | flops | bytes accessed | tf_op | source)
XLA Modules:
  0.0 23.9 jit_solution(6761841361006358148)
XLA Ops:
  0.6 1.5 %shard_map.104 = (f32[184,256]{1,0:T(8,128)S(1)}, f32[136,256]{1,0:T(8,128)S(1)}, f32[48,256]{1,0:T(8,128)S(1)}, s32[1,256]{1,0:T(1,128)S(1)}, s32[1,256]{1,0:T(1,128)S(1)}) custom-call(f32[12,64,256]{2,1,0:T(8,128)} %temp_hbm.3, f32[12,64,256]{2,1,0:T(8,128)} %kappa_hbm.3, f32[12,64,256]{2,1,0:T(8,128)} %slope_hbm.3, f32[12,64,256]{2,1,0:T(8,128)} %power_hbm.3, ...), custom_call_target="tpu_custom_call" | custom-call | tf_op jit(solution)/shard_map/pallas_call | solution.py:549
  2.2 2.4 %collective-permute-start = (f32[136,256]{1,0:T(8,128)S(1)}, f32[136,256]{1,0:T(8,128)S(1)}, u32[]{:S(2)}, u32[]{:S(2)}) collective-permute-start(f32[136,256]{1,0:T(8,128)S(1)} %get-tuple-element.29), channel_id=1, source_target_pairs={{0,24},{8,16},{16,8},{24,0},{1,25},{9,17},{17,9},{25,1},{2,26},{10... | collective-permute-start | bytes 417800 | tf_op jit(solution)/shard_map/ppermute | solution.py:586
  4.6 0.7 %collective-permute-start.2 = (f32[184,256]{1,0:T(8,128)S(1)}, f32[184,256]{1,0:T(8,128)S(1)}, u32[]{:S(2)}, u32[]{:S(2)}) collective-permute-start(f32[184,256]{1,0:T(8,128)S(1)} %get-tuple-element.37.own_ref), channel_id=1, source_target_pairs={{0,8},{8,0},{16,24},{24,16},{1,9},{9,1},{17,25},{25,17},{2,10},{10... | collective-permute-start | bytes 565256 | tf_op jit(solution)/shard_map/ppermute | solution.py:588
  5.3 0.7 %collective-permute-start.1 = (f32[48,256]{1,0:T(8,128)S(1)}, f32[48,256]{1,0:T(8,128)S(1)}, u32[]{:S(2)}, u32[]{:S(2)}) collective-permute-start(f32[48,256]{1,0:T(8,128)S(1)} %get-tuple-element.30), channel_id=1, source_target_pairs={{8,16},{16,8},{9,17},{17,9},{10,18},{18,10},{11,19},{19,11},{12,20... | collective-permute-start | bytes 147464 | tf_op jit(solution)/shard_map/ppermute | solution.py:587
  5.9 2.7 %shard_map.105 = (f32[12,64,256]{2,1,0:T(8,128)S(1)}, f32[12,64,256]{2,1,0:T(8,128)S(1)}, f32[12,64,256]{2,1,0:T(8,128)S(1)}, f32[12,64,256]{2,1,0:T(8,128)S(1)}, f32[12,64,256]{2,1,0:T(8,128)S(1)}) custom-call(f32[12,64,256]{2,1,0:T(8,128)} %temp_hbm.3, f32[12,64,256]{2,1,0:T(8,128)} %kappa_hbm.3, f32[12,64,256]{2,1,0:T(8,128)} %slope_hbm.3, ...), custom_call_target="tpu_custom_call" | custom-call | flops 5898240 | bytes 7077888 | tf_op jit(solution)/shard_map/pallas_call | solution.py:549
  8.7 0.0 collective-permute-done.1.step_ref
  8.7 0.0 collective-permute-done.cross_ref
  8.7 2.0 %collective-permute-start.3 = (f32[136,256]{1,0:T(8,128)S(1)}, f32[136,256]{1,0:T(8,128)S(1)}, u32[]{:S(2)}, u32[]{:S(2)}) collective-permute-start(f32[136,256]{1,0:T(8,128)S(1)} %collective-permute-done.cross_ref), channel_id=1, source_target_pairs={{0,8},{8,0},{16,24},{24,16},{1,9},{9,1},{17,25},{25,17},{2,10},{10... | collective-permute-start | bytes 417800 | tf_op jit(solution)/shard_map/ppermute | solution.py:598
  10.7 0.0 collective-permute-done.2.core_ref
  10.7 1.0 %shard_map.106 = (f32[12,64,256]{2,1,0:T(8,128)S(1)}, f32[96,256]{1,0:T(8,128)S(1)}, f32[16,768]{1,0:T(8,128)S(1)}) custom-call(f32[12,64,256]{2,1,0:T(8,128)S(1)} %get-tuple-element.33.first_ref, f32[12,64,256]{2,1,0:T(8,128)S(1)} %get-tuple-element.34.temp_ref, f32[12,64,256]{2,1,0:T(8,128)S(1)} %get-tuple-element.35.kappa_ref, ...), custom_call_target="tpu_custom_call" | custom-call | flops 5898240 | bytes 7077888 | tf_op jit(solution)/shard_map/pallas_call | solution.py:549
  11.7 0.0 collective-permute-done.3.relay_ref
  11.7 0.6 %shard_map.107 = (f32[12,64,256]{2,1,0:T(8,128)S(1)}, f32[96,256]{1,0:T(8,128)S(1)}, f32[16,1024]{1,0:T(8,128)S(1)}, f32[16,1024]{1,0:T(8,128)S(1)}, f32[128,256]{1,0:T(8,128)S(1)}, /*index=5*/f32[8,256]{1,0:T(8,128)S(1)}) custom-call(f32[12,64,256]{2,1,0:T(8,128)S(1)} %get-tuple-element.39.old_ref, ...), custom_call_target="tpu_custom_call", output_to_operand_aliasing={{0}: (0, {}), {1}: (1, {})} | custom-call | tf_op jit(solution)/shard_map/pallas_call | solution.py:549
  12.2 1.6 %collective-permute-start.4 = (f32[16,1024]{1,0:T(8,128)S(1)}, f32[16,1024]{1,0:T(8,128)S(1)}, u32[]{:S(2)}, u32[]{:S(2)}) collective-permute-start(f32[16,1024]{1,0:T(8,128)S(1)} %get-tuple-element.46.sa_ref), channel_id=1, source_target_pairs={{0,1},{1,0},{2,3},{3,2},{4,5},{5,4},{6,7},{7,6},{8,9},{9,8},{10,11... | collective-permute-start | bytes 196616 | tf_op jit(solution)/shard_map/ppermute | solution.py:616
  13.8 3.5 %collective-permute-start.5 = (f32[16,1024]{1,0:T(8,128)S(1)}, f32[16,1024]{1,0:T(8,128)S(1)}, u32[]{:S(2)}, u32[]{:S(2)}) collective-permute-start(f32[16,1024]{1,0:T(8,128)S(1)} %get-tuple-element.47.sb_ref), channel_id=1, source_target_pairs={{1,2},{2,1},{3,4},{4,3},{5,6},{6,5},{7,0},{0,7},{9,10},{10,9},{11,... | collective-permute-start | bytes 196616 | tf_op jit(solution)/shard_map/ppermute | solution.py:617
  17.4 0.3 %shard_map.108 = (f32[64,256]{1,0:T(8,128)S(1)}, f32[64,256]{1,0:T(8,128)S(1)}) custom-call(f32[128,256]{1,0:T(8,128)S(1)} %get-tuple-element.48.fw_ref, f32[12,64,256]{2,1,0:T(8,128)S(1)} %get-tuple-element.34.temp_ref, f32[12,64,256]{2,1,0:T(8,128)S(1)} %get-tuple-element.43.after_ref.temp_ref, f32[8,256]{1,0:T(8,128)S(1)} %get-tuple-element.49.crow_ref, ...), custom_call_target="tpu_custom_call" | custom-call | tf_op jit(solution)/shard_map/pallas_call | solution.py:549
  17.6 1.4 %collective-permute-start.8 = (f32[64,256]{1,0:T(8,128)S(1)}, f32[64,256]{1,0:T(8,128)S(1)}, u32[]{:S(2)}, u32[]{:S(2)}) collective-permute-start(f32[64,256]{1,0:T(8,128)S(1)} %get-tuple-element.54.own_ref), channel_id=1, source_target_pairs={{0,16},{8,24},{16,0},{24,8},{1,17},{9,25},{17,1},{25,9},{2,18},{10... | collective-permute-start | bytes 196616 | tf_op jit(solution)/shard_map/ppermute | solution.py:622
  19.0 0.0 collective-permute-start.7
  19.0 0.8 %collective-permute-start.6 = (f32[64,256]{1,0:T(8,128)S(1)}, f32[64,256]{1,0:T(8,128)S(1)}, u32[]{:S(2)}, u32[]{:S(2)}) collective-permute-start(f32[64,256]{1,0:T(8,128)S(1)} %get-tuple-element.54.own_ref), channel_id=1, source_target_pairs={{0,24},{8,16},{16,8},{24,0},{1,25},{9,17},{17,9},{25,1},{2,26},{10... | collective-permute-start | bytes 196616 | tf_op jit(solution)/shard_map/ppermute | solution.py:621
  19.9 0.0 collective-permute-done.4.ra_ref
  19.9 0.9 %collective-permute-done.5.rb_ref = f32[16,1024]{1,0:T(8,128)S(1)} collective-permute-done((f32[16,1024]{1,0:T(8,128)S(1)}, f32[16,1024]{1,0:T(8,128)S(1)}, u32[]{:S(2)}, u32[]{:S(2)}) %collective-permute-start.5) | collective-permute-done | bytes 65568 | tf_op jit(solution)/shard_map/ppermute | solution.py:617
  20.8 2.2 %shard_map.109 = (f32[12,64,256]{2,1,0:T(8,128)}, f32[6,64,256]{2,1,0:T(8,128)S(1)}, f32[128,128]{1,0:T(8,128)S(1)}) custom-call(f32[12,64,256]{2,1,0:T(8,128)S(1)} %get-tuple-element.43.after_ref.temp_ref, f32[12,64,256]{2,1,0:T(8,128)S(1)} %get-tuple-element.35.kappa_ref, f32[12,64,256]{2,1,0:T(8,128)S(1)} %get-tuple-element.36.slope_ref, ...), custom_call_target="tpu_custom_call" | custom-call | flops 5898240 | bytes 7077888 | tf_op jit(solution)/shard_map/pallas_call | solution.py:549
  23.0 0.0 collective-permute-done.8.relay_ref
  23.0 0.0 collective-permute-done.7.core_ref
  23.0 0.0 collective-permute-done.6.cross_ref
  23.0 0.9 %shard_map.110 = (f32[12,64,256]{2,1,0:T(8,128)}, f32[64,256]{1,0:T(8,128)}) custom-call(f32[12,64,256]{2,1,0:T(8,128)} %get-tuple-element.52.part_hbm, f32[6,64,256]{2,1,0:T(8,128)S(1)} %get-tuple-element.53.tail_ref, f32[64,256]{1,0:T(8,128)S(1)} %get-tuple-element.54.own_ref, ...), custom_call_target="tpu_custom_call", output_to_operand_aliasing={{0}: (0, {})} | custom-call | tf_op jit(solution)/shard_map/pallas_call | solution.py:549
Async XLA Ops:
  2.2 6.5 %collective-permute-start = (f32[136,256]{1,0:T(8,128)S(1)}, f32[136,256]{1,0:T(8,128)S(1)}, u32[]{:S(2)}, u32[]{:S(2)}) collective-permute-start(f32[136,256]{1,0:T(8,128)S(1)} %get-tuple-element.29), channel_id=1, source_target_pairs={{0,24},{8,16},{16,8},{24,0},{1,25},{9,17},{17,9},{25,1},{2,26},{10... | collective-permute-start | bytes 417800 | tf_op jit(solution)/shard_map/ppermute | solution.py:586
  4.6 6.1 %collective-permute-start.2 = (f32[184,256]{1,0:T(8,128)S(1)}, f32[184,256]{1,0:T(8,128)S(1)}, u32[]{:S(2)}, u32[]{:S(2)}) collective-permute-start(f32[184,256]{1,0:T(8,128)S(1)} %get-tuple-element.37.own_ref), channel_id=1, source_target_pairs={{0,8},{8,0},{16,24},{24,16},{1,9},{9,1},{17,25},{25,17},{2,10},{10... | collective-permute-start | bytes 565256 | tf_op jit(solution)/shard_map/ppermute | solution.py:588
  5.3 3.4 %collective-permute-start.1 = (f32[48,256]{1,0:T(8,128)S(1)}, f32[48,256]{1,0:T(8,128)S(1)}, u32[]{:S(2)}, u32[]{:S(2)}) collective-permute-start(f32[48,256]{1,0:T(8,128)S(1)} %get-tuple-element.30), channel_id=1, source_target_pairs={{8,16},{16,8},{9,17},{17,9},{10,18},{18,10},{11,19},{19,11},{12,20... | collective-permute-start | bytes 147464 | tf_op jit(solution)/shard_map/ppermute | solution.py:587
  8.7 3.0 %collective-permute-start.3 = (f32[136,256]{1,0:T(8,128)S(1)}, f32[136,256]{1,0:T(8,128)S(1)}, u32[]{:S(2)}, u32[]{:S(2)}) collective-permute-start(f32[136,256]{1,0:T(8,128)S(1)} %collective-permute-done.cross_ref), channel_id=1, source_target_pairs={{0,8},{8,0},{16,24},{24,16},{1,9},{9,1},{17,25},{25,17},{2,10},{10... | collective-permute-start | bytes 417800 | tf_op jit(solution)/shard_map/ppermute | solution.py:598
  12.2 7.6 %collective-permute-start.4 = (f32[16,1024]{1,0:T(8,128)S(1)}, f32[16,1024]{1,0:T(8,128)S(1)}, u32[]{:S(2)}, u32[]{:S(2)}) collective-permute-start(f32[16,1024]{1,0:T(8,128)S(1)} %get-tuple-element.46.sa_ref), channel_id=1, source_target_pairs={{0,1},{1,0},{2,3},{3,2},{4,5},{5,4},{6,7},{7,6},{8,9},{9,8},{10,11... | collective-permute-start | bytes 196616 | tf_op jit(solution)/shard_map/ppermute | solution.py:616
  13.8 7.0 %collective-permute-start.5 = (f32[16,1024]{1,0:T(8,128)S(1)}, f32[16,1024]{1,0:T(8,128)S(1)}, u32[]{:S(2)}, u32[]{:S(2)}) collective-permute-start(f32[16,1024]{1,0:T(8,128)S(1)} %get-tuple-element.47.sb_ref), channel_id=1, source_target_pairs={{1,2},{2,1},{3,4},{4,3},{5,6},{6,5},{7,0},{0,7},{9,10},{10,9},{11,... | collective-permute-start | bytes 196616 | tf_op jit(solution)/shard_map/ppermute | solution.py:617
  17.6 5.3 %collective-permute-start.8 = (f32[64,256]{1,0:T(8,128)S(1)}, f32[64,256]{1,0:T(8,128)S(1)}, u32[]{:S(2)}, u32[]{:S(2)}) collective-permute-start(f32[64,256]{1,0:T(8,128)S(1)} %get-tuple-element.54.own_ref), channel_id=1, source_target_pairs={{0,16},{8,24},{16,0},{24,8},{1,17},{9,25},{17,1},{25,9},{2,18},{10... | collective-permute-start | bytes 196616 | tf_op jit(solution)/shard_map/ppermute | solution.py:622
  19.0 4.0 %collective-permute-start.7 = (f32[64,256]{1,0:T(8,128)S(1)}, f32[64,256]{1,0:T(8,128)S(1)}, u32[]{:S(2)}, u32[]{:S(2)}) collective-permute-start(f32[64,256]{1,0:T(8,128)S(1)} %get-tuple-element.54.own_ref), channel_id=1, source_target_pairs={{0,8},{8,0},{16,24},{24,16},{1,9},{9,1},{17,25},{25,17},{2,10},{10... | collective-permute-start | bytes 196616 | tf_op jit(solution)/shard_map/ppermute | solution.py:623
  19.0 4.0 %collective-permute-start.6 = (f32[64,256]{1,0:T(8,128)S(1)}, f32[64,256]{1,0:T(8,128)S(1)}, u32[]{:S(2)}, u32[]{:S(2)}) collective-permute-start(f32[64,256]{1,0:T(8,128)S(1)} %get-tuple-element.54.own_ref), channel_id=1, source_target_pairs={{0,24},{8,16},{16,8},{24,0},{1,25},{9,17},{17,9},{25,1},{2,26},{10... | collective-permute-start | bytes 196616 | tf_op jit(solution)/shard_map/ppermute | solution.py:621

commit v10 on v9

--- a/solution.py
+++ b/solution.py
@@ -9,7 +9,7 @@
 courant = 0.5
 heat_gain = 0.5
 TILE = 128
-CHUNK = 4
+CHUNK = 3
 F32 = jnp.float32
 BF16 = jnp.bfloat16
 

time: 24.1 us -> 24.1 us (level)
  no operation moved by 1% of the time
where the time goes in v10:
time: 24.1 us; the launch traced here: 24 us
  starting transfers between devices  13.1 us (54%)
  Pallas kernels  9.2 us (38%)
  waiting for transfers between devices  0.96 us (4%)
  between operations  0.72 us (3%)
    pallas_call x7, Pallas kernels, call(): pl.pallas_call(body, out_shape=outs, in_specs=[pl.BlockSpec(memory_space=...  9.2 us
    ppermute x1, starting transfers between devices, shards(): rb = lax.ppermute(sb, 'loop', pairs(places, 1, True))  3.55 us
    ppermute x1, starting transfers between devices, shards(): got_cross = lax.ppermute(cross, 'grp', across)  2.44 us
    ppermute x1, starting transfers between devices, shards(): relay = lax.ppermute(got_cross, 'grp', beside)  1.92 us
    ppermute x1, starting transfers between devices, shards(): ra = lax.ppermute(sa, 'loop', pairs(places, 0, True))  1.63 us
    ppermute x1, starting transfers between devices, shards(): lax.ppermute(flow, 'grp', [(i, (i + groups // 2) % groups) for i in range...  1.37 us
    ppermute x1, waiting for transfers between devices, shards(): rb = lax.ppermute(sb, 'loop', pairs(places, 1, True))  0.94 us
    ppermute x1, starting transfers between devices, shards(): got_across = lax.ppermute(flow, 'grp', across)  0.83 us
  transfers between devices with their start and end apart: 9, of which 1 were waited for; matrix products, arithmetic and copies ran while one was open for 0% of the time, Pallas kernels for 26%

profile of v10, /device:TPU:0, one launch (start us, length us, event | category | flops | bytes accessed | tf_op | source)
XLA Modules:
  0.0 24.0 jit_solution(10710991093256202794)
XLA Ops:
  0.6 1.5 %shard_map.104 = (f32[184,256]{1,0:T(8,128)S(1)}, f32[136,256]{1,0:T(8,128)S(1)}, f32[48,256]{1,0:T(8,128)S(1)}, s32[1,256]{1,0:T(1,128)S(1)}, s32[1,256]{1,0:T(1,128)S(1)}) custom-call(f32[12,64,256]{2,1,0:T(8,128)} %temp_hbm.3, f32[12,64,256]{2,1,0:T(8,128)} %kappa_hbm.3, f32[12,64,256]{2,1,0:T(8,128)} %slope_hbm.3, f32[12,64,256]{2,1,0:T(8,128)} %power_hbm.3, ...), custom_call_target="tpu_custom_call" | custom-call | tf_op jit(solution)/shard_map/pallas_call | solution.py:549
  2.2 2.4 %collective-permute-start = (f32[136,256]{1,0:T(8,128)S(1)}, f32[136,256]{1,0:T(8,128)S(1)}, u32[]{:S(2)}, u32[]{:S(2)}) collective-permute-start(f32[136,256]{1,0:T(8,128)S(1)} %get-tuple-element.29), channel_id=1, source_target_pairs={{0,24},{8,16},{16,8},{24,0},{1,25},{9,17},{17,9},{25,1},{2,26},{10... | collective-permute-start | bytes 417800 | tf_op jit(solution)/shard_map/ppermute | solution.py:586
  4.6 0.7 %collective-permute-start.2 = (f32[184,256]{1,0:T(8,128)S(1)}, f32[184,256]{1,0:T(8,128)S(1)}, u32[]{:S(2)}, u32[]{:S(2)}) collective-permute-start(f32[184,256]{1,0:T(8,128)S(1)} %get-tuple-element.37.own_ref), channel_id=1, source_target_pairs={{0,8},{8,0},{16,24},{24,16},{1,9},{9,1},{17,25},{25,17},{2,10},{10... | collective-permute-start | bytes 565256 | tf_op jit(solution)/shard_map/ppermute | solution.py:588
  5.3 0.7 %collective-permute-start.1 = (f32[48,256]{1,0:T(8,128)S(1)}, f32[48,256]{1,0:T(8,128)S(1)}, u32[]{:S(2)}, u32[]{:S(2)}) collective-permute-start(f32[48,256]{1,0:T(8,128)S(1)} %get-tuple-element.30), channel_id=1, source_target_pairs={{8,16},{16,8},{9,17},{17,9},{10,18},{18,10},{11,19},{19,11},{12,20... | collective-permute-start | bytes 147464 | tf_op jit(solution)/shard_map/ppermute | solution.py:587
  5.9 2.8 %shard_map.105 = (f32[12,64,256]{2,1,0:T(8,128)S(1)}, f32[12,64,256]{2,1,0:T(8,128)S(1)}, f32[12,64,256]{2,1,0:T(8,128)S(1)}, f32[12,64,256]{2,1,0:T(8,128)S(1)}, f32[12,64,256]{2,1,0:T(8,128)S(1)}) custom-call(f32[12,64,256]{2,1,0:T(8,128)} %temp_hbm.3, f32[12,64,256]{2,1,0:T(8,128)} %kappa_hbm.3, f32[12,64,256]{2,1,0:T(8,128)} %slope_hbm.3, ...), custom_call_target="tpu_custom_call" | custom-call | flops 5898240 | bytes 7077888 | tf_op jit(solution)/shard_map/pallas_call | solution.py:549
  8.7 0.0 collective-permute-done.1.step_ref
  8.8 0.0 collective-permute-done.cross_ref
  8.8 1.9 %collective-permute-start.3 = (f32[136,256]{1,0:T(8,128)S(1)}, f32[136,256]{1,0:T(8,128)S(1)}, u32[]{:S(2)}, u32[]{:S(2)}) collective-permute-start(f32[136,256]{1,0:T(8,128)S(1)} %collective-permute-done.cross_ref), channel_id=1, source_target_pairs={{0,8},{8,0},{16,24},{24,16},{1,9},{9,1},{17,25},{25,17},{2,10},{10... | collective-permute-start | bytes 417800 | tf_op jit(solution)/shard_map/ppermute | solution.py:598
  10.7 0.0 collective-permute-done.2.core_ref
  10.7 1.0 %shard_map.106 = (f32[12,64,256]{2,1,0:T(8,128)S(1)}, f32[96,256]{1,0:T(8,128)S(1)}, f32[16,768]{1,0:T(8,128)S(1)}) custom-call(f32[12,64,256]{2,1,0:T(8,128)S(1)} %get-tuple-element.33.first_ref, f32[12,64,256]{2,1,0:T(8,128)S(1)} %get-tuple-element.34.temp_ref, f32[12,64,256]{2,1,0:T(8,128)S(1)} %get-tuple-element.35.kappa_ref, ...), custom_call_target="tpu_custom_call" | custom-call | flops 5898240 | bytes 7077888 | tf_op jit(solution)/shard_map/pallas_call | solution.py:549
  11.7 0.0 collective-permute-done.3.relay_ref
  11.7 0.6 %shard_map.107 = (f32[12,64,256]{2,1,0:T(8,128)S(1)}, f32[96,256]{1,0:T(8,128)S(1)}, f32[16,1024]{1,0:T(8,128)S(1)}, f32[16,1024]{1,0:T(8,128)S(1)}, f32[128,256]{1,0:T(8,128)S(1)}, /*index=5*/f32[8,256]{1,0:T(8,128)S(1)}) custom-call(f32[12,64,256]{2,1,0:T(8,128)S(1)} %get-tuple-element.39.old_ref, ...), custom_call_target="tpu_custom_call", output_to_operand_aliasing={{0}: (0, {}), {1}: (1, {})} | custom-call | tf_op jit(solution)/shard_map/pallas_call | solution.py:549
  12.2 1.6 %collective-permute-start.4 = (f32[16,1024]{1,0:T(8,128)S(1)}, f32[16,1024]{1,0:T(8,128)S(1)}, u32[]{:S(2)}, u32[]{:S(2)}) collective-permute-start(f32[16,1024]{1,0:T(8,128)S(1)} %get-tuple-element.46.sa_ref), channel_id=1, source_target_pairs={{0,1},{1,0},{2,3},{3,2},{4,5},{5,4},{6,7},{7,6},{8,9},{9,8},{10,11... | collective-permute-start | bytes 196616 | tf_op jit(solution)/shard_map/ppermute | solution.py:616
  13.9 3.5 %collective-permute-start.5 = (f32[16,1024]{1,0:T(8,128)S(1)}, f32[16,1024]{1,0:T(8,128)S(1)}, u32[]{:S(2)}, u32[]{:S(2)}) collective-permute-start(f32[16,1024]{1,0:T(8,128)S(1)} %get-tuple-element.47.sb_ref), channel_id=1, source_target_pairs={{1,2},{2,1},{3,4},{4,3},{5,6},{6,5},{7,0},{0,7},{9,10},{10,9},{11,... | collective-permute-start | bytes 196616 | tf_op jit(solution)/shard_map/ppermute | solution.py:617
  17.4 0.3 %shard_map.108 = (f32[64,256]{1,0:T(8,128)S(1)}, f32[64,256]{1,0:T(8,128)S(1)}) custom-call(f32[128,256]{1,0:T(8,128)S(1)} %get-tuple-element.48.fw_ref, f32[12,64,256]{2,1,0:T(8,128)S(1)} %get-tuple-element.34.temp_ref, f32[12,64,256]{2,1,0:T(8,128)S(1)} %get-tuple-element.43.after_ref.temp_ref, f32[8,256]{1,0:T(8,128)S(1)} %get-tuple-element.49.crow_ref, ...), custom_call_target="tpu_custom_call" | custom-call | tf_op jit(solution)/shard_map/pallas_call | solution.py:549
  17.7 1.4 %collective-permute-start.8 = (f32[64,256]{1,0:T(8,128)S(1)}, f32[64,256]{1,0:T(8,128)S(1)}, u32[]{:S(2)}, u32[]{:S(2)}) collective-permute-start(f32[64,256]{1,0:T(8,128)S(1)} %get-tuple-element.54.own_ref), channel_id=1, source_target_pairs={{0,16},{8,24},{16,0},{24,8},{1,17},{9,25},{17,1},{25,9},{2,18},{10... | collective-permute-start | bytes 196616 | tf_op jit(solution)/shard_map/ppermute | solution.py:622
  19.1 0.0 collective-permute-start.7
  19.1 0.8 %collective-permute-start.6 = (f32[64,256]{1,0:T(8,128)S(1)}, f32[64,256]{1,0:T(8,128)S(1)}, u32[]{:S(2)}, u32[]{:S(2)}) collective-permute-start(f32[64,256]{1,0:T(8,128)S(1)} %get-tuple-element.54.own_ref), channel_id=1, source_target_pairs={{0,24},{8,16},{16,8},{24,0},{1,25},{9,17},{17,9},{25,1},{2,26},{10... | collective-permute-start | bytes 196616 | tf_op jit(solution)/shard_map/ppermute | solution.py:621
  19.9 0.0 collective-permute-done.4.ra_ref
  19.9 0.9 %collective-permute-done.5.rb_ref = f32[16,1024]{1,0:T(8,128)S(1)} collective-permute-done((f32[16,1024]{1,0:T(8,128)S(1)}, f32[16,1024]{1,0:T(8,128)S(1)}, u32[]{:S(2)}, u32[]{:S(2)}) %collective-permute-start.5) | collective-permute-done | bytes 65568 | tf_op jit(solution)/shard_map/ppermute | solution.py:617
  20.8 2.2 %shard_map.109 = (f32[12,64,256]{2,1,0:T(8,128)}, f32[6,64,256]{2,1,0:T(8,128)S(1)}, f32[128,128]{1,0:T(8,128)S(1)}) custom-call(f32[12,64,256]{2,1,0:T(8,128)S(1)} %get-tuple-element.43.after_ref.temp_ref, f32[12,64,256]{2,1,0:T(8,128)S(1)} %get-tuple-element.35.kappa_ref, f32[12,64,256]{2,1,0:T(8,128)S(1)} %get-tuple-element.36.slope_ref, ...), custom_call_target="tpu_custom_call" | custom-call | flops 5898240 | bytes 7077888 | tf_op jit(solution)/shard_map/pallas_call | solution.py:549
  23.0 0.0 collective-permute-done.8.relay_ref
  23.0 0.0 collective-permute-done.7.core_ref
  23.1 0.0 collective-permute-done.6.cross_ref
  23.1 0.9 %shard_map.110 = (f32[12,64,256]{2,1,0:T(8,128)}, f32[64,256]{1,0:T(8,128)}) custom-call(f32[12,64,256]{2,1,0:T(8,128)} %get-tuple-element.52.part_hbm, f32[6,64,256]{2,1,0:T(8,128)S(1)} %get-tuple-element.53.tail_ref, f32[64,256]{1,0:T(8,128)S(1)} %get-tuple-element.54.own_ref, ...), custom_call_target="tpu_custom_call", output_to_operand_aliasing={{0}: (0, {})} | custom-call | tf_op jit(solution)/shard_map/pallas_call | solution.py:549
Async XLA Ops:
  2.2 6.6 %collective-permute-start = (f32[136,256]{1,0:T(8,128)S(1)}, f32[136,256]{1,0:T(8,128)S(1)}, u32[]{:S(2)}, u32[]{:S(2)}) collective-permute-start(f32[136,256]{1,0:T(8,128)S(1)} %get-tuple-element.29), channel_id=1, source_target_pairs={{0,24},{8,16},{16,8},{24,0},{1,25},{9,17},{17,9},{25,1},{2,26},{10... | collective-permute-start | bytes 417800 | tf_op jit(solution)/shard_map/ppermute | solution.py:586
  4.6 6.1 %collective-permute-start.2 = (f32[184,256]{1,0:T(8,128)S(1)}, f32[184,256]{1,0:T(8,128)S(1)}, u32[]{:S(2)}, u32[]{:S(2)}) collective-permute-start(f32[184,256]{1,0:T(8,128)S(1)} %get-tuple-element.37.own_ref), channel_id=1, source_target_pairs={{0,8},{8,0},{16,24},{24,16},{1,9},{9,1},{17,25},{25,17},{2,10},{10... | collective-permute-start | bytes 565256 | tf_op jit(solution)/shard_map/ppermute | solution.py:588
  5.3 3.5 %collective-permute-start.1 = (f32[48,256]{1,0:T(8,128)S(1)}, f32[48,256]{1,0:T(8,128)S(1)}, u32[]{:S(2)}, u32[]{:S(2)}) collective-permute-start(f32[48,256]{1,0:T(8,128)S(1)} %get-tuple-element.30), channel_id=1, source_target_pairs={{8,16},{16,8},{9,17},{17,9},{10,18},{18,10},{11,19},{19,11},{12,20... | collective-permute-start | bytes 147464 | tf_op jit(solution)/shard_map/ppermute | solution.py:587
  8.8 2.9 %collective-permute-start.3 = (f32[136,256]{1,0:T(8,128)S(1)}, f32[136,256]{1,0:T(8,128)S(1)}, u32[]{:S(2)}, u32[]{:S(2)}) collective-permute-start(f32[136,256]{1,0:T(8,128)S(1)} %collective-permute-done.cross_ref), channel_id=1, source_target_pairs={{0,8},{8,0},{16,24},{24,16},{1,9},{9,1},{17,25},{25,17},{2,10},{10... | collective-permute-start | bytes 417800 | tf_op jit(solution)/shard_map/ppermute | solution.py:598
  12.2 7.7 %collective-permute-start.4 = (f32[16,1024]{1,0:T(8,128)S(1)}, f32[16,1024]{1,0:T(8,128)S(1)}, u32[]{:S(2)}, u32[]{:S(2)}) collective-permute-start(f32[16,1024]{1,0:T(8,128)S(1)} %get-tuple-element.46.sa_ref), channel_id=1, source_target_pairs={{0,1},{1,0},{2,3},{3,2},{4,5},{5,4},{6,7},{7,6},{8,9},{9,8},{10,11... | collective-permute-start | bytes 196616 | tf_op jit(solution)/shard_map/ppermute | solution.py:616
  13.9 7.0 %collective-permute-start.5 = (f32[16,1024]{1,0:T(8,128)S(1)}, f32[16,1024]{1,0:T(8,128)S(1)}, u32[]{:S(2)}, u32[]{:S(2)}) collective-permute-start(f32[16,1024]{1,0:T(8,128)S(1)} %get-tuple-element.47.sb_ref), channel_id=1, source_target_pairs={{1,2},{2,1},{3,4},{4,3},{5,6},{6,5},{7,0},{0,7},{9,10},{10,9},{11,... | collective-permute-start | bytes 196616 | tf_op jit(solution)/shard_map/ppermute | solution.py:617
  17.7 5.3 %collective-permute-start.8 = (f32[64,256]{1,0:T(8,128)S(1)}, f32[64,256]{1,0:T(8,128)S(1)}, u32[]{:S(2)}, u32[]{:S(2)}) collective-permute-start(f32[64,256]{1,0:T(8,128)S(1)} %get-tuple-element.54.own_ref), channel_id=1, source_target_pairs={{0,16},{8,24},{16,0},{24,8},{1,17},{9,25},{17,1},{25,9},{2,18},{10... | collective-permute-start | bytes 196616 | tf_op jit(solution)/shard_map/ppermute | solution.py:622
  19.1 4.0 %collective-permute-start.7 = (f32[64,256]{1,0:T(8,128)S(1)}, f32[64,256]{1,0:T(8,128)S(1)}, u32[]{:S(2)}, u32[]{:S(2)}) collective-permute-start(f32[64,256]{1,0:T(8,128)S(1)} %get-tuple-element.54.own_ref), channel_id=1, source_target_pairs={{0,8},{8,0},{16,24},{24,16},{1,9},{9,1},{17,25},{25,17},{2,10},{10... | collective-permute-start | bytes 196616 | tf_op jit(solution)/shard_map/ppermute | solution.py:623
  19.1 4.0 %collective-permute-start.6 = (f32[64,256]{1,0:T(8,128)S(1)}, f32[64,256]{1,0:T(8,128)S(1)}, u32[]{:S(2)}, u32[]{:S(2)}) collective-permute-start(f32[64,256]{1,0:T(8,128)S(1)} %get-tuple-element.54.own_ref), channel_id=1, source_target_pairs={{0,24},{8,16},{16,8},{24,0},{1,25},{9,17},{17,9},{25,1},{2,26},{10... | collective-permute-start | bytes 196616 | tf_op jit(solution)/shard_map/ppermute | solution.py:621

commit v11 on v9

--- a/solution.py
+++ b/solution.py
@@ -621,7 +621,7 @@
     got_across = lax.ppermute(flow, "grp", across)
     got_over = lax.ppermute(flow, "grp", [(i, (i + groups // 2) % groups) for i in range(groups)])
     got_beside = lax.ppermute(flow, "grp", beside)
-    late = layers // 2
+    late = 2 * layers // 3
     out, tail, adds = call(
         close_kernel,
         (block, shape(late, rows, cols), shape(2 * rows, TILE)),

time: 24.1 us -> 24.1 us (level)
  no operation moved by 1% of the time
where the time goes in v11:
time: 24.1 us; the launch traced here: 23.9 us
  starting transfers between devices  13.1 us (54%)
  Pallas kernels  9.09 us (38%)
  waiting for transfers between devices  0.96 us (4%)
  between operations  0.72 us (3%)
    pallas_call x7, Pallas kernels, call(): pl.pallas_call(body, out_shape=outs, in_specs=[pl.BlockSpec(memory_space=...  9.09 us
    ppermute x1, starting transfers between devices, shards(): rb = lax.ppermute(sb, 'loop', pairs(places, 1, True))  3.55 us
    ppermute x1, starting transfers between devices, shards(): got_cross = lax.ppermute(cross, 'grp', across)  2.44 us
    ppermute x1, starting transfers between devices, shards(): relay = lax.ppermute(got_cross, 'grp', beside)  2.01 us
    ppermute x1, starting transfers between devices, shards(): ra = lax.ppermute(sa, 'loop', pairs(places, 0, True))  1.58 us
    ppermute x1, starting transfers between devices, shards(): lax.ppermute(flow, 'grp', [(i, (i + groups // 2) % groups) for i in range...  1.37 us
    ppermute x1, waiting for transfers between devices, shards(): rb = lax.ppermute(sb, 'loop', pairs(places, 1, True))  0.94 us
    ppermute x1, starting transfers between devices, shards(): got_across = lax.ppermute(flow, 'grp', across)  0.83 us
  transfers between devices with their start and end apart: 9, of which 1 were waited for; matrix products, arithmetic and copies ran while one was open for 0% of the time, Pallas kernels for 26%

profile of v11, /device:TPU:0, one launch (start us, length us, event | category | flops | bytes accessed | tf_op | source)
XLA Modules:
  0.0 23.9 jit_solution(3878359017011173752)
XLA Ops:
  0.6 1.5 %shard_map.104 = (f32[184,256]{1,0:T(8,128)S(1)}, f32[136,256]{1,0:T(8,128)S(1)}, f32[48,256]{1,0:T(8,128)S(1)}, s32[1,256]{1,0:T(1,128)S(1)}, s32[1,256]{1,0:T(1,128)S(1)}) custom-call(f32[12,64,256]{2,1,0:T(8,128)} %temp_hbm.3, f32[12,64,256]{2,1,0:T(8,128)} %kappa_hbm.3, f32[12,64,256]{2,1,0:T(8,128)} %slope_hbm.3, f32[12,64,256]{2,1,0:T(8,128)} %power_hbm.3, ...), custom_call_target="tpu_custom_call" | custom-call | tf_op jit(solution)/shard_map/pallas_call | solution.py:549
  2.2 2.4 %collective-permute-start = (f32[136,256]{1,0:T(8,128)S(1)}, f32[136,256]{1,0:T(8,128)S(1)}, u32[]{:S(2)}, u32[]{:S(2)}) collective-permute-start(f32[136,256]{1,0:T(8,128)S(1)} %get-tuple-element.29), channel_id=1, source_target_pairs={{0,24},{8,16},{16,8},{24,0},{1,25},{9,17},{17,9},{25,1},{2,26},{10... | collective-permute-start | bytes 417800 | tf_op jit(solution)/shard_map/ppermute | solution.py:586
  4.6 0.7 %collective-permute-start.2 = (f32[184,256]{1,0:T(8,128)S(1)}, f32[184,256]{1,0:T(8,128)S(1)}, u32[]{:S(2)}, u32[]{:S(2)}) collective-permute-start(f32[184,256]{1,0:T(8,128)S(1)} %get-tuple-element.37.own_ref), channel_id=1, source_target_pairs={{0,8},{8,0},{16,24},{24,16},{1,9},{9,1},{17,25},{25,17},{2,10},{10... | collective-permute-start | bytes 565256 | tf_op jit(solution)/shard_map/ppermute | solution.py:588
  5.3 0.7 %collective-permute-start.1 = (f32[48,256]{1,0:T(8,128)S(1)}, f32[48,256]{1,0:T(8,128)S(1)}, u32[]{:S(2)}, u32[]{:S(2)}) collective-permute-start(f32[48,256]{1,0:T(8,128)S(1)} %get-tuple-element.30), channel_id=1, source_target_pairs={{8,16},{16,8},{9,17},{17,9},{10,18},{18,10},{11,19},{19,11},{12,20... | collective-permute-start | bytes 147464 | tf_op jit(solution)/shard_map/ppermute | solution.py:587
  5.9 2.7 %shard_map.105 = (f32[12,64,256]{2,1,0:T(8,128)S(1)}, f32[12,64,256]{2,1,0:T(8,128)S(1)}, f32[12,64,256]{2,1,0:T(8,128)S(1)}, f32[12,64,256]{2,1,0:T(8,128)S(1)}, f32[12,64,256]{2,1,0:T(8,128)S(1)}) custom-call(f32[12,64,256]{2,1,0:T(8,128)} %temp_hbm.3, f32[12,64,256]{2,1,0:T(8,128)} %kappa_hbm.3, f32[12,64,256]{2,1,0:T(8,128)} %slope_hbm.3, ...), custom_call_target="tpu_custom_call" | custom-call | flops 5898240 | bytes 7077888 | tf_op jit(solution)/shard_map/pallas_call | solution.py:549
  8.7 0.0 collective-permute-done.1.step_ref
  8.7 0.0 collective-permute-done.cross_ref
  8.7 2.0 %collective-permute-start.3 = (f32[136,256]{1,0:T(8,128)S(1)}, f32[136,256]{1,0:T(8,128)S(1)}, u32[]{:S(2)}, u32[]{:S(2)}) collective-permute-start(f32[136,256]{1,0:T(8,128)S(1)} %collective-permute-done.cross_ref), channel_id=1, source_target_pairs={{0,8},{8,0},{16,24},{24,16},{1,9},{9,1},{17,25},{25,17},{2,10},{10... | collective-permute-start | bytes 417800 | tf_op jit(solution)/shard_map/ppermute | solution.py:598
  10.7 0.0 collective-permute-done.2.core_ref
  10.7 1.0 %shard_map.106 = (f32[12,64,256]{2,1,0:T(8,128)S(1)}, f32[96,256]{1,0:T(8,128)S(1)}, f32[16,768]{1,0:T(8,128)S(1)}) custom-call(f32[12,64,256]{2,1,0:T(8,128)S(1)} %get-tuple-element.33.first_ref, f32[12,64,256]{2,1,0:T(8,128)S(1)} %get-tuple-element.34.temp_ref, f32[12,64,256]{2,1,0:T(8,128)S(1)} %get-tuple-element.35.kappa_ref, ...), custom_call_target="tpu_custom_call" | custom-call | flops 5898240 | bytes 7077888 | tf_op jit(solution)/shard_map/pallas_call | solution.py:549
  11.7 0.0 collective-permute-done.3.relay_ref
  11.7 0.6 %shard_map.107 = (f32[12,64,256]{2,1,0:T(8,128)S(1)}, f32[96,256]{1,0:T(8,128)S(1)}, f32[16,1024]{1,0:T(8,128)S(1)}, f32[16,1024]{1,0:T(8,128)S(1)}, f32[128,256]{1,0:T(8,128)S(1)}, /*index=5*/f32[8,256]{1,0:T(8,128)S(1)}) custom-call(f32[12,64,256]{2,1,0:T(8,128)S(1)} %get-tuple-element.39.old_ref, ...), custom_call_target="tpu_custom_call", output_to_operand_aliasing={{0}: (0, {}), {1}: (1, {})} | custom-call | tf_op jit(solution)/shard_map/pallas_call | solution.py:549
  12.2 1.6 %collective-permute-start.4 = (f32[16,1024]{1,0:T(8,128)S(1)}, f32[16,1024]{1,0:T(8,128)S(1)}, u32[]{:S(2)}, u32[]{:S(2)}) collective-permute-start(f32[16,1024]{1,0:T(8,128)S(1)} %get-tuple-element.46.sa_ref), channel_id=1, source_target_pairs={{0,1},{1,0},{2,3},{3,2},{4,5},{5,4},{6,7},{7,6},{8,9},{9,8},{10,11... | collective-permute-start | bytes 196616 | tf_op jit(solution)/shard_map/ppermute | solution.py:616
  13.8 3.5 %collective-permute-start.5 = (f32[16,1024]{1,0:T(8,128)S(1)}, f32[16,1024]{1,0:T(8,128)S(1)}, u32[]{:S(2)}, u32[]{:S(2)}) collective-permute-start(f32[16,1024]{1,0:T(8,128)S(1)} %get-tuple-element.47.sb_ref), channel_id=1, source_target_pairs={{1,2},{2,1},{3,4},{4,3},{5,6},{6,5},{7,0},{0,7},{9,10},{10,9},{11,... | collective-permute-start | bytes 196616 | tf_op jit(solution)/shard_map/ppermute | solution.py:617
  17.4 0.3 %shard_map.108 = (f32[64,256]{1,0:T(8,128)S(1)}, f32[64,256]{1,0:T(8,128)S(1)}) custom-call(f32[128,256]{1,0:T(8,128)S(1)} %get-tuple-element.48.fw_ref, f32[12,64,256]{2,1,0:T(8,128)S(1)} %get-tuple-element.34.temp_ref, f32[12,64,256]{2,1,0:T(8,128)S(1)} %get-tuple-element.43.after_ref.temp_ref, f32[8,256]{1,0:T(8,128)S(1)} %get-tuple-element.49.crow_ref, ...), custom_call_target="tpu_custom_call" | custom-call | tf_op jit(solution)/shard_map/pallas_call | solution.py:549
  17.6 1.4 %collective-permute-start.8 = (f32[64,256]{1,0:T(8,128)S(1)}, f32[64,256]{1,0:T(8,128)S(1)}, u32[]{:S(2)}, u32[]{:S(2)}) collective-permute-start(f32[64,256]{1,0:T(8,128)S(1)} %get-tuple-element.54.own_ref), channel_id=1, source_target_pairs={{0,16},{8,24},{16,0},{24,8},{1,17},{9,25},{17,1},{25,9},{2,18},{10... | collective-permute-start | bytes 196616 | tf_op jit(solution)/shard_map/ppermute | solution.py:622
  19.0 0.0 collective-permute-start.7
  19.0 0.8 %collective-permute-start.6 = (f32[64,256]{1,0:T(8,128)S(1)}, f32[64,256]{1,0:T(8,128)S(1)}, u32[]{:S(2)}, u32[]{:S(2)}) collective-permute-start(f32[64,256]{1,0:T(8,128)S(1)} %get-tuple-element.54.own_ref), channel_id=1, source_target_pairs={{0,24},{8,16},{16,8},{24,0},{1,25},{9,17},{17,9},{25,1},{2,26},{10... | collective-permute-start | bytes 196616 | tf_op jit(solution)/shard_map/ppermute | solution.py:621
  19.9 0.0 collective-permute-done.4.ra_ref
  19.9 0.9 %collective-permute-done.5.rb_ref = f32[16,1024]{1,0:T(8,128)S(1)} collective-permute-done((f32[16,1024]{1,0:T(8,128)S(1)}, f32[16,1024]{1,0:T(8,128)S(1)}, u32[]{:S(2)}, u32[]{:S(2)}) %collective-permute-start.5) | collective-permute-done | bytes 65568 | tf_op jit(solution)/shard_map/ppermute | solution.py:617
  20.8 2.2 %shard_map.109 = (f32[12,64,256]{2,1,0:T(8,128)}, f32[8,64,256]{2,1,0:T(8,128)S(1)}, f32[128,128]{1,0:T(8,128)S(1)}) custom-call(f32[12,64,256]{2,1,0:T(8,128)S(1)} %get-tuple-element.43.after_ref.temp_ref, f32[12,64,256]{2,1,0:T(8,128)S(1)} %get-tuple-element.35.kappa_ref, f32[12,64,256]{2,1,0:T(8,128)S(1)} %get-tuple-element.36.slope_ref, ...), custom_call_target="tpu_custom_call" | custom-call | flops 5898240 | bytes 7077888 | tf_op jit(solution)/shard_map/pallas_call | solution.py:549
  23.0 0.0 collective-permute-done.8.relay_ref
  23.0 0.0 collective-permute-done.7.core_ref
  23.0 0.0 collective-permute-done.6.cross_ref
  23.0 0.9 %shard_map.110 = (f32[12,64,256]{2,1,0:T(8,128)}, f32[64,256]{1,0:T(8,128)}) custom-call(f32[12,64,256]{2,1,0:T(8,128)} %get-tuple-element.52.part_hbm, f32[8,64,256]{2,1,0:T(8,128)S(1)} %get-tuple-element.53.tail_ref, f32[64,256]{1,0:T(8,128)S(1)} %get-tuple-element.54.own_ref, ...), custom_call_target="tpu_custom_call", output_to_operand_aliasing={{0}: (0, {})} | custom-call | tf_op jit(solution)/shard_map/pallas_call | solution.py:549
Async XLA Ops:
  2.2 6.5 %collective-permute-start = (f32[136,256]{1,0:T(8,128)S(1)}, f32[136,256]{1,0:T(8,128)S(1)}, u32[]{:S(2)}, u32[]{:S(2)}) collective-permute-start(f32[136,256]{1,0:T(8,128)S(1)} %get-tuple-element.29), channel_id=1, source_target_pairs={{0,24},{8,16},{16,8},{24,0},{1,25},{9,17},{17,9},{25,1},{2,26},{10... | collective-permute-start | bytes 417800 | tf_op jit(solution)/shard_map/ppermute | solution.py:586
  4.6 6.1 %collective-permute-start.2 = (f32[184,256]{1,0:T(8,128)S(1)}, f32[184,256]{1,0:T(8,128)S(1)}, u32[]{:S(2)}, u32[]{:S(2)}) collective-permute-start(f32[184,256]{1,0:T(8,128)S(1)} %get-tuple-element.37.own_ref), channel_id=1, source_target_pairs={{0,8},{8,0},{16,24},{24,16},{1,9},{9,1},{17,25},{25,17},{2,10},{10... | collective-permute-start | bytes 565256 | tf_op jit(solution)/shard_map/ppermute | solution.py:588
  5.3 3.4 %collective-permute-start.1 = (f32[48,256]{1,0:T(8,128)S(1)}, f32[48,256]{1,0:T(8,128)S(1)}, u32[]{:S(2)}, u32[]{:S(2)}) collective-permute-start(f32[48,256]{1,0:T(8,128)S(1)} %get-tuple-element.30), channel_id=1, source_target_pairs={{8,16},{16,8},{9,17},{17,9},{10,18},{18,10},{11,19},{19,11},{12,20... | collective-permute-start | bytes 147464 | tf_op jit(solution)/shard_map/ppermute | solution.py:587
  8.7 3.0 %collective-permute-start.3 = (f32[136,256]{1,0:T(8,128)S(1)}, f32[136,256]{1,0:T(8,128)S(1)}, u32[]{:S(2)}, u32[]{:S(2)}) collective-permute-start(f32[136,256]{1,0:T(8,128)S(1)} %collective-permute-done.cross_ref), channel_id=1, source_target_pairs={{0,8},{8,0},{16,24},{24,16},{1,9},{9,1},{17,25},{25,17},{2,10},{10... | collective-permute-start | bytes 417800 | tf_op jit(solution)/shard_map/ppermute | solution.py:598
  12.2 7.6 %collective-permute-start.4 = (f32[16,1024]{1,0:T(8,128)S(1)}, f32[16,1024]{1,0:T(8,128)S(1)}, u32[]{:S(2)}, u32[]{:S(2)}) collective-permute-start(f32[16,1024]{1,0:T(8,128)S(1)} %get-tuple-element.46.sa_ref), channel_id=1, source_target_pairs={{0,1},{1,0},{2,3},{3,2},{4,5},{5,4},{6,7},{7,6},{8,9},{9,8},{10,11... | collective-permute-start | bytes 196616 | tf_op jit(solution)/shard_map/ppermute | solution.py:616
  13.8 7.0 %collective-permute-start.5 = (f32[16,1024]{1,0:T(8,128)S(1)}, f32[16,1024]{1,0:T(8,128)S(1)}, u32[]{:S(2)}, u32[]{:S(2)}) collective-permute-start(f32[16,1024]{1,0:T(8,128)S(1)} %get-tuple-element.47.sb_ref), channel_id=1, source_target_pairs={{1,2},{2,1},{3,4},{4,3},{5,6},{6,5},{7,0},{0,7},{9,10},{10,9},{11,... | collective-permute-start | bytes 196616 | tf_op jit(solution)/shard_map/ppermute | solution.py:617
  17.6 5.3 %collective-permute-start.8 = (f32[64,256]{1,0:T(8,128)S(1)}, f32[64,256]{1,0:T(8,128)S(1)}, u32[]{:S(2)}, u32[]{:S(2)}) collective-permute-start(f32[64,256]{1,0:T(8,128)S(1)} %get-tuple-element.54.own_ref), channel_id=1, source_target_pairs={{0,16},{8,24},{16,0},{24,8},{1,17},{9,25},{17,1},{25,9},{2,18},{10... | collective-permute-start | bytes 196616 | tf_op jit(solution)/shard_map/ppermute | solution.py:622
  19.0 4.0 %collective-permute-start.7 = (f32[64,256]{1,0:T(8,128)S(1)}, f32[64,256]{1,0:T(8,128)S(1)}, u32[]{:S(2)}, u32[]{:S(2)}) collective-permute-start(f32[64,256]{1,0:T(8,128)S(1)} %get-tuple-element.54.own_ref), channel_id=1, source_target_pairs={{0,8},{8,0},{16,24},{24,16},{1,9},{9,1},{17,25},{25,17},{2,10},{10... | collective-permute-start | bytes 196616 | tf_op jit(solution)/shard_map/ppermute | solution.py:623
  19.0 4.0 %collective-permute-start.6 = (f32[64,256]{1,0:T(8,128)S(1)}, f32[64,256]{1,0:T(8,128)S(1)}, u32[]{:S(2)}, u32[]{:S(2)}) collective-permute-start(f32[64,256]{1,0:T(8,128)S(1)} %get-tuple-element.54.own_ref), channel_id=1, source_target_pairs={{0,24},{8,16},{16,8},{24,0},{1,25},{9,17},{17,9},{25,1},{2,26},{10... | collective-permute-start | bytes 196616 | tf_op jit(solution)/shard_map/ppermute | solution.py:621
